TPU v7x, 32 devices: a whole 2x2x4 slice. The times are simulated.
32 devices in a mesh: fsdp: 8 (over z, y), seq: 4 (over x, core).
Axes of the slice: x: 2, y: 2, z: 4, core: 2. Of those that a mesh axis runs over, the one named last changes fastest.
Arguments:
- inputs: bfloat16 [16, 1024, 768], P('fsdp', 'seq'), may hold values from -6 to 6
- segments: int32 [16, 1024], P('fsdp'), may hold values from 0 to 7, never falling along the last dimension, each value on 1 to 512 neighbouring positions
- neighbours: bfloat16 [16, 16, 256, 768], P('fsdp', 'seq'), may hold values from -6 to 6
- ln1_gain: bfloat16 [768], P('fsdp'), may hold values from 0.5 to 1.5
- ln1_bias: bfloat16 [768], P('fsdp'), may hold values from -3 to 3
- w_qkv: bfloat16 [768, 2304], P('fsdp'), may hold values from -0.21875 to 0.21875
- w_attn_out: bfloat16 [768, 768], P('fsdp'), may hold values from -0.875 to 0.875
- ln2_gain: bfloat16 [768], P('fsdp'), may hold values from 0.5 to 1.5
- ln2_bias: bfloat16 [768], P('fsdp'), may hold values from -3 to 3
- cross_q: bfloat16 [768, 768], P('fsdp'), may hold values from -0.21875 to 0.21875
- cross_kv: bfloat16 [768, 1536], P('fsdp'), may hold values from -0.21875 to 0.21875
- cross_out: bfloat16 [768, 768], P('fsdp'), may hold values from -1.25 to 1.25
- ln3_gain: bfloat16 [768], P('fsdp'), may hold values from 0.5 to 1.5
- ln3_bias: bfloat16 [768], P('fsdp'), may hold values from -3 to 3
- w_up: bfloat16 [768, 3072], P('fsdp'), may hold values from -0.21875 to 0.21875
- w_down: bfloat16 [3072, 768], P('fsdp'), may hold values from -0.109375 to 0.109375
- out_grad: bfloat16 [16, 1024, 768], P('fsdp', 'seq'), may hold values from -6 to 6
Outputs:
- outputs: bfloat16 [16, 1024, 768], P('fsdp', 'seq')
- input_grad: float32 [16, 1024, 768], P('fsdp', 'seq')
- neighbour_grad: float32 [16, 16, 256, 768], P('fsdp', 'seq')
- grad_ln1_gain: float32 [768], P('fsdp')
- grad_ln1_bias: float32 [768], P('fsdp')
- grad_w_qkv: float32 [768, 2304], P('fsdp')
- grad_w_attn_out: float32 [768, 768], P('fsdp')
- grad_ln2_gain: float32 [768], P('fsdp')
- grad_ln2_bias: float32 [768], P('fsdp')
- grad_cross_q: float32 [768, 768], P('fsdp')
- grad_cross_kv: float32 [768, 1536], P('fsdp')
- grad_cross_out: float32 [768, 768], P('fsdp')
- grad_ln3_gain: float32 [768], P('fsdp')
- grad_ln3_bias: float32 [768], P('fsdp')
- grad_w_up: float32 [768, 3072], P('fsdp')
- grad_w_down: float32 [3072, 768], P('fsdp')
Inputs may be any that keep to these rules, and one draw needn't show every extreme that they name: `segments`: along each sequence the segment numbers never fall; each of its 8 documents has 1 to 512 tokens, and one has exactly 512.
All inputs are finite; a program needn't handle non-finite values.
Results may differ from a plain program's by a relative error of at most 0.02.
Values may be sent and summed in bfloat16 or wider, within the bound.
No kernel may reach another device: no remote copies, remote signals or barrier semaphores. Data moves between devices by JAX's collectives and lax.ppermute only.
A program may use at most 192 MiB of HBM per device.

v0:
```python
import jax
import jax.numpy as jnp
from jax import lax
from jax.sharding import PartitionSpec as P

HEADS = 12
HEAD_DIM = 64
SPAN = 64


EPS = 1e-05
NEG = -1e30


def layer_norm(values, gain_row, bias_row):
    centre = values - jnp.mean(values, -1, keepdims=True)
    spread = jnp.mean(centre * centre, -1, keepdims=True)
    return centre * lax.rsqrt(spread + EPS) * gain_row + bias_row


def gelu_tanh(values):
    return jax.nn.gelu(values, approximate=True)


def product(left_side, right_side):
    return jnp.dot(left_side, right_side, preferred_element_type=jnp.float32)


def trans_left(left_side, right_side):
    return lax.dot_general(
        left_side, right_side, (((0,), (0,)), ((), ())), preferred_element_type=jnp.float32
    )


def trans_right(left_side, right_side):
    return lax.dot_general(
        left_side, right_side, (((1,), (1,)), ((), ())), preferred_element_type=jnp.float32
    )


def block_mask(seg_row, places, row_start, row_stop):
    same_doc = seg_row[row_start:row_stop, None] == seg_row[None, :]
    return same_doc & (places[None, :] <= places[row_start:row_stop, None])


def self_forward(query_all, key_all, value_all, seg_row, heads_here):
    length = query_all.shape[0]
    score_scale = HEAD_DIM ** (-0.5)
    query_h = query_all.reshape(length, heads_here, HEAD_DIM)
    key_h = key_all.reshape(length, heads_here, HEAD_DIM)
    value_h = value_all.reshape(length, heads_here, HEAD_DIM)
    block_rows = min(512, length)
    places = jnp.arange(length)
    out_blocks = []
    lse_blocks = []
    for row_start in range(0, length, block_rows):
        row_stop = row_start + block_rows
        allowed = block_mask(seg_row, places, row_start, row_stop)
        scores = (
            jnp.einsum(
                "qhd,khd->hqk",
                query_h[row_start:row_stop],
                key_h,
                preferred_element_type=jnp.float32,
            )
            * score_scale
        )
        scores = jnp.where(allowed[None], scores, NEG)
        row_top = jnp.max(scores, -1, keepdims=True)
        raised = jnp.exp(scores - row_top)
        row_total = jnp.sum(raised, -1, keepdims=True)
        weights = (raised / row_total).astype(jnp.bfloat16)
        out_blocks.append(
            jnp.einsum("hqk,khd->qhd", weights, value_h, preferred_element_type=jnp.float32).astype(
                jnp.bfloat16
            )
        )
        lse_blocks.append(row_top + jnp.log(row_total))
    mixed_all = jnp.concatenate(out_blocks, 0).reshape(length, heads_here * HEAD_DIM)
    return (mixed_all, jnp.concatenate(lse_blocks, 1))


def self_backward(query_all, key_all, value_all, seg_row, lse_all, grad_all, heads_here):
    length = query_all.shape[0]
    score_scale = HEAD_DIM ** (-0.5)
    query_h = query_all.reshape(length, heads_here, HEAD_DIM)
    key_h = key_all.reshape(length, heads_here, HEAD_DIM)
    value_h = value_all.reshape(length, heads_here, HEAD_DIM)
    grad_h = grad_all.reshape(length, heads_here, HEAD_DIM)
    block_rows = min(512, length)
    places = jnp.arange(length)
    query_blocks = []
    key_acc = jnp.zeros((length, heads_here, HEAD_DIM), jnp.float32)
    value_acc = jnp.zeros((length, heads_here, HEAD_DIM), jnp.float32)
    for row_start in range(0, length, block_rows):
        row_stop = row_start + block_rows
        allowed = block_mask(seg_row, places, row_start, row_stop)
        query_part = query_h[row_start:row_stop]
        grad_part = grad_h[row_start:row_stop]
        scores = (
            jnp.einsum("qhd,khd->hqk", query_part, key_h, preferred_element_type=jnp.float32)
            * score_scale
        )
        scores = jnp.where(allowed[None], scores, NEG)
        weights = jnp.exp(scores - lse_all[:, row_start:row_stop])
        grad_weights = jnp.einsum(
            "qhd,khd->hqk", grad_part, value_h, preferred_element_type=jnp.float32
        )
        delta_row = jnp.sum(weights * grad_weights, -1, keepdims=True)
        grad_scores = (weights * (grad_weights - delta_row)).astype(jnp.bfloat16)
        query_blocks.append(
            jnp.einsum("hqk,khd->qhd", grad_scores, key_h, preferred_element_type=jnp.float32)
            * score_scale
        )
        key_acc = (
            key_acc
            + jnp.einsum(
                "hqk,qhd->khd", grad_scores, query_part, preferred_element_type=jnp.float32
            )
            * score_scale
        )
        value_acc = value_acc + jnp.einsum(
            "hqk,qhd->khd",
            weights.astype(jnp.bfloat16),
            grad_part,
            preferred_element_type=jnp.float32,
        )
    stacked = jnp.stack([jnp.concatenate(query_blocks, 0), key_acc, value_acc], 1)
    return stacked.astype(jnp.bfloat16).reshape(length, 3, heads_here * HEAD_DIM)


def cross_forward(query_rows, memory_kv):
    local_rows, width = query_rows.shape
    spans = local_rows // SPAN
    neighbour_count = memory_kv.shape[0] // spans
    score_scale = HEAD_DIM ** (-0.5)
    query_h = query_rows.reshape(spans, SPAN, HEADS, HEAD_DIM)
    memory_h = memory_kv.reshape(spans, neighbour_count, 2, HEADS, HEAD_DIM)
    scores = (
        jnp.einsum(
            "cqhd,ckhd->chqk", query_h, memory_h[:, :, 0], preferred_element_type=jnp.float32
        )
        * score_scale
    )
    row_top = jnp.max(scores, -1, keepdims=True)
    raised = jnp.exp(scores - row_top)
    weights = raised / jnp.sum(raised, -1, keepdims=True)
    mixed_rows = jnp.einsum(
        "chqk,ckhd->cqhd",
        weights.astype(jnp.bfloat16),
        memory_h[:, :, 1],
        preferred_element_type=jnp.float32,
    )
    return (mixed_rows.astype(jnp.bfloat16).reshape(local_rows, width), weights)


def cross_backward(query_rows, memory_kv, weights, grad_mixed):
    local_rows, width = query_rows.shape
    spans = local_rows // SPAN
    neighbour_count = memory_kv.shape[0] // spans
    score_scale = HEAD_DIM ** (-0.5)
    query_h = query_rows.reshape(spans, SPAN, HEADS, HEAD_DIM)
    memory_h = memory_kv.reshape(spans, neighbour_count, 2, HEADS, HEAD_DIM)
    grad_h = grad_mixed.reshape(spans, SPAN, HEADS, HEAD_DIM)
    grad_weights = jnp.einsum(
        "cqhd,ckhd->chqk", grad_h, memory_h[:, :, 1], preferred_element_type=jnp.float32
    )
    delta_row = jnp.sum(weights * grad_weights, -1, keepdims=True)
    grad_scores = (weights * (grad_weights - delta_row)).astype(jnp.bfloat16)
    grad_query = (
        jnp.einsum(
            "chqk,ckhd->cqhd", grad_scores, memory_h[:, :, 0], preferred_element_type=jnp.float32
        )
        * score_scale
    )
    grad_key = (
        jnp.einsum("chqk,cqhd->ckhd", grad_scores, query_h, preferred_element_type=jnp.float32)
        * score_scale
    )
    grad_value = jnp.einsum(
        "chqk,cqhd->ckhd", weights.astype(jnp.bfloat16), grad_h, preferred_element_type=jnp.float32
    )
    grad_memory = (
        jnp.stack([grad_key, grad_value], 2)
        .astype(jnp.bfloat16)
        .reshape(spans * neighbour_count, 2 * width)
    )
    return (grad_query.astype(jnp.bfloat16).reshape(local_rows, width), grad_memory)


def layer_forward(full_set, token_rows, seg_row, neighbour_rows, heads_here):
    (
        gain_one,
        bias_one,
        w_qkv,
        w_attn_out,
        gain_two,
        bias_two,
        cross_q,
        cross_kv,
        cross_out,
        gain_three,
        bias_three,
        w_up,
        w_down,
    ) = full_set
    local_rows, width = token_rows.shape
    token_float = token_rows.astype(jnp.float32)
    normed_one = layer_norm(
        token_float, gain_one.astype(jnp.float32), bias_one.astype(jnp.float32)
    ).astype(jnp.bfloat16)
    packed = product(normed_one, w_qkv).astype(jnp.bfloat16).reshape(local_rows, 3, width)
    heads_all = lax.all_to_all(packed, "seq", split_axis=2, concat_axis=0, tiled=True)
    mixed_all, lse_all = self_forward(
        heads_all[:, 0], heads_all[:, 1], heads_all[:, 2], seg_row, heads_here
    )
    mixed_local = lax.all_to_all(mixed_all, "seq", split_axis=0, concat_axis=1, tiled=True)
    after_self = token_float + product(mixed_local, w_attn_out)
    normed_two = layer_norm(
        after_self, gain_two.astype(jnp.float32), bias_two.astype(jnp.float32)
    ).astype(jnp.bfloat16)
    query_rows = product(normed_two, cross_q).astype(jnp.bfloat16)
    neighbour_flat = neighbour_rows.reshape(-1, width)
    memory_kv = product(neighbour_flat, cross_kv).astype(jnp.bfloat16)
    cross_mixed, cross_weights = cross_forward(query_rows, memory_kv)
    after_cross = after_self + product(cross_mixed, cross_out)
    normed_three = layer_norm(
        after_cross, gain_three.astype(jnp.float32), bias_three.astype(jnp.float32)
    ).astype(jnp.bfloat16)
    hidden = product(normed_three, w_up)
    activated = gelu_tanh(hidden).astype(jnp.bfloat16)
    result = (after_cross + product(activated, w_down)).astype(jnp.bfloat16)
    saved = (
        token_float,
        normed_one,
        heads_all,
        lse_all,
        mixed_local,
        after_self,
        normed_two,
        query_rows,
        neighbour_flat,
        memory_kv,
        cross_weights,
        cross_mixed,
        after_cross,
        normed_three,
        hidden,
        activated,
    )
    return (result, saved)


def layer_backward(full_set, saved, grad_rows, seg_row, heads_here):
    (
        gain_one,
        bias_one,
        w_qkv,
        w_attn_out,
        gain_two,
        bias_two,
        cross_q,
        cross_kv,
        cross_out,
        gain_three,
        bias_three,
        w_up,
        w_down,
    ) = full_set
    (
        token_float,
        normed_one,
        heads_all,
        lse_all,
        mixed_local,
        after_self,
        normed_two,
        query_rows,
        neighbour_flat,
        memory_kv,
        cross_weights,
        cross_mixed,
        after_cross,
        normed_three,
        hidden,
        activated,
    ) = saved
    local_rows, width = token_float.shape
    grad_float = grad_rows.astype(jnp.float32)
    grad_down = trans_left(activated, grad_rows)
    grad_act = trans_right(grad_rows, w_down)
    gelu_out, gelu_pull = jax.vjp(gelu_tanh, hidden)
    grad_hidden = gelu_pull(grad_act)[0].astype(jnp.bfloat16)
    grad_up = trans_left(normed_three, grad_hidden)
    grad_norm3 = trans_right(grad_hidden, w_up)
    norm_out3, pull_three = jax.vjp(
        layer_norm, after_cross, gain_three.astype(jnp.float32), bias_three.astype(jnp.float32)
    )
    back_three, grad_gain3, grad_bias3 = pull_three(grad_norm3)
    grad_after_cross = grad_float + back_three
    grad_branch = grad_after_cross.astype(jnp.bfloat16)
    grad_cross_out = trans_left(cross_mixed, grad_branch)
    grad_cross_mixed = trans_right(grad_branch, cross_out).astype(jnp.bfloat16)
    grad_query, grad_memory = cross_backward(query_rows, memory_kv, cross_weights, grad_cross_mixed)
    grad_cross_q = trans_left(normed_two, grad_query)
    grad_cross_kv = trans_left(neighbour_flat, grad_memory)
    neighbour_back = trans_right(grad_memory, cross_kv)
    grad_norm2 = trans_right(grad_query, cross_q)
    norm_out2, pull_two = jax.vjp(
        layer_norm, after_self, gain_two.astype(jnp.float32), bias_two.astype(jnp.float32)
    )
    back_two, grad_gain2, grad_bias2 = pull_two(grad_norm2)
    grad_after_self = grad_after_cross + back_two
    grad_attn = grad_after_self.astype(jnp.bfloat16)
    grad_attn_out = trans_left(mixed_local, grad_attn)
    grad_mixed = trans_right(grad_attn, w_attn_out).astype(jnp.bfloat16)
    grad_mixed_all = lax.all_to_all(grad_mixed, "seq", split_axis=1, concat_axis=0, tiled=True)
    grad_packed_all = self_backward(
        heads_all[:, 0],
        heads_all[:, 1],
        heads_all[:, 2],
        seg_row,
        lse_all,
        grad_mixed_all,
        heads_here,
    )
    grad_packed = lax.all_to_all(
        grad_packed_all, "seq", split_axis=0, concat_axis=2, tiled=True
    ).reshape(local_rows, 3 * width)
    grad_qkv = trans_left(normed_one, grad_packed)
    grad_norm1 = trans_right(grad_packed, w_qkv)
    norm_out1, pull_one = jax.vjp(
        layer_norm, token_float, gain_one.astype(jnp.float32), bias_one.astype(jnp.float32)
    )
    back_one, grad_gain1, grad_bias1 = pull_one(grad_norm1)
    input_back = grad_after_self + back_one
    grads = (
        grad_gain1,
        grad_bias1,
        grad_qkv,
        grad_attn_out,
        grad_gain2,
        grad_bias2,
        grad_cross_q,
        grad_cross_kv,
        grad_cross_out,
        grad_gain3,
        grad_bias3,
        grad_up,
        grad_down,
    )
    return (grads, input_back, neighbour_back)


def per_device(
    inputs,
    segments,
    neighbours,
    ln1_gain,
    ln1_bias,
    w_qkv,
    w_attn_out,
    ln2_gain,
    ln2_bias,
    cross_q,
    cross_kv,
    cross_out,
    ln3_gain,
    ln3_bias,
    w_up,
    w_down,
    out_grad,
):
    shards = (
        ln1_gain,
        ln1_bias,
        w_qkv,
        w_attn_out,
        ln2_gain,
        ln2_bias,
        cross_q,
        cross_kv,
        cross_out,
        ln3_gain,
        ln3_bias,
        w_up,
        w_down,
    )
    heads_here = HEADS // lax.axis_size("seq")
    owners = lax.axis_size("fsdp")
    grad_sums = tuple(
        (jnp.zeros((piece.shape[0] * owners,) + piece.shape[1:], jnp.float32) for piece in shards)
    )
    output_list = []
    input_list = []
    neighbour_list = []
    for member in range(inputs.shape[0]):
        forward_set = (
            lax.all_gather(shards[0], "fsdp", axis=0, tiled=True),
            lax.all_gather(shards[1], "fsdp", axis=0, tiled=True),
            lax.all_gather(shards[2], "fsdp", axis=0, tiled=True),
            lax.all_gather(shards[3], "fsdp", axis=0, tiled=True),
            lax.all_gather(shards[4], "fsdp", axis=0, tiled=True),
            lax.all_gather(shards[5], "fsdp", axis=0, tiled=True),
            lax.all_gather(shards[6], "fsdp", axis=0, tiled=True),
            lax.all_gather(shards[7], "fsdp", axis=0, tiled=True),
            lax.all_gather(shards[8], "fsdp", axis=0, tiled=True),
            lax.all_gather(shards[9], "fsdp", axis=0, tiled=True),
            lax.all_gather(shards[10], "fsdp", axis=0, tiled=True),
            lax.all_gather(shards[11], "fsdp", axis=0, tiled=True),
            lax.all_gather(shards[12], "fsdp", axis=0, tiled=True),
        )
        result, saved = layer_forward(
            forward_set, inputs[member], segments[member], neighbours[member], heads_here
        )
        backward_set = (
            lax.all_gather(shards[0], "fsdp", axis=0, tiled=True),
            lax.all_gather(shards[1], "fsdp", axis=0, tiled=True),
            lax.all_gather(shards[2], "fsdp", axis=0, tiled=True),
            lax.all_gather(shards[3], "fsdp", axis=0, tiled=True),
            lax.all_gather(shards[4], "fsdp", axis=0, tiled=True),
            lax.all_gather(shards[5], "fsdp", axis=0, tiled=True),
            lax.all_gather(shards[6], "fsdp", axis=0, tiled=True),
            lax.all_gather(shards[7], "fsdp", axis=0, tiled=True),
            lax.all_gather(shards[8], "fsdp", axis=0, tiled=True),
            lax.all_gather(shards[9], "fsdp", axis=0, tiled=True),
            lax.all_gather(shards[10], "fsdp", axis=0, tiled=True),
            lax.all_gather(shards[11], "fsdp", axis=0, tiled=True),
            lax.all_gather(shards[12], "fsdp", axis=0, tiled=True),
        )
        grads, input_back, neighbour_back = layer_backward(
            backward_set, saved, out_grad[member], segments[member], heads_here
        )
        grad_sums = tuple(
            (running_sum + grad_part for running_sum, grad_part in zip(grad_sums, grads))
        )
        output_list.append(result)
        input_list.append(input_back)
        neighbour_list.append(neighbour_back.reshape(neighbours.shape[1:]))
    (
        sum_gain1,
        sum_bias1,
        sum_qkv,
        sum_attn_out,
        sum_gain2,
        sum_bias2,
        sum_cross_q,
        sum_cross_kv,
        sum_cross_out,
        sum_gain3,
        sum_bias3,
        sum_up,
        sum_down,
    ) = grad_sums
    column_parts = (
        lax.psum_scatter(
            sum_qkv.astype(jnp.bfloat16), "seq", scatter_dimension=1, tiled=True
        ).astype(jnp.float32),
        lax.psum_scatter(
            sum_attn_out.astype(jnp.bfloat16), "seq", scatter_dimension=1, tiled=True
        ).astype(jnp.float32),
        lax.psum_scatter(
            sum_cross_q.astype(jnp.bfloat16), "seq", scatter_dimension=1, tiled=True
        ).astype(jnp.float32),
        lax.psum_scatter(
            sum_cross_kv.astype(jnp.bfloat16), "seq", scatter_dimension=1, tiled=True
        ).astype(jnp.float32),
        lax.psum_scatter(
            sum_cross_out.astype(jnp.bfloat16), "seq", scatter_dimension=1, tiled=True
        ).astype(jnp.float32),
        lax.psum_scatter(
            sum_up.astype(jnp.bfloat16), "seq", scatter_dimension=1, tiled=True
        ).astype(jnp.float32),
        lax.psum_scatter(
            sum_down.astype(jnp.bfloat16), "seq", scatter_dimension=1, tiled=True
        ).astype(jnp.float32),
    )
    part_qkv, part_attn_out, part_cross_q, part_cross_kv, part_cross_out, part_up, part_down = (
        column_parts
    )
    owned_parts = (
        lax.psum_scatter(sum_gain1, "fsdp", scatter_dimension=0, tiled=True),
        lax.psum_scatter(sum_bias1, "fsdp", scatter_dimension=0, tiled=True),
        lax.psum_scatter(sum_gain2, "fsdp", scatter_dimension=0, tiled=True),
        lax.psum_scatter(sum_bias2, "fsdp", scatter_dimension=0, tiled=True),
        lax.psum_scatter(sum_gain3, "fsdp", scatter_dimension=0, tiled=True),
        lax.psum_scatter(sum_bias3, "fsdp", scatter_dimension=0, tiled=True),
        lax.psum_scatter(part_qkv, "fsdp", scatter_dimension=0, tiled=True),
        lax.psum_scatter(part_attn_out, "fsdp", scatter_dimension=0, tiled=True),
        lax.psum_scatter(part_cross_q, "fsdp", scatter_dimension=0, tiled=True),
        lax.psum_scatter(part_cross_kv, "fsdp", scatter_dimension=0, tiled=True),
        lax.psum_scatter(part_cross_out, "fsdp", scatter_dimension=0, tiled=True),
        lax.psum_scatter(part_up, "fsdp", scatter_dimension=0, tiled=True),
        lax.psum_scatter(part_down, "fsdp", scatter_dimension=0, tiled=True),
    )
    (
        own_gain1,
        own_bias1,
        own_gain2,
        own_bias2,
        own_gain3,
        own_bias3,
        own_qkv,
        own_attn_out,
        own_cross_q,
        own_cross_kv,
        own_cross_out,
        own_up,
        own_down,
    ) = owned_parts
    matrices = (
        lax.all_gather(own_qkv.astype(jnp.bfloat16), "seq", axis=1, tiled=True).astype(
            own_qkv.dtype
        ),
        lax.all_gather(own_attn_out.astype(jnp.bfloat16), "seq", axis=1, tiled=True).astype(
            own_attn_out.dtype
        ),
        lax.all_gather(own_cross_q.astype(jnp.bfloat16), "seq", axis=1, tiled=True).astype(
            own_cross_q.dtype
        ),
        lax.all_gather(own_cross_kv.astype(jnp.bfloat16), "seq", axis=1, tiled=True).astype(
            own_cross_kv.dtype
        ),
        lax.all_gather(own_cross_out.astype(jnp.bfloat16), "seq", axis=1, tiled=True).astype(
            own_cross_out.dtype
        ),
        lax.all_gather(own_up.astype(jnp.bfloat16), "seq", axis=1, tiled=True).astype(own_up.dtype),
        lax.all_gather(own_down.astype(jnp.bfloat16), "seq", axis=1, tiled=True).astype(
            own_down.dtype
        ),
    )
    vectors = lax.psum((own_gain1, own_bias1, own_gain2, own_bias2, own_gain3, own_bias3), "seq")
    return (
        jnp.stack(output_list),
        jnp.stack(input_list),
        jnp.stack(neighbour_list),
        vectors[0],
        vectors[1],
        matrices[0],
        matrices[1],
        vectors[2],
        vectors[3],
        matrices[2],
        matrices[3],
        matrices[4],
        vectors[4],
        vectors[5],
        matrices[5],
        matrices[6],
    )


def solution(mesh):
    return jax.shard_map(
        per_device,
        mesh=mesh,
        in_specs=(
            P("fsdp", "seq", None),
            P("fsdp", None),
            P("fsdp", "seq", None, None),
            P("fsdp"),
            P("fsdp"),
            P("fsdp", None),
            P("fsdp", None),
            P("fsdp"),
            P("fsdp"),
            P("fsdp", None),
            P("fsdp", None),
            P("fsdp", None),
            P("fsdp"),
            P("fsdp"),
            P("fsdp", None),
            P("fsdp", None),
            P("fsdp", "seq", None),
        ),
        out_specs=(
            P("fsdp", "seq", None),
            P("fsdp", "seq", None),
            P("fsdp", "seq", None, None),
            P("fsdp"),
            P("fsdp"),
            P("fsdp", None),
            P("fsdp", None),
            P("fsdp"),
            P("fsdp"),
            P("fsdp", None),
            P("fsdp", None),
            P("fsdp", None),
            P("fsdp"),
            P("fsdp"),
            P("fsdp", None),
            P("fsdp", None),
        ),
        check_vma=False,
    )
```

profile of v0, /device:TPU:9, one launch (start us, length us, event | category | flops | bytes accessed | tf_op | source)
XLA Modules:
  0.0 1297.0 jit_solution(1946272474161372065)
XLA Ops:
  20.5 28.9 %all-reduce.14 = (bf16[768]{0:T(1024)(128)(2,1)S(1)}, bf16[768]{0:T(1024)(128)(2,1)S(1)}, bf16[768]{0:T(1024)(128)(2,1)S(1)}, bf16[768]{0:T(1024)(128)(2,1)S(1)}...) all-reduce(bf16[768]{0:T(1024)(128)(2,1)S(1)} %dynamic-update-slice, ...), channel_id=1, replica_groups=mesh['fsdp'=8,'seq'=4] {'fsdp'}, use_global_device_ids=true, to_apply=%add.1 | all-reduce | flops 4608 | bytes 18432
  62.5 5.6 convolution_convert_fusion.2
  68.1 4.7 copy.225
  72.8 6.2 reshape.653
  79.0 48.5 %all-gather.9.cloned.1.call-done = bf16[768,2304]{1,0:T(8,128)(2,1)} async-done(((bf16[96,2304]{1,0:T(8,128)(2,1)}), bf16[768,2304]{1,0:T(8,128)(2,1)}) %all-gather.9.cloned.1.call-update) | async-done | bytes 3538960 | tf_op jit(solution)/shard_map/all_gather | solution.py:401
  133.4 5.8 all-to-all-start.2
  139.3 6.5 convolution_convert_fusion.3
  151.7 6.7 all-to-all-done.2
  158.5 5.4 all-to-all-start
  163.9 5.2 fusion.228
  169.1 4.6 copy.214
  173.7 6.2 reshape.649
  179.9 5.2 fusion.226
  201.2 3.9 all-to-all-start.3
  217.8 4.1 all-to-all-start.1
  233.3 9.7 fusion.68
  257.8 9.7 fusion.67
  276.2 56.4 %all-gather.19.cloned.1.call-done = bf16[768,3072]{1,0:T(8,128)(2,1)} async-done(((bf16[96,3072]{1,0:T(8,128)(2,1)}), bf16[768,3072]{1,0:T(8,128)(2,1)}) %all-gather.19.cloned.1.call-update) | async-done | bytes 4718608 | tf_op jit(solution)/shard_map/all_gather | solution.py:410
  332.7 5.5 fusion.205
  338.1 74.4 %all-gather.21.cloned.1.call-done = bf16[3072,768]{1,0:T(8,128)(2,1)} async-done(((bf16[384,768]{1,0:T(8,128)(2,1)}), bf16[3072,768]{1,0:T(8,128)(2,1)}) %all-gather.21.cloned.1.call-update) | async-done | bytes 4718608 | tf_op jit(solution)/shard_map/all_gather | solution.py:411
  412.6 6.2 fusion.23
  441.4 4.0 multiply_reduce_fusion.5
  449.8 4.1 multiply_reduce_fusion.4
  466.8 4.0 multiply_reduce_fusion.11
  479.5 6.6 all-to-all-start.6
  486.1 9.8 convolution_bitcast_fusion
  510.1 9.7 convolution_bitcast_fusion.1
  529.2 3.8 fusion.40
  539.5 4.9 fusion.24
  544.3 6.0 multiply_reduce_fusion
  550.7 4.0 multiply_reduce_fusion.1
  560.2 4.6 fusion.28
  564.9 6.2 multiply_reduce_fusion.3
  577.6 4.8 fusion.83
  584.7 5.4 multiply_convert_fusion
  596.0 6.7 pad_maximum_fusion.2
  602.7 4.7 all-to-all-start.7
  607.4 5.5 multiply_convert_fusion.3
  629.1 6.2 pad_maximum_fusion.1
  639.0 4.2 copy.252
  643.2 20.4 %all-to-all-done.5 = bf16[1024,3,192]{2,1,0:T(4,128)(2,1)S(1)} async-done(((bf16[1024,3,192]{2,1,0:T(4,128)(2,1)}), bf16[1024,3,192]{2,1,0:T(4,128)(2,1)S(1)}, u32[]{:S(2)}, u32[]{:S(2)}) %all-to-all-start.5) | async-done | bytes 1179680 | tf_op jit(solution)/shard_map/all_to_all | solution.py:327
  684.3 3.8 add_convert_fusion.1
  697.0 13.6 %reduce-scatter.25.cloned.1.call-done = bf16[768,576]{0,1:T(8,128)(2,1)} async-done(((bf16[768,2304]{0,1:T(8,128)(2,1)}), bf16[768,576]{0,1:T(8,128)(2,1)}) %reduce-scatter.25.cloned.1.call-update) | async-done | bytes 884752 | tf_op jit(solution)/shard_map/reduce_scatter | solution.py:456
  713.9 5.2 fusion.89
  719.1 42.6 %reduce-scatter.39.cloned.1.call-done = bf16[3072,192]{0,1:T(8,128)(2,1)} async-done(((bf16[3072,768]{0,1:T(8,128)(2,1)}), bf16[3072,192]{0,1:T(8,128)(2,1)}) %reduce-scatter.39.cloned.1.call-update) | async-done | bytes 1179664 | tf_op jit(solution)/shard_map/reduce_scatter | solution.py:474
  762.0 5.4 fusion.90
  785.3 26.7 %reduce-scatter.35.cloned.1.call-done = bf16[768,768]{1,0:T(8,128)(2,1)} async-done(((bf16[768,3072]{1,0:T(8,128)(2,1)}), bf16[768,768]{1,0:T(8,128)(2,1)}) %reduce-scatter.35.cloned.1.call-update) | async-done | bytes 1179664 | tf_op jit(solution)/shard_map/reduce_scatter | solution.py:471
  812.1 3.7 fusion.130
  816.7 28.8 %all-reduce.12 = (f32[768]{0:T(1024)S(1)}, f32[768]{0:T(1024)S(1)}, f32[768]{0:T(1024)S(1)}, f32[768]{0:T(1024)S(1)}, f32[768]{0:T(1024)S(1)}, /*index=5*/f32[768]{0:T(1024)S(1)}) all-reduce(f32[768]{0:T(1024)S(1)} %add.363, f32[768]{0:T(1024)S(1)} %add.364, f32[768]{0:T(1024)} %add.370, ...), channel_id=2, replica_groups=mesh['fsdp'=8,'seq'=4] {'fsdp'}, use_global_device_ids=true, to_apply=%region_44.45.clone | all-reduce | flops 4608 | bytes 36864
  845.9 13.0 %all-reduce.13 = (f32[96]{0:T(128)}, f32[96]{0:T(128)}, f32[96]{0:T(128)}, f32[96]{0:T(128)}, f32[96]{0:T(128)}, /*index=5*/f32[96]{0:T(128)}) all-reduce(f32[96]{0:T(128)S(1)} %dynamic-slice.7, f32[96]{0:T(128)S(1)} %dynamic-slice.9, f32[96]{0:T(128)S(1)} %dynamic-slice.11, ...), channel_id=1, replica_groups=mesh['fsdp'=8,'seq'=4] {'seq'}, use_global_device_ids=true, to_apply=%region_45.46 | all-reduce | flops 576 | bytes 4608 | tf_op jit(solution)/shard_map/psum | solution.py:532
  862.1 14.4 %reduce-scatter.47.cloned.1.call-done = f32[96,192]{1,0:T(8,128)} async-done(((f32[768,192]{1,0:T(8,128)}), f32[96,192]{1,0:T(8,128)}) %reduce-scatter.47.cloned.1.call-update) | async-done | bytes 73744
  877.5 7.9 all_gather.108
  886.3 55.6 %reduce-scatter.51.cloned.1.call-done = f32[96,192]{1,0:T(8,128)} async-done(((f32[768,192]{1,0:T(8,128)}), f32[96,192]{1,0:T(8,128)}) %reduce-scatter.51.cloned.1.call-update) | async-done | bytes 73744
  942.9 7.9 all_gather.110
  951.7 55.3 %reduce-scatter.45.cloned.1.call-done = f32[96,192]{1,0:T(8,128)} async-done(((f32[768,192]{1,0:T(8,128)}), f32[96,192]{1,0:T(8,128)}) %reduce-scatter.45.cloned.1.call-update) | async-done | bytes 73744
  1008.1 8.3 all_gather.107
  1017.2 57.1 %reduce-scatter.49.cloned.1.call-done = f32[96,384]{1,0:T(8,128)} async-done(((f32[768,384]{1,0:T(8,128)}), f32[96,384]{1,0:T(8,128)}) %reduce-scatter.49.cloned.1.call-update) | async-done | bytes 147472
  1075.4 8.9 all_gather.109
  1085.2 59.4 %reduce-scatter.43.cloned.1.call-done = f32[96,576]{1,0:T(8,128)} async-done(((f32[768,576]{1,0:T(8,128)}), f32[96,576]{1,0:T(8,128)}) %reduce-scatter.43.cloned.1.call-update) | async-done | bytes 221200
  1145.8 8.6 all-gather
  1156.2 54.9 %reduce-scatter.41.cloned.1.call-done = bf16[384,192]{0,1:T(8,128)(2,1)} async-done(((bf16[3072,192]{0,1:T(8,128)(2,1)}), bf16[384,192]{0,1:T(8,128)(2,1)}) %reduce-scatter.41.cloned.1.call-update) | async-done | bytes 147472 | tf_op jit(solution)/shard_map/reduce_scatter | solution.py:494
  1211.1 10.2 all_gather.112
  1222.6 55.7 %reduce-scatter.37.cloned.1.call-done = bf16[96,768]{1,0:T(8,128)(2,1)} async-done(((bf16[768,768]{1,0:T(8,128)(2,1)}), bf16[96,768]{1,0:T(8,128)(2,1)}) %reduce-scatter.37.cloned.1.call-update) | async-done | bytes 147472 | tf_op jit(solution)/shard_map/reduce_scatter | solution.py:493
  1278.3 10.2 all_gather.111
  (675 shorter events, 285.5 us)
Async XLA Ops:
  7.2 43.6 %copy-start.6 = (bf16[2,256,768]{2,1,0:T(8,128)(2,1)S(1)}, bf16[2,256,768]{2,1,0:T(8,128)(2,1)}, u32[]{:S(2)}) copy-start(bf16[2,256,768]{2,1,0:T(8,128)(2,1)} %param.17) | copy-start | bytes 2359300
  7.2 55.3 %all-gather.13.cloned.1.call-start = ((), (), s32[]{:S(2)}) async-start(), calls=%async_computation.24 | async-start | bytes 2654208 | tf_op jit(solution)/shard_map/all_gather | solution.py:406
  7.9 119.6 %all-gather.9.cloned.1.call-start = ((), (), s32[]{:S(2)}) async-start(), calls=%async_computation.22 | async-start | bytes 3981312 | tf_op jit(solution)/shard_map/all_gather | solution.py:401
  8.7 213.5 %all-gather.11.cloned.1.call-start = ((), (), s32[]{:S(2)}) async-start(), calls=%async_computation.23 | async-start | bytes 1327104 | tf_op jit(solution)/shard_map/all_gather | solution.py:402
  9.4 214.9 %all-gather.15.cloned.1.call-start = ((), (), s32[]{:S(2)}) async-start(), calls=%async_computation.25 | async-start | bytes 1327104 | tf_op jit(solution)/shard_map/all_gather | solution.py:405
  10.0 260.5 %all-gather.17.cloned.1.call-start = ((), (), s32[]{:S(2)}) async-start(), calls=%async_computation.26 | async-start | bytes 1327104 | tf_op jit(solution)/shard_map/all_gather | solution.py:407
  10.6 322.1 %all-gather.19.cloned.1.call-start = ((), (), s32[]{:S(2)}) async-start(), calls=%async_computation.27 | async-start | bytes 5308416 | tf_op jit(solution)/shard_map/all_gather | solution.py:410
  11.1 401.4 %all-gather.21.cloned.1.call-start = ((), (), s32[]{:S(2)}) async-start(), calls=%async_computation.28 | async-start | bytes 5308416 | tf_op jit(solution)/shard_map/all_gather | solution.py:411
  49.4 96.3 %copy-start.117 = (f32[768]{0:T(1024)}, f32[768]{0:T(1024)S(1)}, u32[]{:S(2)}) copy-start(f32[768]{0:T(1024)S(1)} %convert_element_type.370) | copy-start | bytes 9220
  50.7 76.7 %copy-start.130 = (f32[256]{0:T(256)}, f32[256]{0:T(256)S(1)}, u32[]{:S(2)}) copy-start(f32[256]{0:T(256)S(1)} %get-tuple-element.231) | copy-start | bytes 3076
  50.7 95.0 %copy-start.132 = (f32[256]{0:T(256)}, f32[256]{0:T(256)S(1)}, u32[]{:S(2)}) copy-start(f32[256]{0:T(256)S(1)} %get-tuple-element.232) | copy-start | bytes 3076
  51.7 94.1 %copy-start.137 = (f32[256]{0:T(256)}, f32[256]{0:T(256)S(1)}, u32[]{:S(2)}) copy-start(f32[256]{0:T(256)S(1)} %fusion.192) | copy-start | bytes 3076
  51.7 75.8 %copy-start.140 = (f32[256]{0:T(256)}, f32[256]{0:T(256)S(1)}, u32[]{:S(2)}) copy-start(f32[256]{0:T(256)S(1)} %fusion.195) | copy-start | bytes 3076
  51.7 94.0 %copy-start.106 = (f32[768]{0:T(1024)}, f32[768]{0:T(1024)S(1)}, u32[]{:S(2)}) copy-start(f32[768]{0:T(1024)S(1)} %convert_element_type.369) | copy-start | bytes 9220
  52.9 369.0 %copy-start.96 = (f32[768]{0:T(1024)}, f32[768]{0:T(1024)S(1)}, u32[]{:S(2)}) copy-start(f32[768]{0:T(1024)S(1)} %convert_element_type.388) | copy-start | bytes 9220
  56.2 11.9 copy-start.85
  133.4 25.0 %all-to-all-start.2 = ((bf16[256,3,768]{0,1,2:T(4,128)(2,1)}), bf16[256,3,768]{0,1,2:T(4,128)(2,1)S(1)}, u32[]{:S(2)}, u32[]{:S(2)}) async-start(bf16[256,3,768]{0,1,2:T(4,128)(2,1)} %copy.221), calls=%async_computation.2 | async-start | bytes 3145728 | tf_op jit(solution)/shard_map/all_to_all | solution.py:213
  158.5 27.8 %all-to-all-start = ((bf16[256,3,768]{0,1,2:T(4,128)(2,1)}), bf16[256,3,768]{0,1,2:T(4,128)(2,1)}, u32[]{:S(2)}, u32[]{:S(2)}) async-start(bf16[256,3,768]{0,1,2:T(4,128)(2,1)} %copy.210), calls=%async_computation | async-start | bytes 3145728 | tf_op jit(solution)/shard_map/all_to_all | solution.py:213
  186.1 8.1 copy-start.71
  186.2 8.0 copy-start.31
  186.2 11.0 copy-start.51
  188.3 16.7 %copy-start.69 = (bf16[512,1,192]{0,2,1:T(8,128)(2,1)}, bf16[512,1,192]{0,2,1:T(8,128)(2,1)S(1)}, u32[]{:S(2)}) copy-start(bf16[512,1,192]{0,2,1:T(8,128)(2,1)S(1)} %get-tuple-element.155) | copy-start | bytes 589828
  188.4 22.5 %copy-start.77 = (bf16[512,1,192]{0,2,1:T(8,128)(2,1)}, bf16[512,1,192]{0,2,1:T(8,128)(2,1)S(1)}, u32[]{:S(2)}) copy-start(bf16[512,1,192]{0,2,1:T(8,128)(2,1)S(1)} %get-tuple-element.154) | copy-start | bytes 589828
  188.4 22.4 %copy-start.29 = (bf16[1024,1,192]{0,2,1:T(8,128)(2,1)}, bf16[1024,1,192]{0,2,1:T(8,128)(2,1)S(1)}, u32[]{:S(2)}) copy-start(bf16[1024,1,192]{0,2,1:T(8,128)(2,1)S(1)} %get-tuple-element.156) | copy-start | bytes 1179652
  188.4 25.4 %copy-start.49 = (bf16[1024,1,192]{0,2,1:T(8,128)(2,1)}, bf16[1024,1,192]{0,2,1:T(8,128)(2,1)S(1)}, u32[]{:S(2)}) copy-start(bf16[1024,1,192]{0,2,1:T(8,128)(2,1)S(1)} %get-tuple-element.157) | copy-start | bytes 1179652
  201.2 16.6 %all-to-all-start.3 = ((bf16[4,256,192]{1,2,0:T(8,128)(2,1)}), bf16[4,256,192]{1,2,0:T(8,128)(2,1)S(1)}, u32[]{:S(2)}, u32[]{:S(2)}) async-start(bf16[4,256,192]{1,2,0:T(8,128)(2,1)} %copy.224), calls=%async_computation.3 | async-start | bytes 786432 | tf_op jit(solution)/shard_map/all_to_all | solution.py:217
  216.7 7.7 copy-start.114
  216.7 7.7 copy-start.119
  217.8 8.4 copy-start.53
  217.8 28.2 %all-to-all-start.1 = ((bf16[4,256,192]{1,2,0:T(8,128)(2,1)}), bf16[4,256,192]{1,2,0:T(8,128)(2,1)}, u32[]{:S(2)}, u32[]{:S(2)}) async-start(bf16[4,256,192]{1,2,0:T(8,128)(2,1)} %copy.213), calls=%async_computation.1 | async-start | bytes 786432 | tf_op jit(solution)/shard_map/all_to_all | solution.py:217
  221.9 466.3 %reduce-scatter.29.cloned.1.call-start = ((), (), s32[]{:S(2)}) async-start(), calls=%async_computation.31 | async-start | bytes 1474560 | tf_op jit(solution)/shard_map/reduce_scatter | solution.py:462
  233.3 12.7 copy-start.13
  272.6 156.4 %copy-start.16 = (f32[256,768]{1,0:T(8,128)}, f32[256,768]{1,0:T(8,128)S(1)}, u32[]{:S(2)}) copy-start(f32[256,768]{1,0:T(8,128)S(1)} %get-tuple-element.205) | copy-start | bytes 2359300
  463.0 227.3 %reduce-scatter.33.cloned.1.call-start = ((), (), s32[]{:S(2)}) async-start(), calls=%async_computation.33 | async-start | bytes 1474560 | tf_op jit(solution)/shard_map/reduce_scatter | solution.py:468
  478.0 22.5 %copy-start.20 = (f32[256,768]{1,0:T(8,128)}, f32[256,768]{1,0:T(8,128)S(1)}, u32[]{:S(2)}) copy-start(f32[256,768]{1,0:T(8,128)S(1)} %get-tuple-element.165) | copy-start | bytes 2359300
  478.0 55.0 %copy-start.18 = (f32[256,768]{1,0:T(8,128)}, f32[256,768]{1,0:T(8,128)S(1)}, u32[]{:S(2)}) copy-start(f32[256,768]{1,0:T(8,128)S(1)} %get-tuple-element.164) | copy-start | bytes 2359300
  479.5 55.0 %all-to-all-start.6 = ((bf16[256,4,192]{0,2,1:T(8,128)(2,1)}), bf16[256,4,192]{0,2,1:T(8,128)(2,1)}, u32[]{:S(2)}, u32[]{:S(2)}) async-start(bf16[256,4,192]{0,2,1:T(8,128)(2,1)} %bitcast.59), calls=%async_computation.6 | async-start | bytes 786432 | tf_op jit(solution)/shard_map/all_to_all | solution.py:317
  486.1 9.8 copy-start.39
  486.1 206.4 %reduce-scatter.27.cloned.1.call-start = ((), (), s32[]{:S(2)}) async-start(), calls=%async_computation.30 | async-start | bytes 1474560 | tf_op jit(solution)/shard_map/reduce_scatter | solution.py:459
  502.1 192.5 %reduce-scatter.31.cloned.1.call-start = ((), (), s32[]{:S(2)}) async-start(), calls=%async_computation.32 | async-start | bytes 2949120 | tf_op jit(solution)/shard_map/reduce_scatter | solution.py:465
  510.1 9.7 copy-start.37
  534.5 25.0 %all-to-all-start.4 = ((bf16[256,4,192]{0,2,1:T(8,128)(2,1)}), bf16[256,4,192]{0,2,1:T(8,128)(2,1)S(1)}, u32[]{:S(2)}, u32[]{:S(2)}) async-start(bf16[256,4,192]{0,2,1:T(8,128)(2,1)} %bitcast.43), calls=%async_computation.4 | async-start | bytes 786432 | tf_op jit(solution)/shard_map/all_to_all | solution.py:317
  560.2 10.8 slice-start.2
  595.9 17.7 %slice-start.4 = ((s8[6291456]{0:T(1024)(128)(4,1)}), s8[2097152]{0:T(1024)(128)(4,1)S(1)}, s32[]{:S(2)}) async-start(s8[6291456]{0:T(1024)(128)(4,1)} %bitcast.412), calls=%async_computation.47 | async-start | bytes 4194304
  602.7 32.6 %all-to-all-start.7 = ((bf16[1024,3,192]{2,1,0:T(4,128)(2,1)}), bf16[1024,3,192]{2,1,0:T(4,128)(2,1)}, u32[]{:S(2)}, u32[]{:S(2)}) async-start(bf16[1024,3,192]{2,1,0:T(4,128)(2,1)} %pad_maximum_fusion.2), calls=%async_computation.7 | async-start | bytes 4194304 | tf_op jit(solution)/shard_map/all_to_all | solution.py:327
  635.3 28.3 %all-to-all-start.5 = ((bf16[1024,3,192]{2,1,0:T(4,128)(2,1)}), bf16[1024,3,192]{2,1,0:T(4,128)(2,1)S(1)}, u32[]{:S(2)}, u32[]{:S(2)}) async-start(bf16[1024,3,192]{2,1,0:T(4,128)(2,1)} %pad_maximum_fusion.1), calls=%async_computation.5 | async-start | bytes 4194304 | tf_op jit(solution)/shard_map/all_to_all | solution.py:327
  638.9 71.7 %reduce-scatter.25.cloned.1.call-start = ((), (), s32[]{:S(2)}) async-start(), calls=%async_computation.29 | async-start | bytes 4423680 | tf_op jit(solution)/shard_map/reduce_scatter | solution.py:456
  638.9 27.0 %copy-start.7 = (bf16[2,256,768]{2,1,0:T(8,128)(2,1)S(1)}, bf16[2,256,768]{2,1,0:T(8,128)(2,1)}, u32[]{:S(2)}) copy-start(bf16[2,256,768]{2,1,0:T(8,128)(2,1)} %param.17) | copy-start | bytes 2359300
  638.9 27.0 %copy-start.107 = (f32[768]{0:T(1024)S(1)}, f32[768]{0:T(1024)}, u32[]{:S(2)}) copy-start(f32[768]{0:T(1024)} %copy-done.106) | copy-start | bytes 9220
  639.0 27.0 %copy-start.118 = (f32[768]{0:T(1024)S(1)}, f32[768]{0:T(1024)}, u32[]{:S(2)}) copy-start(f32[768]{0:T(1024)} %copy-done.117) | copy-start | bytes 9220
  639.0 27.0 %copy-start.133 = (f32[256]{0:T(256)S(1)}, f32[256]{0:T(256)}, u32[]{:S(2)}) copy-start(f32[256]{0:T(256)} %copy-done.132) | copy-start | bytes 3076
  639.0 27.0 %copy-start.138 = (f32[256]{0:T(256)S(1)}, f32[256]{0:T(256)}, u32[]{:S(2)}) copy-start(f32[256]{0:T(256)} %copy-done.137) | copy-start | bytes 3076
  671.6 90.1 %reduce-scatter.39.cloned.1.call-start = ((), (), s32[]{:S(2)}) async-start(), calls=%async_computation.36 | async-start | bytes 5898240 | tf_op jit(solution)/shard_map/reduce_scatter | solution.py:474
  680.0 132.0 %reduce-scatter.35.cloned.1.call-start = ((), (), s32[]{:S(2)}) async-start(), calls=%async_computation.34 | async-start | bytes 5898240 | tf_op jit(solution)/shard_map/reduce_scatter | solution.py:471
  688.1 188.4 %reduce-scatter.47.cloned.1.call-start = ((), (), s32[]{:S(2)}) async-start(), calls=%async_computation.40 | async-start | bytes 884736
  690.3 251.7 %reduce-scatter.51.cloned.1.call-start = ((), (), s32[]{:S(2)}) async-start(), calls=%async_computation.42 | async-start | bytes 884736
  692.4 314.7 %reduce-scatter.45.cloned.1.call-start = ((), (), s32[]{:S(2)}) async-start(), calls=%async_computation.39 | async-start | bytes 884736
  694.5 379.8 %reduce-scatter.49.cloned.1.call-start = ((), (), s32[]{:S(2)}) async-start(), calls=%async_computation.41 | async-start | bytes 1327104
  697.0 447.6 %reduce-scatter.43.cloned.1.call-start = ((), (), s32[]{:S(2)}) async-start(), calls=%async_computation.38 | async-start | bytes 2211840
  713.2 498.0 %reduce-scatter.41.cloned.1.call-start = ((), (), s32[]{:S(2)}) async-start(), calls=%async_computation.37 | async-start | bytes 1327104 | tf_op jit(solution)/shard_map/reduce_scatter | solution.py:494
  761.7 516.6 %reduce-scatter.37.cloned.1.call-start = ((), (), s32[]{:S(2)}) async-start(), calls=%async_computation.35 | async-start | bytes 1327104 | tf_op jit(solution)/shard_map/reduce_scatter | solution.py:493
  783.3 28.7 %copy-start.33 = (bf16[256,3,4,192]{0,3,2,1:T(8,128)(2,1)S(1)}, bf16[256,3,4,192]{0,3,2,1:T(8,128)(2,1)}, u32[]{:S(2)}) copy-start(bf16[256,3,4,192]{0,3,2,1:T(8,128)(2,1)} %copy.241) | copy-start | bytes 3538948
  812.0 46.9 %copy-start.19 = (f32[256,768]{1,0:T(8,128)S(1)}, f32[256,768]{1,0:T(8,128)}, u32[]{:S(2)}) copy-start(f32[256,768]{1,0:T(8,128)} %copy-done.18) | copy-start | bytes 2359300
  812.0 46.9 %copy-start.21 = (f32[256,768]{1,0:T(8,128)S(1)}, f32[256,768]{1,0:T(8,128)}, u32[]{:S(2)}) copy-start(f32[256,768]{1,0:T(8,128)} %copy-done.20) | copy-start | bytes 2359300
  (157 other events, 479.6 us)
Sparse Core Ops, SparseCore 0:
  10.2 52.2 all-gather.12
  64.7 62.7 all-gather.8
  129.7 39.8 all-gather.10
  171.6 39.8 all-gather.14
  213.5 39.8 all-gather.16
  255.4 77.2 all-gather.18
  334.8 77.6 all-gather.20
  463.1 26.1 reduce-scatter.28
  491.9 27.8 reduce-scatter.32
  522.2 30.0 reduce-scatter.26
  554.8 30.7 reduce-scatter.30
  671.7 38.8 reduce-scatter.24
  713.7 47.9 reduce-scatter.38
  764.1 47.7 reduce-scatter.34
  815.1 61.3 reduce-scatter.46
  879.7 62.2 reduce-scatter.50
  945.1 61.9 reduce-scatter.44
  1010.3 63.9 reduce-scatter.48
  1077.8 66.7 reduce-scatter.42
  1147.8 63.2 reduce-scatter.40
  1214.5 63.7 reduce-scatter.36
where the time goes:
time: 1310 us; the launch traced here: 1300 us
  waiting for transfers between devices  650 us (50%)
  matrix products  228 us (17%)
  local copies, waits for them, and re-layouts  157 us (12%)
  blocking collectives  133 us (10%)
  other arithmetic  71.5 us (5%)
  starting transfers between devices  39.3 us (3%)
  between operations  19.2 us (1%)
    unnamed x26, waiting for transfers between devices  246 us
    all_gather x1, waiting for transfers between devices, per_device(): lax.all_gather(shards[12], 'fsdp', axis=0, tiled=True)  74.4 us
    unnamed x2, blocking collectives  57.7 us
    all_gather x1, waiting for transfers between devices, per_device(): lax.all_gather(shards[11], 'fsdp', axis=0, tiled=True)  56.4 us
    reduce_scatter x1, waiting for transfers between devices, per_device(): lax.psum_scatter(part_up, 'fsdp', scatter_dimension=0, tiled=True)  55.7 us
    reduce_scatter x1, waiting for transfers between devices, per_device(): lax.psum_scatter(part_down, 'fsdp', scatter_dimension=0, tiled=True)  54.9 us
    unnamed x421, local copies, waits for them, and re-layouts  51 us
    all_gather x1, waiting for transfers between devices, per_device(): lax.all_gather(shards[2], 'fsdp', axis=0, tiled=True)  48.5 us
  transfers between devices with their start and end apart: 29, of which 16 were waited for; matrix products, arithmetic and copies ran while one was open for 30% of the time, Pallas kernels for 0%

commit v1 on v0

v1 whole, which is shorter than its diff:
```python
import functools

import jax
import jax.numpy as jnp
from jax import lax
from jax.experimental import pallas as pl
from jax.experimental.pallas import tpu as pltpu
from jax.sharding import PartitionSpec as P

HEADS = 12
HEAD_DIM = 64
SPAN = 64
EPS = 1e-05
NEG = -1e30
WINDOW = 512
SCALE = HEAD_DIM ** (-0.5)
BF = jnp.bfloat16
F32 = jnp.float32
LIMIT = 60 * 1024 * 1024

GELU_A = 0.7978845608028654
GELU_B = 0.044715


def dot(a, b):
    return lax.dot_general(a, b, (((1,), (0,)), ((), ())), preferred_element_type=F32)


def dot_nt(a, b):
    return lax.dot_general(a, b, (((1,), (1,)), ((), ())), preferred_element_type=F32)


def dot_tn(a, b):
    return lax.dot_general(a, b, (((0,), (0,)), ((), ())), preferred_element_type=F32)


def params(**kw):
    return pltpu.CompilerParams(vmem_limit_bytes=LIMIT, **kw)


def head_mask(rows, head):
    lane = lax.broadcasted_iota(jnp.int32, (rows, 2 * HEAD_DIM), 1)
    return (lane < HEAD_DIM) if head == 0 else (lane >= HEAD_DIM)


def allowed_keys(segc_ref, segr_ref, k0, k1, q0, q1):
    same = segc_ref[k0:k1, :] == segr_ref[:, q0:q1]
    kpos = lax.broadcasted_iota(jnp.int32, (k1 - k0, q1 - q0), 0) + k0
    qpos = lax.broadcasted_iota(jnp.int32, (k1 - k0, q1 - q0), 1) + q0
    return same & (kpos <= qpos)


def self_fwd_kernel(q_ref, k_ref, v_ref, segc_ref, segr_ref, o_ref, lse_ref, vt_ref, *, block):
    length = q_ref.shape[0]
    vt_ref[...] = v_ref[...].astype(F32).T.astype(BF)
    row = lax.broadcasted_iota(jnp.int32, (2 * HEAD_DIM, block), 0)
    for q0 in range(0, length, block):
        q1 = q0 + block
        k0 = max(0, q0 - WINDOW)
        keep = allowed_keys(segc_ref, segr_ref, k0, q1, q0, q1)
        q = q_ref[q0:q1, :]
        outs = []
        for head in range(2):
            qh = jnp.where(head_mask(block, head), q * SCALE, 0).astype(BF)
            s = jnp.where(keep, dot_nt(k_ref[k0:q1, :], qh), NEG)
            top = jnp.max(s, 0, keepdims=True)
            e = jnp.exp(s - top)
            total = jnp.sum(e, 0, keepdims=True)
            outs.append(dot(vt_ref[:, k0:q1], e.astype(BF)) / total)
            lse_ref[0, head : head + 1, q0:q1] = top + jnp.log(total)
        o = jnp.where(row < HEAD_DIM, outs[0], outs[1])
        o_ref[q0:q1, :] = o.T.astype(BF)


def self_forward(qkv, segc, segr):
    length, width = qkv.shape
    pairs = width // (6 * HEAD_DIM)
    pair = 2 * HEAD_DIM
    return pl.pallas_call(
        functools.partial(self_fwd_kernel, block=256),
        grid=(pairs,),
        in_specs=[
            pl.BlockSpec((length, pair), lambda j: (0, j)),
            pl.BlockSpec((length, pair), lambda j: (0, pairs + j)),
            pl.BlockSpec((length, pair), lambda j: (0, 2 * pairs + j)),
            pl.BlockSpec((length, 1), lambda j: (0, 0)),
            pl.BlockSpec((1, length), lambda j: (0, 0)),
        ],
        out_specs=[
            pl.BlockSpec((length, pair), lambda j: (0, j)),
            pl.BlockSpec((1, 8, length), lambda j: (j, 0, 0)),
        ],
        out_shape=[
            jax.ShapeDtypeStruct((length, pairs * pair), BF),
            jax.ShapeDtypeStruct((pairs, 8, length), F32),
        ],
        scratch_shapes=[pltpu.VMEM((pair, length), BF)],
        compiler_params=params(),
        cost_estimate=pl.CostEstimate(
            flops=8 * pairs * length * length * HEAD_DIM,
            bytes_accessed=10 * length * pairs * pair,
            transcendentals=2 * pairs * length * length // 2,
        ),
        name="self_forward",
    )(qkv, qkv, qkv, segc, segr)


def self_bwd_kernel(
    q_ref, k_ref, v_ref, do_ref, segc_ref, segr_ref, lse_ref, dq_ref, dk_ref, dv_ref, kt_ref, dka, dva, *, block
):
    length = q_ref.shape[0]
    kt_ref[...] = k_ref[...].astype(F32).T.astype(BF)
    dka[...] = jnp.zeros_like(dka)
    dva[...] = jnp.zeros_like(dva)
    row = lax.broadcasted_iota(jnp.int32, (2 * HEAD_DIM, block), 0)
    for q0 in range(0, length, block):
        q1 = q0 + block
        k0 = max(0, q0 - WINDOW)
        keep = allowed_keys(segc_ref, segr_ref, k0, q1, q0, q1)
        q = q_ref[q0:q1, :]
        do = do_ref[q0:q1, :]
        dqs = []
        for head in range(2):
            mine = head_mask(block, head)
            qh = jnp.where(mine, q * SCALE, 0).astype(BF)
            doh = jnp.where(mine, do, 0).astype(BF)
            s = jnp.where(keep, dot_nt(k_ref[k0:q1, :], qh), NEG)
            p = jnp.exp(s - lse_ref[0, head : head + 1, q0:q1])
            dp = dot_nt(v_ref[k0:q1, :], doh)
            delta = jnp.sum(p * dp, 0, keepdims=True)
            ds = (p * (dp - delta)).astype(BF)
            dka[k0:q1, :] += dot(ds, qh)
            dva[k0:q1, :] += dot(p.astype(BF), doh)
            dqs.append(dot(kt_ref[:, k0:q1], ds))
        dq = jnp.where(row < HEAD_DIM, dqs[0], dqs[1]) * SCALE
        dq_ref[q0:q1, :] = dq.T.astype(BF)
    dk_ref[...] = dka[...].astype(BF)
    dv_ref[...] = dva[...].astype(BF)


def self_backward(qkv, do, segc, segr, lse):
    length, width = qkv.shape
    pairs = width // (6 * HEAD_DIM)
    pair = 2 * HEAD_DIM
    column = pl.BlockSpec((length, pair), lambda j: (0, j))
    return pl.pallas_call(
        functools.partial(self_bwd_kernel, block=256),
        grid=(pairs,),
        in_specs=[
            column,
            pl.BlockSpec((length, pair), lambda j: (0, pairs + j)),
            pl.BlockSpec((length, pair), lambda j: (0, 2 * pairs + j)),
            column,
            pl.BlockSpec((length, 1), lambda j: (0, 0)),
            pl.BlockSpec((1, length), lambda j: (0, 0)),
            pl.BlockSpec((1, 8, length), lambda j: (j, 0, 0)),
        ],
        out_specs=[column] * 3,
        out_shape=[jax.ShapeDtypeStruct((length, pairs * pair), BF)] * 3,
        scratch_shapes=[
            pltpu.VMEM((pair, length), BF),
            pltpu.VMEM((length, pair), F32),
            pltpu.VMEM((length, pair), F32),
        ],
        compiler_params=params(),
        cost_estimate=pl.CostEstimate(
            flops=20 * pairs * length * length * HEAD_DIM,
            bytes_accessed=16 * length * pairs * pair,
            transcendentals=pairs * length * length,
        ),
        name="self_backward",
    )(qkv, qkv, qkv, do, segc, segr, lse)


def stack_heads(block):
    rows = block.shape[0]
    return jnp.concatenate(
        [jnp.where(head_mask(rows, head), block, 0) for head in range(2)], 0
    ).astype(BF)


def unstack_heads(block):
    rows = block.shape[0] // 2
    return jnp.where(head_mask(rows, 0), block[:rows], block[rows:])


def cross_weights(k, qs):
    s = dot_nt(k, qs)
    e = jnp.exp(s - jnp.max(s, 0, keepdims=True))
    return e, jnp.sum(e, 0, keepdims=True)


def cross_fwd_kernel(q_ref, k_ref, v_ref, o_ref):
    pair = 2 * HEAD_DIM
    for at in range(0, q_ref.shape[1], pair):
        cols = slice(at, at + pair)
        qs = stack_heads(q_ref[:, cols] * SCALE)
        e, total = cross_weights(k_ref[:, cols], qs)
        o = dot_tn((e / total).astype(BF), v_ref[:, cols])
        o_ref[:, cols] = unstack_heads(o).astype(BF)


def cross_forward(cq, ckv):
    tokens, width = cq.shape
    spans = tokens // SPAN
    memory = ckv.shape[0] // spans
    return pl.pallas_call(
        cross_fwd_kernel,
        grid=(spans,),
        in_specs=[
            pl.BlockSpec((SPAN, width), lambda i: (i, 0)),
            pl.BlockSpec((memory, width), lambda i: (i, 0)),
            pl.BlockSpec((memory, width), lambda i: (i, 1)),
        ],
        out_specs=pl.BlockSpec((SPAN, width), lambda i: (i, 0)),
        out_shape=jax.ShapeDtypeStruct((tokens, width), BF),
        compiler_params=params(),
        cost_estimate=pl.CostEstimate(
            flops=4 * tokens * memory * width,
            bytes_accessed=4 * tokens * width + 4 * spans * memory * width,
            transcendentals=tokens * memory * HEADS,
        ),
        name="cross_forward",
    )(cq, ckv, ckv)


def cross_bwd_kernel(q_ref, k_ref, v_ref, do_ref, dq_ref, dkv_ref):
    pair = 2 * HEAD_DIM
    width = q_ref.shape[1]
    for at in range(0, width, pair):
        cols = slice(at, at + pair)
        qs = stack_heads(q_ref[:, cols] * SCALE)
        dos = stack_heads(do_ref[:, cols])
        k = k_ref[:, cols]
        e, total = cross_weights(k, qs)
        p = e / total
        dp = dot_nt(v_ref[:, cols], dos)
        delta = jnp.sum(p * dp, 0, keepdims=True)
        ds = (p * (dp - delta)).astype(BF)
        dq_ref[:, cols] = (unstack_heads(dot_tn(ds, k)) * SCALE).astype(BF)
        dkv_ref[:, cols] = dot(ds, qs).astype(BF)
        dkv_ref[:, width + at : width + at + pair] = dot(p.astype(BF), dos).astype(BF)


def cross_backward(cq, ckv, do):
    tokens, width = cq.shape
    spans = tokens // SPAN
    memory = ckv.shape[0] // spans
    return pl.pallas_call(
        cross_bwd_kernel,
        grid=(spans,),
        in_specs=[
            pl.BlockSpec((SPAN, width), lambda i: (i, 0)),
            pl.BlockSpec((memory, width), lambda i: (i, 0)),
            pl.BlockSpec((memory, width), lambda i: (i, 1)),
            pl.BlockSpec((SPAN, width), lambda i: (i, 0)),
        ],
        out_specs=[
            pl.BlockSpec((SPAN, width), lambda i: (i, 0)),
            pl.BlockSpec((memory, 2 * width), lambda i: (i, 0)),
        ],
        out_shape=[
            jax.ShapeDtypeStruct((tokens, width), BF),
            jax.ShapeDtypeStruct((spans * memory, 2 * width), BF),
        ],
        compiler_params=params(),
        cost_estimate=pl.CostEstimate(
            flops=10 * tokens * memory * width,
            bytes_accessed=6 * tokens * width + 8 * spans * memory * width,
            transcendentals=tokens * memory * HEADS,
        ),
        name="cross_backward",
    )(cq, ckv, ckv, do)


def ffn_kernel(h_ref, dy_ref, *refs, quarters, carry, chunk):
    ups, downs = refs[:quarters], refs[quarters : 2 * quarters]
    rest = refs[2 * quarters :]
    if carry:
        y0_ref, dh0_ref, rest = rest[0], rest[1], rest[2:]
    y_ref, dh_ref = rest[0], rest[1]
    grads = rest[2:]
    step = pl.program_id(0)
    width = h_ref.shape[1]

    @pl.when(step == 0)
    def _():
        y_ref[...] = y0_ref[...] if carry else jnp.zeros_like(y_ref)
        dh_ref[...] = dh0_ref[...] if carry else jnp.zeros_like(dh_ref)

    h = h_ref[...]
    dy = dy_ref[...]
    at = pl.multiple_of(step * chunk, chunk)
    for up_ref, down_ref, g_ref in zip(ups, downs, grads):
        up, down = up_ref[...], down_ref[...]
        u = dot(h, up)
        t = jnp.tanh(GELU_A * (u + GELU_B * (u * u * u)))
        gl = (0.5 * u * (1.0 + t)).astype(BF)
        y_ref[...] += dot(gl, down)
        slope = 0.5 * (1.0 + t) + 0.5 * u * (1.0 - t * t) * (GELU_A * (1.0 + 3.0 * GELU_B * (u * u)))
        du = (dot_nt(dy, down) * slope).astype(BF)
        dh_ref[...] += dot_nt(du, up)
        g_ref[:, pl.ds(at, chunk)] = dot_tn(h, du).astype(BF)
        g_ref[pl.ds(at, chunk), pl.ds(width, width)] = dot_tn(gl, dy).astype(BF)


def feed_forward(h, dy, weights, carry=None):
    tokens, width = h.shape
    n = len(weights)
    hidden = weights[0].shape[0]
    chunk = 256
    whole = pl.BlockSpec((tokens, width), lambda j: (0, 0))
    operands = [h, dy, *weights, *weights]
    in_specs = [whole, whole]
    in_specs += [pl.BlockSpec((width, chunk), lambda j: (0, j))] * n
    in_specs += [pl.BlockSpec((chunk, width), lambda j: (j, 1))] * n
    if carry is not None:
        operands += list(carry)
        in_specs += [whole, whole]
    out = pl.pallas_call(
        functools.partial(ffn_kernel, quarters=n, carry=carry is not None, chunk=chunk),
        grid=(hidden // chunk,),
        in_specs=in_specs,
        out_specs=[whole, whole] + [pl.BlockSpec((hidden, 2 * width), lambda j: (0, 0))] * n,
        out_shape=[jax.ShapeDtypeStruct((tokens, width), F32)] * 2
        + [jax.ShapeDtypeStruct((hidden, 2 * width), BF)] * n,
        compiler_params=params(),
        cost_estimate=pl.CostEstimate(
            flops=12 * n * tokens * width * hidden,
            bytes_accessed=8 * n * width * hidden + 16 * tokens * width,
            transcendentals=n * tokens * hidden,
        ),
        name="feed_forward",
    )(*operands)
    return out[0], out[1], out[2:]


def assemble_kernel(idx_ref, *refs, n, rows):
    pieces, out_ref, sem = refs[:n], refs[n], refs[n + 1]
    copies = []
    for i in range(n):
        at = pl.multiple_of(idx_ref[i] * rows, rows)
        copies.append(pltpu.make_async_copy(pieces[i], out_ref.at[pl.ds(at, rows), :], sem.at[i]))
    for copy in copies:
        copy.start()
    for copy in copies:
        copy.wait()


def assemble(pieces, places):
    rows, cols = pieces[0].shape
    n = len(pieces)
    return pl.pallas_call(
        functools.partial(assemble_kernel, n=n, rows=rows),
        grid_spec=pltpu.PrefetchScalarGridSpec(
            num_scalar_prefetch=1,
            grid=(1,),
            in_specs=[pl.BlockSpec(memory_space=pl.ANY)] * n,
            out_specs=pl.BlockSpec((n * rows, cols), lambda i, idx: (0, 0)),
            scratch_shapes=[pltpu.SemaphoreType.DMA((n,))],
        ),
        out_shape=jax.ShapeDtypeStruct((n * rows, cols), pieces[0].dtype),
        compiler_params=params(),
        cost_estimate=pl.CostEstimate(
            flops=0, bytes_accessed=4 * n * rows * cols, transcendentals=0
        ),
        name="assemble",
    )(jnp.stack(places).astype(jnp.int32), *pieces)


class Place:
    def __init__(self):
        self.n = lax.axis_size("fsdp")
        f = lax.axis_index("fsdp")
        s = lax.axis_index("seq")
        self.z, self.y = f // 2, f % 2
        self.x, self.c = s // 2, s % 2
        self.s = s
        self.direct = self.n == 8

    def swap_core(self, value):
        return lax.ppermute(value, "seq", [(0, 1), (1, 0), (2, 3), (3, 2)])

    def swap_x(self, value):
        return lax.ppermute(value, "seq", [(0, 2), (2, 0), (1, 3), (3, 1)])

    def swap_y(self, value):
        return lax.ppermute(value, "fsdp", [(i, i ^ 1) for i in range(self.n)])

    def shift_z(self, value, hops):
        return lax.ppermute(value, "fsdp", [(i, (i + 2 * hops) % self.n) for i in range(self.n)])

    def gather(self, piece):
        if not self.direct:
            return lax.all_gather(piece, "fsdp", axis=0, tiled=True)
        columns = [piece] + [self.shift_z(piece, k) for k in (1, 2, 3)]
        others = [self.swap_y(p) for p in columns]
        base = [2 * ((self.z - k) % 4) for k in range(4)]
        return assemble(
            columns + others, [b + self.y for b in base] + [b + 1 - self.y for b in base]
        )

    def scatter(self, blocks):
        rows, cols = blocks.shape[1:]
        if not self.direct:
            return lax.psum_scatter(
                blocks.astype(BF), "fsdp", scatter_dimension=0, tiled=False
            ).astype(F32)
        blocks = blocks.reshape(4, 2, rows, cols)
        sent = pick(blocks, 1 - self.y, 1)
        kept = pick(blocks, self.y, 1)
        column = (kept.astype(F32) + self.swap_y(sent.astype(BF)).astype(F32)).astype(BF)
        total = pick(column, self.z, 0).astype(F32)
        for k in (1, 2, 3):
            total = total + self.shift_z(pick(column, (self.z + k) % 4, 0), k).astype(F32)
        return total


def pick(value, index, axis):
    return lax.dynamic_index_in_dim(value, index, axis, keepdims=False)


def ordered(flag, first, second, axis):
    low = jnp.where(flag == 0, first, second)
    high = jnp.where(flag == 0, second, first)
    return jnp.stack([low, high], axis)


def norm_stats(values):
    centre = values - jnp.mean(values, -1, keepdims=True)
    r = lax.rsqrt(jnp.mean(centre * centre, -1, keepdims=True) + EPS)
    return centre * r, r


def norm(values, gain, bias):
    xhat, _ = norm_stats(values)
    return (xhat * gain + bias).astype(BF)


def norm_back(values, gain, dh):
    xhat, r = norm_stats(values)
    dg = dh * gain
    dv = r * (
        dg - jnp.mean(dg, -1, keepdims=True) - xhat * jnp.mean(dg * xhat, -1, keepdims=True)
    )
    return dv, jnp.sum(dh * xhat, 0), jnp.sum(dh, 0)


def per_device(
    inputs, segments, neighbours,
    ln1_gain, ln1_bias, w_qkv, w_attn_out, ln2_gain, ln2_bias, cross_q, cross_kv, cross_out,
    ln3_gain, ln3_bias, w_up, w_down, out_grad,
):
    at = Place()
    x, c = at.x, at.c
    seqs, piece, width = inputs.shape
    half = width // 2
    rows = w_qkv.shape[0]
    tokens = seqs * piece

    theirs = at.swap_x(pick(inputs, 1 - x, 0))
    mine = pick(inputs, x, 0)
    blocks = ordered(x, mine, theirs, 0)
    sequence = ordered(c, blocks, at.swap_core(blocks), 1).reshape(4 * piece, width)
    seg = pick(segments, x, 0)
    segc, segr = seg[:, None], seg[None, :]

    vectors = jnp.stack([ln1_gain, ln1_bias, ln2_gain, ln2_bias, ln3_gain, ln3_bias], 1)
    vectors = jnp.pad(vectors, ((0, 0), (0, 128 - vectors.shape[1])))
    qkv_half = pick(w_qkv.reshape(rows, 3, 2, half), c, 2).reshape(rows, 3 * half)
    group_a = at.gather(jnp.concatenate([qkv_half, vectors], 1))
    wqkv = group_a[:, : 3 * half]
    gains = group_a[:, 3 * half : 3 * half + 6].T.astype(F32)
    g1, b1, g2, b2, g3, b3 = (gains[i] for i in range(6))

    def half_of(weight):
        return lax.dynamic_slice_in_dim(weight, c * (weight.shape[1] // 2), weight.shape[1] // 2, 1)

    group_b = at.gather(
        jnp.concatenate([half_of(w) for w in (cross_kv, w_attn_out, cross_q, cross_out)], 1)
    )
    group_b2 = at.swap_core(group_b)

    def both(start, size):
        a, b = group_b[:, start : start + size], group_b2[:, start : start + size]
        return ordered(c, a, b, 1).reshape(width, 2 * size)

    wckv = both(0, width)
    wao = both(width, half)
    wcq = both(width + half, half)
    wco = both(2 * width, half)

    unit = w_down.shape[0] // 4
    up_quarter = pick(w_up.reshape(rows, -1, 4, unit), at.s, 2).reshape(rows, -1)
    down_quarter = pick(w_down.reshape(4, unit, width), at.s, 0)
    q00 = at.gather(jnp.concatenate([up_quarter, down_quarter], 1))
    q10 = at.swap_x(q00)
    q01 = at.swap_core(q00)
    q11 = at.swap_core(q10)

    seqf = sequence.astype(F32)
    h1 = norm(seqf, g1, b1)
    qkv = dot(h1, wqkv).astype(BF)
    att_heads, lse = self_forward(qkv, segc, segr)
    by_x = att_heads.reshape(2, 2, piece, half)
    got = at.swap_x(pick(by_x, 1 - x, 0))
    chip = ordered(x, pick(by_x, x, 0), got, 0)
    got = at.swap_core(pick(chip, 1 - c, 1))
    att = ordered(c, pick(chip, c, 1), got, 2).reshape(tokens, width)

    xin = inputs.reshape(tokens, width).astype(F32)
    x1 = xin + dot(att, wao)
    h2 = norm(x1, g2, b2)
    cq = dot(h2, wcq).astype(BF)
    nb = neighbours.reshape(-1, width)
    ckv = dot(nb, wckv).astype(BF)
    cro = cross_forward(cq, ckv)
    x2 = x1 + dot(cro, wco)
    h3 = norm(x2, g3, b3)
    dy = out_grad.reshape(tokens, width)
    y, dh3, own_grads = feed_forward(h3, dy, [q00, q10])
    y, dh3, far_grads = feed_forward(h3, dy, [q01, q11], (y, dh3))
    outputs = (x2 + y).astype(BF).reshape(seqs, piece, width)

    f0 = at.swap_core(far_grads[0])
    f1 = at.swap_core(far_grads[1])
    away = (own_grads[1].astype(F32) + f1.astype(F32)).astype(BF)
    ffn_sum = own_grads[0].astype(F32) + f0.astype(F32) + at.swap_x(away).astype(F32)
    ffn_own = at.scatter(ffn_sum.reshape(at.n, rows, 2 * width)).astype(BF)
    ffn_x = ordered(x, ffn_own, at.swap_x(ffn_own), 0)
    ffn_all = ordered(c, ffn_x, at.swap_core(ffn_x), 1).reshape(4, rows, 2 * width).astype(F32)
    grad_up = ffn_all[:, :, :width].reshape(4, rows, -1, unit).transpose(1, 2, 0, 3).reshape(rows, -1)
    grad_down = ffn_all[:, :, width:].reshape(4 * unit, width)

    dv3, gg3, gb3 = norm_back(x2, g3, dh3)
    dx2 = dy.astype(F32) + dv3
    dc = dx2.astype(BF)
    grad_co = dot_tn(cro, dc).astype(BF)
    dcro = dot_nt(dc, wco).astype(BF)
    dcq, dckv = cross_backward(cq, ckv, dcro)
    grad_cq = dot_tn(h2, dcq).astype(BF)
    dh2 = dot_nt(dcq, wcq)
    grad_ckv = dot_tn(nb, dckv).astype(BF)
    neighbour_grad = dot_nt(dckv, wckv)
    dv2, gg2, gb2 = norm_back(x1, g2, dh2)
    dx1 = dx2 + dv2
    da = dx1.astype(BF)
    grad_ao = dot_tn(att, da).astype(BF)
    datt = dot_nt(da, wao).astype(BF)

    datt = datt.reshape(seqs, piece, 2, half)
    got = at.swap_core(pick(datt, 1 - c, 2))
    chip = ordered(c, pick(datt, c, 2), got, 1)
    got = at.swap_x(pick(chip, 1 - x, 0))
    do = ordered(x, pick(chip, x, 0), got, 0).reshape(4 * piece, half)
    dqkv = jnp.concatenate(self_backward(qkv, do, segc, segr, lse), 1)
    grad_qkv = dot_tn(h1, dqkv).astype(BF)
    part = dot_nt(dqkv, wqkv).astype(BF).reshape(2, 2, piece, width)
    got = at.swap_core(pick(part, 1 - c, 1))
    chip = (pick(part, c, 1).astype(F32) + got.astype(F32)).astype(BF)
    got = at.swap_x(pick(chip, 1 - x, 0))
    dh1 = ordered(x, pick(chip, x, 0), got, 0).reshape(tokens, width).astype(F32)
    dv1, gg1, gb1 = norm_back(xin, g1, dh1)
    input_grad = (dx1 + dv1).reshape(seqs, piece, width)

    def reduce_halves(halves_sent, halves_kept):
        got = at.swap_core(halves_sent)
        blocks = halves_kept.astype(F32) + got.astype(F32)
        return finish(blocks)

    def finish(blocks):
        own = at.scatter(blocks.reshape(at.n, rows, -1))
        return own + at.swap_x(own.astype(BF)).astype(F32)

    def halves(grad, which):
        return lax.dynamic_slice_in_dim(grad, which * (grad.shape[1] // 2), grad.shape[1] // 2, 1)

    def joined(own, other):
        return ordered(c, own, other, 1).reshape(rows, -1)

    three = (grad_ckv, grad_cq, grad_co)
    own_b = reduce_halves(
        jnp.concatenate([halves(g, 1 - c) for g in three], 1),
        jnp.concatenate([halves(g, c) for g in three], 1),
    )
    far_b = at.swap_core(own_b.astype(BF)).astype(F32)
    out_ckv = joined(own_b[:, :width], far_b[:, :width])
    out_cq = joined(own_b[:, width : width + half], far_b[:, width : width + half])
    out_co = joined(own_b[:, width + half :], far_b[:, width + half :])

    vec = jnp.stack([gg1, gb1, gg2, gb2, gg3, gb3], 1)
    vec = vec + at.swap_core(vec)
    vec = jnp.pad(vec, ((0, 0), (0, 128 - 6)))
    kept_ao = halves(grad_ao, c).astype(F32) + at.swap_core(halves(grad_ao, 1 - c)).astype(F32)
    own_a = finish(jnp.concatenate([grad_qkv.astype(F32), kept_ao, vec], 1))
    far_a = at.swap_core(own_a[:, : 4 * half].astype(BF)).astype(F32)
    out_qkv = ordered(
        c, own_a[:, : 3 * half].reshape(rows, 3, half), far_a[:, : 3 * half].reshape(rows, 3, half), 2
    ).reshape(rows, 6 * half)
    out_ao = joined(own_a[:, 3 * half : 4 * half], far_a[:, 3 * half :])
    vecs = own_a[:, 4 * half : 4 * half + 6].T

    return (
        outputs, input_grad, neighbour_grad.reshape(neighbours.shape),
        vecs[0], vecs[1], out_qkv, out_ao, vecs[2], vecs[3], out_cq, out_ckv, out_co,
        vecs[4], vecs[5], grad_up, grad_down,
    )


def solution(mesh):
    row, mat = P("fsdp"), P("fsdp", None)
    tok, mem = P("fsdp", "seq", None), P("fsdp", "seq", None, None)
    weights = (row, row, mat, mat, row, row, mat, mat, mat, row, row, mat, mat)
    return jax.shard_map(
        per_device,
        mesh=mesh,
        in_specs=(tok, mat, mem, *weights, tok),
        out_specs=(tok, tok, mem, *weights),
        check_vma=False,
    )
```

time: 1310 us -> 568 us (0.43)
  waiting for transfers between devices: 650 us -> 177 us
  matrix products: 228 us -> 49.5 us
  blocking collectives: 133 us -> 0 us
  Pallas kernels: 0 us -> 99.3 us
  local copies, waits for them, and re-layouts: 157 us -> 92.2 us
  starting transfers between devices: 39.3 us -> 77.1 us
  between operations: 19.2 us -> 2.09 us
    unnamed x26 -> x0, waiting for transfers between devices: 246 us -> none
    reduce_scatter x9 -> x0, waiting for transfers between devices: 194 us -> none  [the longest x1 55.7 us: per_device(): lax.psum_scatter(part_up, 'fsdp', scatter_dimension=0, tiled=True)]
    all_gather x7 -> x0, waiting for transfers between devices: 183 us -> none  [the longest x1 74.4 us: per_device(): lax.all_gather(shards[12], 'fsdp', axis=0, tiled=True)]
    dot_general x78 -> x15, matrix products: 228 us -> 49.5 us  [the longest x5 19.7 us: dot(): lax.dot_general(a, b, (((1,), (0,)), ((), ())), preferred_element_type=F32)]
    ppermute x0 -> x57, waiting for transfers between devices: none -> 177 us  [the longest x15 85.8 us: swap_y(): return lax.ppermute(value, 'fsdp', [(i, i ^ 1) for i in range(self.n)])]
    pallas_call x0 -> x9, Pallas kernels: none -> 99.3 us  [the longest x2 29.1 us: feed_forward(): pl.pallas_call(functools.partial(ffn_kernel, quarters=n, carry=carry is n...]
    ppermute x0 -> x57, starting transfers between devices: none -> 77.1 us  [the longest x15 31.9 us: swap_y(): return lax.ppermute(value, 'fsdp', [(i, i ^ 1) for i in range(self.n)])]
    all_gather x7 -> x0, blocking collectives: 62 us -> none  [the longest x1 10.2 us: per_device(): lax.all_gather(own_up.astype(jnp.bfloat16), 'seq', axis=1, tiled=True)]
  transfers between devices with their start and end apart: 29 -> 57, of which waited for: 16 -> 25; matrix products, arithmetic and copies ran while one was open for 30% -> 28% of each run, Pallas kernels for 0% -> 12%
where the time goes in v1:
time: 568 us; the launch traced here: 561 us
  waiting for transfers between devices  177 us (31%)
  Pallas kernels  99.3 us (17%)
  local copies, waits for them, and re-layouts  92.2 us (16%)
  starting transfers between devices  77.1 us (14%)
  other arithmetic  63 us (11%)
  matrix products  49.5 us (9%)
    ppermute x15, waiting for transfers between devices, swap_y(): return lax.ppermute(value, 'fsdp', [(i, i ^ 1) for i in range(self.n)])  85.8 us
    ppermute x18, waiting for transfers between devices, shift_z(): lax.ppermute(value, 'fsdp', [(i, (i + 2 * hops) % self.n) for i in range(...  69.3 us
    ppermute x15, starting transfers between devices, swap_y(): return lax.ppermute(value, 'fsdp', [(i, i ^ 1) for i in range(self.n)])  31.9 us
    pallas_call x2, Pallas kernels, feed_forward(): pl.pallas_call(functools.partial(ffn_kernel, quarters=n, carry=carry is n...  29.1 us
    ppermute x9, waiting for transfers between devices, swap_x(): return lax.ppermute(value, 'seq', [(0, 2), (2, 0), (1, 3), (3, 1)])  22.3 us
    another operation x24, other arithmetic, ordered(): return jnp.stack([low, high], axis)  20.1 us
    ppermute x18, starting transfers between devices, shift_z(): lax.ppermute(value, 'fsdp', [(i, (i + 2 * hops) % self.n) for i in range(...  20 us
    dot_general x5, matrix products, dot(): lax.dot_general(a, b, (((1,), (0,)), ((), ())), preferred_element_type=F32)  19.7 us
  transfers between devices with their start and end apart: 57, of which 25 were waited for; matrix products, arithmetic and copies ran while one was open for 28% of the time, Pallas kernels for 12%

profile of v1, /device:TPU:9, one launch (start us, length us, event | category | flops | bytes accessed | tf_op | source)
XLA Modules:
  0.0 560.6 jit_solution(10511512289399015870)
XLA Ops:
  2.8 2.5 dynamic-slice_reduce_fusion
  14.2 2.9 reshape.342
  17.1 2.4 dynamic-slice_reduce_fusion.1
  28.3 3.1 collective-permute-start.20
  31.4 13.6 %collective-permute-start.22 = (bf16[96,1536]{1,0:T(8,128)(2,1)S(1)}, bf16[96,1536]{1,0:T(8,128)(2,1)S(1)}, u32[]{:S(2)}, u32[]{:S(2)}) collective-permute-start(bf16[96,1536]{1,0:T(8,128)(2,1)S(1)} %pad_maximum_fusion.13.refs_0_), channel_id=1, source_target_pairs={{0,4},{4,0},{8,12},{12,8},{16,20},{20,16},{24,28},{28,24},{1,5},{5... | collective-permute-start | bytes 884744 | tf_op jit(solution)/shard_map/ppermute | solution.py:388
  49.1 4.4 collective-permute-done.20.refs_2_
  53.5 3.2 collective-permute-start.12
  56.7 15.1 %collective-permute-done.21.refs_3_ = bf16[96,1536]{1,0:T(8,128)(2,1)} collective-permute-done((bf16[96,1536]{1,0:T(8,128)(2,1)S(1)}, bf16[96,1536]{1,0:T(8,128)(2,1)}, u32[]{:S(2)}, u32[]{:S(2)}) %collective-permute-start.21) | collective-permute-done | bytes 294944 | tf_op jit(solution)/shard_map/ppermute | solution.py:391
  86.0 3.1 collective-permute-done.8.refs_7_
  93.5 3.6 assemble.3
  98.7 3.1 collective-permute-done.24.refs_6_
  103.9 4.2 collective-permute-done.25.refs_7_
  112.7 3.7 assemble.5.refs_0_.refs_2_
  118.1 5.8 %collective-permute-done.15.refs_5_ = bf16[96,1920]{1,0:T(8,128)(2,1)} collective-permute-done((bf16[96,1920]{1,0:T(8,128)(2,1)}, bf16[96,1920]{1,0:T(8,128)(2,1)}, u32[]{:S(2)}, u32[]{:S(2)}) %collective-permute-start.15) | collective-permute-done | bytes 368672 | tf_op jit(solution)/shard_map/ppermute | solution.py:388
  123.9 7.9 %collective-permute-done.16.refs_6_ = bf16[96,1920]{1,0:T(8,128)(2,1)} collective-permute-done((bf16[96,1920]{1,0:T(8,128)(2,1)}, bf16[96,1920]{1,0:T(8,128)(2,1)}, u32[]{:S(2)}, u32[]{:S(2)}) %collective-permute-start.16) | collective-permute-done | bytes 368672 | tf_op jit(solution)/shard_map/ppermute | solution.py:388
  131.8 7.9 %collective-permute-done.17.refs_7_ = bf16[96,1920]{1,0:T(8,128)(2,1)} collective-permute-done((bf16[96,1920]{1,0:T(8,128)(2,1)}, bf16[96,1920]{1,0:T(8,128)(2,1)}, u32[]{:S(2)}, u32[]{:S(2)}) %collective-permute-start.17) | collective-permute-done | bytes 368672 | tf_op jit(solution)/shard_map/ppermute | solution.py:388
  139.7 4.1 assemble.4
  150.1 3.7 convolution_convert_fusion.1.q_ref.k_ref.v_ref
  153.8 13.6 %self_forward.1 = (bf16[1024,384]{1,0:T(8,128)(2,1)}, f32[3,8,1024]{2,1,0:T(8,128)}) custom-call(bf16[1024,1152]{1,0:T(8,128)(2,1)} %convolution_convert_fusion.1.q_ref.k_ref.v_ref, bf16[1024,1152]{1,0:T(8,128)(2,1)} %convolution_convert_fusion.1.q_ref.k_ref.v_ref, bf16[1024,1152]{1,0:T(8,128)(2,1)} %convolution_convert_fusion.1.q_ref.k_ref.v_ref, ...), custom_call_target="tpu_custom_call" | custom-call | flops 1610612736 | bytes 3932160 | tf_op jit(solution)/shard_map/self_forward/pallas_call | solution.py:79
  171.2 8.0 %collective-permute-done.9 = bf16[2,256,384]{2,1,0:T(8,128)(2,1)} collective-permute-done((bf16[2,256,384]{2,1,0:T(8,128)(2,1)S(1)}, bf16[2,256,384]{2,1,0:T(8,128)(2,1)}, u32[]{:S(2)}, u32[]{:S(2)}) %collective-permute-start.9) | collective-permute-done | bytes 393248 | tf_op jit(solution)/shard_map/ppermute | solution.py:385
  191.4 4.3 copy.168
  195.6 3.5 select_bitcast_fusion.7
  200.3 2.4 copy.166
  202.7 2.6 fusion.63
  208.3 7.0 %fusion.k_ref.v_ref = bf16[2048,1536]{1,0:T(8,128)(2,1)} fusion(bf16[768,1536]{0,1:T(8,128)(2,1)S(1)} %bitcast.345, bf16[2048,768]{1,0:T(8,128)(2,1)S(1)} %bitcast.329), kind=kOutput, calls=%fused_computation.1 | convolution fusion | flops 4834983936 | bytes 11796480 | tf_op jit(solution)/shard_map/dot_general | solution.py:26
  216.5 2.4 copy.170
  218.8 2.4 copy.167
  221.2 3.5 convolution_convert_fusion.10.q_ref
  224.8 10.6 %cross_forward.1 = bf16[512,768]{1,0:T(8,128)(2,1)} custom-call(bf16[512,768]{1,0:T(8,128)(2,1)} %convolution_convert_fusion.10.q_ref, bf16[2048,1536]{1,0:T(8,128)(2,1)} %fusion.k_ref.v_ref, bf16[2048,1536]{1,0:T(8,128)(2,1)} %fusion.k_ref.v_ref), custom_call_target="tpu_custom_call" | custom-call | flops 402653184 | bytes 7864320 | tf_op jit(solution)/shard_map/cross_forward/pallas_call | solution.py:207
  235.3 2.9 fusion.64
  239.8 14.0 %feed_forward.2 = (f32[512,768]{1,0:T(8,128)}, f32[512,768]{1,0:T(8,128)}, bf16[768,1536]{1,0:T(8,128)(2,1)}, bf16[768,1536]{1,0:T(8,128)(2,1)}) custom-call(bf16[512,768]{1,0:T(8,128)(2,1)} %add_convert_fusion.2.h_ref, bf16[512,768]{1,0:T(8,128)(2,1)} %bitcast.357, bf16[768,1536]{1,0:T(8,128)(2,1)} %assemble.5.refs_0_.refs_2_, ...), custom_call_target="tpu_custom_call" | custom-call | flops 7247757312 | bytes 15728640 | tf_op jit(solution)/shard_map/feed_forward/pallas_call | solution.py:320
  253.8 15.1 %feed_forward.3 = (f32[512,768]{1,0:T(8,128)}, f32[512,768]{1,0:T(8,128)}, bf16[768,1536]{1,0:T(8,128)(2,1)}, bf16[768,1536]{1,0:T(8,128)(2,1)}) custom-call(bf16[512,768]{1,0:T(8,128)(2,1)} %add_convert_fusion.2.h_ref, bf16[512,768]{1,0:T(8,128)(2,1)} %bitcast.358, bf16[768,1536]{1,0:T(8,128)(2,1)} %collective-permute-done.26.refs_0_.refs_2_, ...), custom_call_target="tpu_custom_call" | custom-call | flops 7247757312 | bytes 15728640 | tf_op jit(solution)/shard_map/feed_forward/pallas_call | solution.py:320
  268.9 2.7 multiply_reduce_fusion.1
  271.8 3.0 multiply_add_fusion.1
  278.3 18.7 %cross_backward.1 = (bf16[512,768]{1,0:T(8,128)(2,1)}, bf16[2048,1536]{1,0:T(8,128)(2,1)}) custom-call(bf16[512,768]{1,0:T(8,128)(2,1)} %convolution_convert_fusion.10.q_ref, bf16[2048,1536]{1,0:T(8,128)(2,1)} %fusion.k_ref.v_ref, bf16[2048,1536]{1,0:T(8,128)(2,1)} %fusion.k_ref.v_ref, bf16[512,768]{1,0:T(8,128)(2,1)} %convolution_convert_fusion.9.do_ref), custom_call_target="tpu_custom_call" | custom-call | flops 1006632960 | bytes 14942208 | tf_op jit(solution)/shard_map/cross_backward/pallas_call | solution.py:249
  297.0 3.7 convolution_convert_fusion.6
  303.5 6.4 %convolution_convert_fusion.2 = bf16[1536,768]{1,0:T(8,128)(2,1)} fusion(bf16[2048,1536]{1,0:T(8,128)(2,1)S(1)} %copy-done.64, bf16[2048,768]{1,0:T(8,128)(2,1)S(1)} %bitcast.330), kind=kOutput, calls=%fused_computation.8 | convolution fusion | flops 4833017856 | bytes 11796480 | tf_op jit(solution)/shard_map/dot_general | solution.py:34
  323.0 6.1 %collective-permute-done.30 = bf16[2,256,384]{2,1,0:T(8,128)(2,1)S(1)} collective-permute-done((bf16[2,256,384]{2,1,0:T(8,128)(2,1)S(1)}, bf16[2,256,384]{2,1,0:T(8,128)(2,1)S(1)}, u32[]{:S(2)}, u32[]{:S(2)}) %collective-permute-start.30) | collective-permute-done | bytes 393248 | tf_op jit(solution)/shard_map/ppermute | solution.py:385
  330.3 16.0 %self_backward.1 = (bf16[1024,384]{1,0:T(8,128)(2,1)}, bf16[1024,384]{1,0:T(8,128)(2,1)}, bf16[1024,384]{1,0:T(8,128)(2,1)}) custom-call(bf16[1024,1152]{1,0:T(8,128)(2,1)} %convolution_convert_fusion.1.q_ref.k_ref.v_ref, bf16[1024,1152]{1,0:T(8,128)(2,1)} %convolution_convert_fusion.1.q_ref.k_ref.v_ref, ...), custom_call_target="tpu_custom_call" | custom-call | flops 4026531840 | bytes 6291456 | tf_op jit(solution)/shard_map/self_backward/pallas_call | solution.py:146
  352.9 7.1 %fusion.65 = f32[2,4,256,768]{3,2,1,0:T(8,128)} fusion(bf16[2,4,256,1536]{3,2,1,0:T(8,128)(2,1)S(1)} %bitcast.383, bf16[768,1536,1,1]{0,1,3,2:T(8,128)(2,1)S(1)} %bitcast.346), kind=kOutput, calls=%fused_computation.248 | convolution fusion | flops 4831838208 | bytes 14942208 | tf_op jit(solution)/shard_map/dot_general | solution.py:30
  363.0 4.0 fusion.1
  367.0 4.9 collective-permute-done.32
  381.2 2.5 copy-done.6
  386.4 4.4 convert_add_fusion.1
  390.8 6.1 %copy.182 = f32[768,1536]{1,0:T(8,128)} copy(f32[768,1536]{0,1:T(8,128)} %convert_add_fusion.1) | data formatting | bytes 9437184 | tf_op jit(solution)/shard_map/add | solution.py:568
  399.2 2.4 add_convert_fusion
  402.9 11.9 %collective-permute-done.35 = bf16[4,96,1664]{2,1,0:T(8,128)(2,1)} collective-permute-done((bf16[4,96,1664]{2,1,0:T(8,128)(2,1)}, bf16[4,96,1664]{2,1,0:T(8,128)(2,1)}, u32[]{:S(2)}, u32[]{:S(2)}) %collective-permute-start.35) | collective-permute-done | bytes 1277984 | tf_op jit(solution)/shard_map/ppermute | solution.py:388
  414.8 2.4 fusion.6
  417.5 22.6 %collective-permute-done.42 = bf16[4,96,1536]{2,1,0:T(8,128)(2,1)S(1)} collective-permute-done((bf16[4,96,1536]{2,1,0:T(8,128)(2,1)S(1)}, bf16[4,96,1536]{2,1,0:T(8,128)(2,1)S(1)}, u32[]{:S(2)}, u32[]{:S(2)}) %collective-permute-start.42) | collective-permute-done | bytes 1179680 | tf_op jit(solution)/shard_map/ppermute | solution.py:388
  443.8 3.1 collective-permute-start.44
  446.9 2.5 collective-permute-done.38
  449.6 13.2 %collective-permute-done.43 = bf16[96,1536]{1,0:T(8,128)(2,1)S(1)} collective-permute-done((bf16[96,1536]{1,0:T(8,128)(2,1)S(1)}, bf16[96,1536]{1,0:T(8,128)(2,1)S(1)}, u32[]{:S(2)}, u32[]{:S(2)}) %collective-permute-start.43) | collective-permute-done | bytes 294944 | tf_op jit(solution)/shard_map/ppermute | solution.py:391
  464.2 4.9 collective-permute-done.44
  469.1 4.5 collective-permute-done.45
  475.5 2.5 convert_add_fusion
  482.6 2.4 collective-permute-start.40
  488.9 18.2 %collective-permute-done.51 = bf16[4,96,1536]{2,1,0:T(8,128)(2,1)} collective-permute-done((bf16[4,96,1536]{2,1,0:T(8,128)(2,1)}, bf16[4,96,1536]{2,1,0:T(8,128)(2,1)}, u32[]{:S(2)}, u32[]{:S(2)}) %collective-permute-start.51) | collective-permute-done | bytes 1179680 | tf_op jit(solution)/shard_map/ppermute | solution.py:388
  507.2 2.4 fusion.7
  512.8 2.5 collective-permute-done.52
  515.3 17.2 %collective-permute-done.53 = bf16[96,1536]{1,0:T(8,128)(2,1)S(1)} collective-permute-done((bf16[96,1536]{1,0:T(8,128)(2,1)S(1)}, bf16[96,1536]{1,0:T(8,128)(2,1)S(1)}, u32[]{:S(2)}, u32[]{:S(2)}) %collective-permute-start.53) | collective-permute-done | bytes 294944 | tf_op jit(solution)/shard_map/ppermute | solution.py:391
  539.1 3.3 collective-permute-done.55
  550.2 2.9 reshape.355
  553.1 3.7 copy.188
  556.8 3.6 reshape.356
  (370 shorter events, 160.4 us)
Async XLA Ops:
  0.6 207.7 %copy-start = (bf16[2,4,256,768]{3,2,1,0:T(8,128)(2,1)S(1)}, bf16[2,4,256,768]{3,2,1,0:T(8,128)(2,1)}, u32[]{:S(2)}) copy-start(bf16[2,4,256,768]{3,2,1,0:T(8,128)(2,1)} %param.19) | copy-start | bytes 9437188
  6.2 20.9 %collective-permute-start.2 = (bf16[96,1280]{1,0:T(8,128)(2,1)}, bf16[96,1280]{1,0:T(8,128)(2,1)}, u32[]{:S(2)}, u32[]{:S(2)}) collective-permute-start(bf16[96,1280]{1,0:T(8,128)(2,1)} %fusion.55.refs_0_), channel_id=1, source_target_pairs={{0,8},{4,12},{8,16},{12,20},{16,24},{20,28},{24,0},{28,4},{1,9},{5... | collective-permute-start | bytes 737288 | tf_op jit(solution)/shard_map/ppermute | solution.py:391
  7.5 20.8 %collective-permute-start.3 = (bf16[96,1280]{1,0:T(8,128)(2,1)}, bf16[96,1280]{1,0:T(8,128)(2,1)}, u32[]{:S(2)}, u32[]{:S(2)}) collective-permute-start(bf16[96,1280]{1,0:T(8,128)(2,1)} %fusion.55.refs_0_), channel_id=1, source_target_pairs={{0,16},{4,20},{8,24},{12,28},{16,0},{20,4},{24,8},{28,12},{1,17},{... | collective-permute-start | bytes 737288 | tf_op jit(solution)/shard_map/ppermute | solution.py:391
  8.5 22.8 %collective-permute-start.4 = (bf16[96,1280]{1,0:T(8,128)(2,1)}, bf16[96,1280]{1,0:T(8,128)(2,1)}, u32[]{:S(2)}, u32[]{:S(2)}) collective-permute-start(bf16[96,1280]{1,0:T(8,128)(2,1)} %fusion.55.refs_0_), channel_id=1, source_target_pairs={{0,24},{4,28},{8,0},{12,4},{16,8},{20,12},{24,16},{28,20},{1,25},{... | collective-permute-start | bytes 737288 | tf_op jit(solution)/shard_map/ppermute | solution.py:391
  10.0 21.4 %collective-permute-start.5 = (bf16[96,1280]{1,0:T(8,128)(2,1)}, bf16[96,1280]{1,0:T(8,128)(2,1)}, u32[]{:S(2)}, u32[]{:S(2)}) collective-permute-start(bf16[96,1280]{1,0:T(8,128)(2,1)} %fusion.55.refs_0_), channel_id=1, source_target_pairs={{0,4},{4,0},{8,12},{12,8},{16,20},{20,16},{24,28},{28,24},{1,5},{5... | collective-permute-start | bytes 737288 | tf_op jit(solution)/shard_map/ppermute | solution.py:388
  13.0 60.5 %collective-permute-start = (bf16[256,768]{1,0:T(8,128)(2,1)}, bf16[256,768]{1,0:T(8,128)(2,1)}, u32[]{:S(2)}, u32[]{:S(2)}) collective-permute-start(bf16[256,768]{1,0:T(8,128)(2,1)} %dynamic-slice_bitcast_fusion.5), channel_id=1, source_target_pairs={{0,2},{2,0},{1,3},{3,1},{4,6},{6,4},{5,7},{7,5},{8,10},{10,8},{9,1... | collective-permute-start | bytes 1179656 | tf_op jit(solution)/shard_map/ppermute | solution.py:385
  23.0 50.5 %copy-start.44 = (bf16[96,1536]{1,0:T(8,128)(2,1)}, bf16[96,1536]{1,0:T(8,128)(2,1)S(1)}, u32[]{:S(2)}) copy-start(bf16[96,1536]{1,0:T(8,128)(2,1)S(1)} %pad_maximum_fusion.13.refs_0_) | copy-start | bytes 884740
  27.1 20.5 %collective-permute-start.19 = (bf16[96,1536]{1,0:T(8,128)(2,1)S(1)}, bf16[96,1536]{1,0:T(8,128)(2,1)}, u32[]{:S(2)}, u32[]{:S(2)}) collective-permute-start(bf16[96,1536]{1,0:T(8,128)(2,1)S(1)} %pad_maximum_fusion.13.refs_0_), channel_id=1, source_target_pairs={{0,8},{4,12},{8,16},{12,20},{16,24},{20,28},{24,0},{28,4},{1,9},{5... | collective-permute-start | bytes 884744 | tf_op jit(solution)/shard_map/ppermute | solution.py:391
  28.3 25.2 %collective-permute-start.20 = (bf16[96,1536]{1,0:T(8,128)(2,1)S(1)}, bf16[96,1536]{1,0:T(8,128)(2,1)}, u32[]{:S(2)}, u32[]{:S(2)}) collective-permute-start(bf16[96,1536]{1,0:T(8,128)(2,1)S(1)} %pad_maximum_fusion.13.refs_0_), channel_id=1, source_target_pairs={{0,16},{4,20},{8,24},{12,28},{16,0},{20,4},{24,8},{28,12},{1,17},{... | collective-permute-start | bytes 884744 | tf_op jit(solution)/shard_map/ppermute | solution.py:391
  31.4 40.4 %collective-permute-start.21 = (bf16[96,1536]{1,0:T(8,128)(2,1)S(1)}, bf16[96,1536]{1,0:T(8,128)(2,1)}, u32[]{:S(2)}, u32[]{:S(2)}) collective-permute-start(bf16[96,1536]{1,0:T(8,128)(2,1)S(1)} %pad_maximum_fusion.13.refs_0_), channel_id=1, source_target_pairs={{0,24},{4,28},{8,0},{12,4},{16,8},{20,12},{24,16},{28,20},{1,25},{... | collective-permute-start | bytes 884744 | tf_op jit(solution)/shard_map/ppermute | solution.py:391
  31.4 42.1 %collective-permute-start.22 = (bf16[96,1536]{1,0:T(8,128)(2,1)S(1)}, bf16[96,1536]{1,0:T(8,128)(2,1)S(1)}, u32[]{:S(2)}, u32[]{:S(2)}) collective-permute-start(bf16[96,1536]{1,0:T(8,128)(2,1)S(1)} %pad_maximum_fusion.13.refs_0_), channel_id=1, source_target_pairs={{0,4},{4,0},{8,12},{12,8},{16,20},{20,16},{24,28},{28,24},{1,5},{5... | collective-permute-start | bytes 884744 | tf_op jit(solution)/shard_map/ppermute | solution.py:388
  47.6 43.6 %copy-start.56 = (s32[2,1024]{1,0:T(2,128)S(1)}, s32[2,1024]{1,0:T(2,128)}, u32[]{:S(2)}) copy-start(s32[2,1024]{1,0:T(2,128)} %param.18) | copy-start | bytes 24580
  47.6 30.3 %collective-permute-start.11 = (bf16[96,1920]{1,0:T(8,128)(2,1)}, bf16[96,1920]{1,0:T(8,128)(2,1)}, u32[]{:S(2)}, u32[]{:S(2)}) collective-permute-start(bf16[96,1920]{1,0:T(8,128)(2,1)} %pad_maximum_fusion.12.refs_0_), channel_id=1, source_target_pairs={{0,8},{4,12},{8,16},{12,20},{16,24},{20,28},{24,0},{28,4},{1,9},{5... | collective-permute-start | bytes 1105928 | tf_op jit(solution)/shard_map/ppermute | solution.py:391
  53.5 25.8 %collective-permute-start.12 = (bf16[96,1920]{1,0:T(8,128)(2,1)}, bf16[96,1920]{1,0:T(8,128)(2,1)}, u32[]{:S(2)}, u32[]{:S(2)}) collective-permute-start(bf16[96,1920]{1,0:T(8,128)(2,1)} %pad_maximum_fusion.12.refs_0_), channel_id=1, source_target_pairs={{0,16},{4,20},{8,24},{12,28},{16,0},{20,4},{24,8},{28,12},{1,17},{... | collective-permute-start | bytes 1105928 | tf_op jit(solution)/shard_map/ppermute | solution.py:391
  71.8 9.3 %collective-permute-start.6 = (bf16[96,1280]{1,0:T(8,128)(2,1)}, bf16[96,1280]{1,0:T(8,128)(2,1)}, u32[]{:S(2)}, u32[]{:S(2)}) collective-permute-start(bf16[96,1280]{1,0:T(8,128)(2,1)} %collective-permute-done.2.refs_1_), channel_id=1, source_target_pairs={{0,4},{4,0},{8,12},{12,8},{16,20},{20,16},{24,28},{28,24},{1,5},{5... | collective-permute-start | bytes 737288 | tf_op jit(solution)/shard_map/ppermute | solution.py:388
  73.5 10.4 %collective-permute-start.7 = (bf16[96,1280]{1,0:T(8,128)(2,1)}, bf16[96,1280]{1,0:T(8,128)(2,1)}, u32[]{:S(2)}, u32[]{:S(2)}) collective-permute-start(bf16[96,1280]{1,0:T(8,128)(2,1)} %collective-permute-done.3.refs_2_), channel_id=1, source_target_pairs={{0,4},{4,0},{8,12},{12,8},{16,20},{20,16},{24,28},{28,24},{1,5},{5... | collective-permute-start | bytes 737288 | tf_op jit(solution)/shard_map/ppermute | solution.py:388
  74.2 14.9 %collective-permute-start.8 = (bf16[96,1280]{1,0:T(8,128)(2,1)}, bf16[96,1280]{1,0:T(8,128)(2,1)}, u32[]{:S(2)}, u32[]{:S(2)}) collective-permute-start(bf16[96,1280]{1,0:T(8,128)(2,1)} %collective-permute-done.4.refs_3_), channel_id=1, source_target_pairs={{0,4},{4,0},{8,12},{12,8},{16,20},{20,16},{24,28},{28,24},{1,5},{5... | collective-permute-start | bytes 737288 | tf_op jit(solution)/shard_map/ppermute | solution.py:388
  77.9 68.1 %collective-permute-start.1 = (bf16[2,256,768]{2,1,0:T(8,128)(2,1)}, bf16[2,256,768]{2,1,0:T(8,128)(2,1)}, u32[]{:S(2)}, u32[]{:S(2)}) collective-permute-start(bf16[2,256,768]{2,1,0:T(8,128)(2,1)} %pad_maximum_fusion.7), channel_id=1, source_target_pairs={{0,1},{1,0},{2,3},{3,2},{4,5},{5,4},{6,7},{7,6},{8,9},{9,8},{10,11... | collective-permute-start | bytes 2359304 | tf_op jit(solution)/shard_map/ppermute | solution.py:382
  79.3 17.8 %collective-permute-start.13 = (bf16[96,1920]{1,0:T(8,128)(2,1)}, bf16[96,1920]{1,0:T(8,128)(2,1)}, u32[]{:S(2)}, u32[]{:S(2)}) collective-permute-start(bf16[96,1920]{1,0:T(8,128)(2,1)} %pad_maximum_fusion.12.refs_0_), channel_id=1, source_target_pairs={{0,24},{4,28},{8,0},{12,4},{16,8},{20,12},{24,16},{28,20},{1,25},{... | collective-permute-start | bytes 1105928 | tf_op jit(solution)/shard_map/ppermute | solution.py:391
  81.1 16.1 %collective-permute-start.23 = (bf16[96,1536]{1,0:T(8,128)(2,1)}, bf16[96,1536]{1,0:T(8,128)(2,1)}, u32[]{:S(2)}, u32[]{:S(2)}) collective-permute-start(bf16[96,1536]{1,0:T(8,128)(2,1)} %collective-permute-done.19.refs_1_), channel_id=1, source_target_pairs={{0,4},{4,0},{8,12},{12,8},{16,20},{20,16},{24,28},{28,24},{1,5},{5... | collective-permute-start | bytes 884744 | tf_op jit(solution)/shard_map/ppermute | solution.py:388
  83.9 17.9 %collective-permute-start.24 = (bf16[96,1536]{1,0:T(8,128)(2,1)}, bf16[96,1536]{1,0:T(8,128)(2,1)}, u32[]{:S(2)}, u32[]{:S(2)}) collective-permute-start(bf16[96,1536]{1,0:T(8,128)(2,1)} %collective-permute-done.20.refs_2_), channel_id=1, source_target_pairs={{0,4},{4,0},{8,12},{12,8},{16,20},{20,16},{24,28},{28,24},{1,5},{5... | collective-permute-start | bytes 884744 | tf_op jit(solution)/shard_map/ppermute | solution.py:388
  89.1 19.0 %collective-permute-start.25 = (bf16[96,1536]{1,0:T(8,128)(2,1)}, bf16[96,1536]{1,0:T(8,128)(2,1)}, u32[]{:S(2)}, u32[]{:S(2)}) collective-permute-start(bf16[96,1536]{1,0:T(8,128)(2,1)} %collective-permute-done.21.refs_3_), channel_id=1, source_target_pairs={{0,4},{4,0},{8,12},{12,8},{16,20},{20,16},{24,28},{28,24},{1,5},{5... | collective-permute-start | bytes 884744 | tf_op jit(solution)/shard_map/ppermute | solution.py:388
  97.2 19.3 %collective-permute-start.14 = (bf16[96,1920]{1,0:T(8,128)(2,1)}, bf16[96,1920]{1,0:T(8,128)(2,1)}, u32[]{:S(2)}, u32[]{:S(2)}) collective-permute-start(bf16[96,1920]{1,0:T(8,128)(2,1)} %pad_maximum_fusion.12.refs_0_), channel_id=1, source_target_pairs={{0,4},{4,0},{8,12},{12,8},{16,20},{20,16},{24,28},{28,24},{1,5},{5... | collective-permute-start | bytes 1105928 | tf_op jit(solution)/shard_map/ppermute | solution.py:388
  97.3 26.6 %collective-permute-start.15 = (bf16[96,1920]{1,0:T(8,128)(2,1)}, bf16[96,1920]{1,0:T(8,128)(2,1)}, u32[]{:S(2)}, u32[]{:S(2)}) collective-permute-start(bf16[96,1920]{1,0:T(8,128)(2,1)} %collective-permute-done.11.refs_1_), channel_id=1, source_target_pairs={{0,4},{4,0},{8,12},{12,8},{16,20},{20,16},{24,28},{28,24},{1,5},{5... | collective-permute-start | bytes 1105928 | tf_op jit(solution)/shard_map/ppermute | solution.py:388
  101.8 30.0 %collective-permute-start.16 = (bf16[96,1920]{1,0:T(8,128)(2,1)}, bf16[96,1920]{1,0:T(8,128)(2,1)}, u32[]{:S(2)}, u32[]{:S(2)}) collective-permute-start(bf16[96,1920]{1,0:T(8,128)(2,1)} %collective-permute-done.12.refs_2_), channel_id=1, source_target_pairs={{0,4},{4,0},{8,12},{12,8},{16,20},{20,16},{24,28},{28,24},{1,5},{5... | collective-permute-start | bytes 1105928 | tf_op jit(solution)/shard_map/ppermute | solution.py:388
  108.1 31.6 %collective-permute-start.17 = (bf16[96,1920]{1,0:T(8,128)(2,1)}, bf16[96,1920]{1,0:T(8,128)(2,1)}, u32[]{:S(2)}, u32[]{:S(2)}) collective-permute-start(bf16[96,1920]{1,0:T(8,128)(2,1)} %collective-permute-done.13.refs_3_), channel_id=1, source_target_pairs={{0,4},{4,0},{8,12},{12,8},{16,20},{20,16},{24,28},{28,24},{1,5},{5... | collective-permute-start | bytes 1105928 | tf_op jit(solution)/shard_map/ppermute | solution.py:388
  116.5 29.5 %copy-start.25 = (bf16[1,256,768]{2,1,0:T(8,128)(2,1)S(1)}, bf16[1,256,768]{2,1,0:T(8,128)(2,1)}, u32[]{:S(2)}) copy-start(bf16[1,256,768]{2,1,0:T(8,128)(2,1)} %copy-done.24) | copy-start | bytes 1179652
  116.5 70.9 %collective-permute-start.27 = (bf16[768,1536]{1,0:T(8,128)(2,1)}, bf16[768,1536]{1,0:T(8,128)(2,1)}, u32[]{:S(2)}, u32[]{:S(2)}) collective-permute-start(bf16[768,1536]{1,0:T(8,128)(2,1)} %assemble.5.refs_0_.refs_2_), channel_id=1, source_target_pairs={{0,2},{2,0},{1,3},{3,1},{4,6},{6,4},{5,7},{7,5},{8,10},{10,8},{9,1... | collective-permute-start | bytes 7077896 | tf_op jit(solution)/shard_map/ppermute | solution.py:385
  143.8 44.1 %collective-permute-start.18 = (bf16[768,1920]{1,0:T(8,128)(2,1)}, bf16[768,1920]{1,0:T(8,128)(2,1)}, u32[]{:S(2)}, u32[]{:S(2)}) collective-permute-start(bf16[768,1920]{1,0:T(8,128)(2,1)} %assemble.4), channel_id=1, source_target_pairs={{0,1},{1,0},{2,3},{3,2},{4,5},{5,4},{6,7},{7,6},{8,9},{9,8},{10,11... | collective-permute-start | bytes 8847368 | tf_op jit(solution)/shard_map/ppermute | solution.py:382
  168.4 10.8 %collective-permute-start.9 = (bf16[2,256,384]{2,1,0:T(8,128)(2,1)S(1)}, bf16[2,256,384]{2,1,0:T(8,128)(2,1)}, u32[]{:S(2)}, u32[]{:S(2)}) collective-permute-start(bf16[2,256,384]{2,1,0:T(8,128)(2,1)S(1)} %dynamic-slice_bitcast_fusion.4), channel_id=1, source_target_pairs={{0,2},{2,0},{1,3},{3,1},{4,6},{6,4},{5,7},{7,5},{8,10},{10,8},{9,1... | collective-permute-start | bytes 1179656 | tf_op jit(solution)/shard_map/ppermute | solution.py:385
  181.3 3.0 collective-permute-start.10
  184.2 69.6 %collective-permute-start.26 = (bf16[768,1536]{1,0:T(8,128)(2,1)}, bf16[768,1536]{1,0:T(8,128)(2,1)}, u32[]{:S(2)}, u32[]{:S(2)}) collective-permute-start(bf16[768,1536]{1,0:T(8,128)(2,1)} %assemble.5.refs_0_.refs_2_), channel_id=1, source_target_pairs={{0,1},{1,0},{2,3},{3,2},{4,5},{5,4},{6,7},{7,6},{8,9},{9,8},{10,11... | collective-permute-start | bytes 7077896 | tf_op jit(solution)/shard_map/ppermute | solution.py:382
  187.4 66.4 %collective-permute-start.28 = (bf16[768,1536]{1,0:T(8,128)(2,1)}, bf16[768,1536]{1,0:T(8,128)(2,1)}, u32[]{:S(2)}, u32[]{:S(2)}) collective-permute-start(bf16[768,1536]{1,0:T(8,128)(2,1)} %collective-permute-done.27.refs_1_.refs_3_), channel_id=1, source_target_pairs={{0,1},{1,0},{2,3},{3,2},{4,5},{5,4},{6,7},{7,6},{8,9},{9,8},{10,11... | collective-permute-start | bytes 7077896 | tf_op jit(solution)/shard_map/ppermute | solution.py:382
  301.9 96.9 %collective-permute-start.49 = (bf16[768,1536]{1,0:T(8,128)(2,1)}, bf16[768,1536]{1,0:T(8,128)(2,1)}, u32[]{:S(2)}, u32[]{:S(2)}) collective-permute-start(bf16[768,1536]{1,0:T(8,128)(2,1)} %get-tuple-element.45), channel_id=1, source_target_pairs={{0,1},{1,0},{2,3},{3,2},{4,5},{5,4},{6,7},{7,6},{8,9},{9,8},{10,11... | collective-permute-start | bytes 7077896 | tf_op jit(solution)/shard_map/ppermute | solution.py:382
  302.0 173.4 %collective-permute-start.48 = (bf16[768,1536]{1,0:T(8,128)(2,1)}, bf16[768,1536]{1,0:T(8,128)(2,1)}, u32[]{:S(2)}, u32[]{:S(2)}) collective-permute-start(bf16[768,1536]{1,0:T(8,128)(2,1)} %get-tuple-element.43), channel_id=1, source_target_pairs={{0,1},{1,0},{2,3},{3,2},{4,5},{5,4},{6,7},{7,6},{8,9},{9,8},{10,11... | collective-permute-start | bytes 7077896 | tf_op jit(solution)/shard_map/ppermute | solution.py:382
  313.9 4.8 collective-permute-start.29
  318.7 67.6 %collective-permute-start.41 = (bf16[768,1536]{0,1:T(8,128)(2,1)}, bf16[768,1536]{0,1:T(8,128)(2,1)}, u32[]{:S(2)}, u32[]{:S(2)}) collective-permute-start(bf16[768,1536]{0,1:T(8,128)(2,1)} %pad_maximum_fusion.1), channel_id=1, source_target_pairs={{0,1},{1,0},{2,3},{3,2},{4,5},{5,4},{6,7},{7,6},{8,9},{9,8},{10,11... | collective-permute-start | bytes 7077896 | tf_op jit(solution)/shard_map/ppermute | solution.py:382
  318.9 10.2 %collective-permute-start.30 = (bf16[2,256,384]{2,1,0:T(8,128)(2,1)S(1)}, bf16[2,256,384]{2,1,0:T(8,128)(2,1)S(1)}, u32[]{:S(2)}, u32[]{:S(2)}) collective-permute-start(bf16[2,256,384]{2,1,0:T(8,128)(2,1)S(1)} %fusion.38), channel_id=1, source_target_pairs={{0,2},{2,0},{1,3},{3,1},{4,6},{6,4},{5,7},{7,5},{8,10},{10,8},{9,1... | collective-permute-start | bytes 1179656 | tf_op jit(solution)/shard_map/ppermute | solution.py:385
  322.2 37.9 %collective-permute-start.33 = (bf16[768,384]{1,0:T(8,128)(2,1)}, bf16[768,384]{1,0:T(8,128)(2,1)S(1)}, u32[]{:S(2)}, u32[]{:S(2)}) collective-permute-start(bf16[768,384]{1,0:T(8,128)(2,1)} %constant_dynamic-slice_fusion.4), channel_id=1, source_target_pairs={{0,1},{1,0},{2,3},{3,2},{4,5},{5,4},{6,7},{7,6},{8,9},{9,8},{10,11... | collective-permute-start | bytes 1769480 | tf_op jit(solution)/shard_map/ppermute | solution.py:382
  351.5 9.8 %collective-permute-start.31 = (bf16[2,256,768]{2,1,0:T(8,128)(2,1)S(1)}, bf16[2,256,768]{2,1,0:T(8,128)(2,1)S(1)}, u32[]{:S(2)}, u32[]{:S(2)}) collective-permute-start(bf16[2,256,768]{2,1,0:T(8,128)(2,1)S(1)} %dynamic-slice_bitcast_fusion.2), channel_id=1, source_target_pairs={{0,1},{1,0},{2,3},{3,2},{4,5},{5,4},{6,7},{7,6},{8,9},{9,8},{10,11... | collective-permute-start | bytes 2359304 | tf_op jit(solution)/shard_map/ppermute | solution.py:382
  361.5 10.4 %collective-permute-start.32 = (bf16[256,768]{1,0:T(8,128)(2,1)S(1)}, bf16[256,768]{1,0:T(8,128)(2,1)S(1)}, u32[]{:S(2)}, u32[]{:S(2)}) collective-permute-start(bf16[256,768]{1,0:T(8,128)(2,1)S(1)} %dynamic-slice_bitcast_fusion.3), channel_id=1, source_target_pairs={{0,2},{2,0},{1,3},{3,1},{4,6},{6,4},{5,7},{7,5},{8,10},{10,8},{9,1... | collective-permute-start | bytes 1179656 | tf_op jit(solution)/shard_map/ppermute | solution.py:385
  375.0 4.3 collective-permute-start.34
  384.9 29.9 %collective-permute-start.35 = (bf16[4,96,1664]{2,1,0:T(8,128)(2,1)}, bf16[4,96,1664]{2,1,0:T(8,128)(2,1)}, u32[]{:S(2)}, u32[]{:S(2)}) collective-permute-start(bf16[4,96,1664]{2,1,0:T(8,128)(2,1)} %fusion.25), channel_id=1, source_target_pairs={{0,4},{4,0},{8,12},{12,8},{16,20},{20,16},{24,28},{28,24},{1,5},{5... | collective-permute-start | bytes 3833864 | tf_op jit(solution)/shard_map/ppermute | solution.py:388
  398.8 41.2 %collective-permute-start.42 = (bf16[4,96,1536]{2,1,0:T(8,128)(2,1)S(1)}, bf16[4,96,1536]{2,1,0:T(8,128)(2,1)S(1)}, u32[]{:S(2)}, u32[]{:S(2)}) collective-permute-start(bf16[4,96,1536]{2,1,0:T(8,128)(2,1)S(1)} %fusion.26), channel_id=1, source_target_pairs={{0,4},{4,0},{8,12},{12,8},{16,20},{20,16},{24,28},{28,24},{1,5},{5... | collective-permute-start | bytes 3538952 | tf_op jit(solution)/shard_map/ppermute | solution.py:388
  398.9 41.2 %slice-start = ((s8[4718592]{0:T(1024)(128)(4,1)}), s8[4194304]{0:T(1024)(128)(4,1)S(1)}, s32[]{:S(2)}) async-start(s8[4718592]{0:T(1024)(128)(4,1)} %bitcast.334), calls=%async_computation | async-start | bytes 8388608
  399.2 40.8 %slice-start.1 = ((s8[4718592]{0:T(1024)(128)(4,1)}), s8[524288]{0:T(1024)(128)(4,1)S(1)}, s32[]{:S(2)}) async-start(s8[4718592]{0:T(1024)(128)(4,1)} %bitcast.334), calls=%async_computation.1 | async-start | bytes 1048576
  401.6 73.8 %collective-permute-start.50 = (bf16[768,1536]{1,0:T(8,128)(2,1)S(1)}, bf16[768,1536]{1,0:T(8,128)(2,1)S(1)}, u32[]{:S(2)}, u32[]{:S(2)}) collective-permute-start(bf16[768,1536]{1,0:T(8,128)(2,1)S(1)} %add_convert_fusion), channel_id=1, source_target_pairs={{0,2},{2,0},{1,3},{3,1},{4,6},{6,4},{5,7},{7,5},{8,10},{10,8},{9,1... | collective-permute-start | bytes 7077896 | tf_op jit(solution)/shard_map/ppermute | solution.py:385
  417.3 23.2 %collective-permute-start.36 = (bf16[96,1664]{1,0:T(8,128)(2,1)S(1)}, bf16[96,1664]{1,0:T(8,128)(2,1)S(1)}, u32[]{:S(2)}, u32[]{:S(2)}) collective-permute-start(bf16[96,1664]{1,0:T(8,128)(2,1)S(1)} %get-tuple-element.88), channel_id=1, source_target_pairs={{0,8},{4,12},{8,16},{12,20},{16,24},{20,28},{24,0},{28,4},{1,9},{5... | collective-permute-start | bytes 958472 | tf_op jit(solution)/shard_map/ppermute | solution.py:391
  417.4 26.4 %collective-permute-start.37 = (bf16[96,1664]{1,0:T(8,128)(2,1)S(1)}, bf16[96,1664]{1,0:T(8,128)(2,1)S(1)}, u32[]{:S(2)}, u32[]{:S(2)}) collective-permute-start(bf16[96,1664]{1,0:T(8,128)(2,1)S(1)} %get-tuple-element.90), channel_id=1, source_target_pairs={{0,16},{4,20},{8,24},{12,28},{16,0},{20,4},{24,8},{28,12},{1,17},{... | collective-permute-start | bytes 958472 | tf_op jit(solution)/shard_map/ppermute | solution.py:391
  440.0 9.3 %collective-permute-start.38 = (bf16[96,1664]{1,0:T(8,128)(2,1)S(1)}, bf16[96,1664]{1,0:T(8,128)(2,1)S(1)}, u32[]{:S(2)}, u32[]{:S(2)}) collective-permute-start(bf16[96,1664]{1,0:T(8,128)(2,1)S(1)} %get-tuple-element.89), channel_id=1, source_target_pairs={{0,24},{4,28},{8,0},{12,4},{16,8},{20,12},{24,16},{28,20},{1,25},{... | collective-permute-start | bytes 958472 | tf_op jit(solution)/shard_map/ppermute | solution.py:391
  440.5 22.2 %collective-permute-start.43 = (bf16[96,1536]{1,0:T(8,128)(2,1)S(1)}, bf16[96,1536]{1,0:T(8,128)(2,1)S(1)}, u32[]{:S(2)}, u32[]{:S(2)}) collective-permute-start(bf16[96,1536]{1,0:T(8,128)(2,1)S(1)} %get-tuple-element.106), channel_id=1, source_target_pairs={{0,8},{4,12},{8,16},{12,20},{16,24},{20,28},{24,0},{28,4},{1,9},{5... | collective-permute-start | bytes 884744 | tf_op jit(solution)/shard_map/ppermute | solution.py:391
  443.8 25.3 %collective-permute-start.44 = (bf16[96,1536]{1,0:T(8,128)(2,1)S(1)}, bf16[96,1536]{1,0:T(8,128)(2,1)S(1)}, u32[]{:S(2)}, u32[]{:S(2)}) collective-permute-start(bf16[96,1536]{1,0:T(8,128)(2,1)S(1)} %get-tuple-element.108), channel_id=1, source_target_pairs={{0,16},{4,20},{8,24},{12,28},{16,0},{20,4},{24,8},{28,12},{1,17},{... | collective-permute-start | bytes 884744 | tf_op jit(solution)/shard_map/ppermute | solution.py:391
  449.4 24.2 %collective-permute-start.45 = (bf16[96,1536]{1,0:T(8,128)(2,1)S(1)}, bf16[96,1536]{1,0:T(8,128)(2,1)S(1)}, u32[]{:S(2)}, u32[]{:S(2)}) collective-permute-start(bf16[96,1536]{1,0:T(8,128)(2,1)S(1)} %get-tuple-element.107), channel_id=1, source_target_pairs={{0,24},{4,28},{8,0},{12,4},{16,8},{20,12},{24,16},{28,20},{1,25},{... | collective-permute-start | bytes 884744 | tf_op jit(solution)/shard_map/ppermute | solution.py:391
  449.5 25.9 %copy-start.41 = (bf16[768,1536]{1,0:T(8,128)(2,1)S(1)}, bf16[768,1536]{1,0:T(8,128)(2,1)}, u32[]{:S(2)}) copy-start(bf16[768,1536]{1,0:T(8,128)(2,1)} %get-tuple-element.42) | copy-start | bytes 7077892
  462.8 12.5 %collective-permute-start.39 = (bf16[96,1664]{1,0:T(8,128)(2,1)S(1)}, bf16[96,1664]{1,0:T(8,128)(2,1)S(1)}, u32[]{:S(2)}, u32[]{:S(2)}) collective-permute-start(bf16[96,1664]{1,0:T(8,128)(2,1)S(1)} %fusion.56), channel_id=1, source_target_pairs={{0,2},{2,0},{1,3},{3,1},{4,6},{6,4},{5,7},{7,5},{8,10},{10,8},{9,1... | collective-permute-start | bytes 958472 | tf_op jit(solution)/shard_map/ppermute | solution.py:385
  473.7 12.1 %collective-permute-start.46 = (bf16[96,1536]{1,0:T(8,128)(2,1)S(1)}, bf16[96,1536]{1,0:T(8,128)(2,1)S(1)}, u32[]{:S(2)}, u32[]{:S(2)}) collective-permute-start(bf16[96,1536]{1,0:T(8,128)(2,1)S(1)} %fusion.57), channel_id=1, source_target_pairs={{0,2},{2,0},{1,3},{3,1},{4,6},{6,4},{5,7},{7,5},{8,10},{10,8},{9,1... | collective-permute-start | bytes 884744 | tf_op jit(solution)/shard_map/ppermute | solution.py:385
  481.3 25.8 %collective-permute-start.51 = (bf16[4,96,1536]{2,1,0:T(8,128)(2,1)}, bf16[4,96,1536]{2,1,0:T(8,128)(2,1)}, u32[]{:S(2)}, u32[]{:S(2)}) collective-permute-start(bf16[4,96,1536]{2,1,0:T(8,128)(2,1)} %fusion.27), channel_id=1, source_target_pairs={{0,4},{4,0},{8,12},{12,8},{16,20},{20,16},{24,28},{28,24},{1,5},{5... | collective-permute-start | bytes 3538952 | tf_op jit(solution)/shard_map/ppermute | solution.py:388
  482.6 4.2 collective-permute-start.40
  486.8 51.2 %collective-permute-start.47 = (bf16[96,1536]{1,0:T(8,128)(2,1)S(1)}, bf16[96,1536]{1,0:T(8,128)(2,1)}, u32[]{:S(2)}, u32[]{:S(2)}) collective-permute-start(bf16[96,1536]{1,0:T(8,128)(2,1)S(1)} %get-tuple-element.70), channel_id=1, source_target_pairs={{0,1},{1,0},{2,3},{3,2},{4,5},{5,4},{6,7},{7,6},{8,9},{9,8},{10,11... | collective-permute-start | bytes 884744 | tf_op jit(solution)/shard_map/ppermute | solution.py:382
  509.6 5.6 %collective-permute-start.52 = (bf16[96,1536]{1,0:T(8,128)(2,1)S(1)}, bf16[96,1536]{1,0:T(8,128)(2,1)S(1)}, u32[]{:S(2)}, u32[]{:S(2)}) collective-permute-start(bf16[96,1536]{1,0:T(8,128)(2,1)S(1)} %get-tuple-element.97), channel_id=1, source_target_pairs={{0,8},{4,12},{8,16},{12,20},{16,24},{20,28},{24,0},{28,4},{1,9},{5... | collective-permute-start | bytes 884744 | tf_op jit(solution)/shard_map/ppermute | solution.py:391
  509.7 22.7 %collective-permute-start.53 = (bf16[96,1536]{1,0:T(8,128)(2,1)S(1)}, bf16[96,1536]{1,0:T(8,128)(2,1)S(1)}, u32[]{:S(2)}, u32[]{:S(2)}) collective-permute-start(bf16[96,1536]{1,0:T(8,128)(2,1)S(1)} %get-tuple-element.99), channel_id=1, source_target_pairs={{0,16},{4,20},{8,24},{12,28},{16,0},{20,4},{24,8},{28,12},{1,17},{... | collective-permute-start | bytes 884744 | tf_op jit(solution)/shard_map/ppermute | solution.py:391
  509.8 24.9 %collective-permute-start.54 = (bf16[96,1536]{1,0:T(8,128)(2,1)S(1)}, bf16[96,1536]{1,0:T(8,128)(2,1)S(1)}, u32[]{:S(2)}, u32[]{:S(2)}) collective-permute-start(bf16[96,1536]{1,0:T(8,128)(2,1)S(1)} %get-tuple-element.98), channel_id=1, source_target_pairs={{0,24},{4,28},{8,0},{12,4},{16,8},{20,12},{24,16},{28,20},{1,25},{... | collective-permute-start | bytes 884744 | tf_op jit(solution)/shard_map/ppermute | solution.py:391
  534.8 7.5 %collective-permute-start.55 = (bf16[96,1536]{1,0:T(8,128)(2,1)S(1)}, bf16[96,1536]{1,0:T(8,128)(2,1)}, u32[]{:S(2)}, u32[]{:S(2)}) collective-permute-start(bf16[96,1536]{1,0:T(8,128)(2,1)S(1)} %fusion.32), channel_id=1, source_target_pairs={{0,2},{2,0},{1,3},{3,1},{4,6},{6,4},{5,7},{7,5},{8,10},{10,8},{9,1... | collective-permute-start | bytes 884744 | tf_op jit(solution)/shard_map/ppermute | solution.py:385
  543.4 4.6 collective-permute-start.56
  (63 other events, 241.2 us)

commit v2 on v1

--- a/solution.py
+++ b/solution.py
@@ -335,27 +335,33 @@
     return out[0], out[1], out[2:]
 
 
-def assemble_kernel(idx_ref, *refs, n, rows):
-    pieces, out_ref, sem = refs[:n], refs[n], refs[n + 1]
+def assemble_kernel(idx_ref, *refs, counts, rows):
+    pieces, out_ref, sem = refs[: len(counts)], refs[len(counts)], refs[len(counts) + 1]
     copies = []
-    for i in range(n):
-        at = pl.multiple_of(idx_ref[i] * rows, rows)
-        copies.append(pltpu.make_async_copy(pieces[i], out_ref.at[pl.ds(at, rows), :], sem.at[i]))
+    for piece, count in zip(pieces, counts):
+        for j in range(count):
+            i = len(copies)
+            at = pl.multiple_of(idx_ref[i] * rows, rows)
+            copies.append(
+                pltpu.make_async_copy(
+                    piece.at[pl.ds(j * rows, rows), :], out_ref.at[pl.ds(at, rows), :], sem.at[i]
+                )
+            )
     for copy in copies:
         copy.start()
     for copy in copies:
         copy.wait()
 
 
-def assemble(pieces, places):
-    rows, cols = pieces[0].shape
-    n = len(pieces)
-    return pl.pallas_call(
-        functools.partial(assemble_kernel, n=n, rows=rows),
+def assemble(pieces, places, rows):
+    counts = [p.shape[0] // rows for p in pieces]
+    cols, n = pieces[0].shape[1], sum(counts)
+    return pl.pallas_call(
+        functools.partial(assemble_kernel, counts=counts, rows=rows),
         grid_spec=pltpu.PrefetchScalarGridSpec(
             num_scalar_prefetch=1,
             grid=(1,),
-            in_specs=[pl.BlockSpec(memory_space=pl.ANY)] * n,
+            in_specs=[pl.BlockSpec(memory_space=pl.ANY)] * len(pieces),
             out_specs=pl.BlockSpec((n * rows, cols), lambda i, idx: (0, 0)),
             scratch_shapes=[pltpu.SemaphoreType.DMA((n,))],
         ),
@@ -366,6 +372,137 @@
         ),
         name="assemble",
     )(jnp.stack(places).astype(jnp.int32), *pieces)
+
+
+def merge_kernel(c_ref, own_ref, far_ref, *refs, sizes):
+    outs, sem = refs[:-1], refs[-1]
+    copies, start = [], 0
+    for out_ref, size in zip(outs, sizes):
+        for source, side in ((own_ref, c_ref[0]), (far_ref, 1 - c_ref[0])):
+            at = pl.multiple_of(side * size, size)
+            copies.append(
+                pltpu.make_async_copy(
+                    source.at[:, pl.ds(start, size)], out_ref.at[:, pl.ds(at, size)], sem.at[len(copies)]
+                )
+            )
+        start += size
+    for copy in copies:
+        copy.start()
+    for copy in copies:
+        copy.wait()
+
+
+def merge(own, far, c, sizes):
+    rows = own.shape[0]
+    return pl.pallas_call(
+        functools.partial(merge_kernel, sizes=sizes),
+        grid_spec=pltpu.PrefetchScalarGridSpec(
+            num_scalar_prefetch=1,
+            grid=(1,),
+            in_specs=[pl.BlockSpec(memory_space=pl.ANY)] * 2,
+            out_specs=[pl.BlockSpec((rows, 2 * n), lambda i, idx: (0, 0)) for n in sizes],
+            scratch_shapes=[pltpu.SemaphoreType.DMA((2 * len(sizes),))],
+        ),
+        out_shape=[jax.ShapeDtypeStruct((rows, 2 * n), own.dtype) for n in sizes],
+        compiler_params=params(),
+        cost_estimate=pl.CostEstimate(
+            flops=0, bytes_accessed=8 * rows * sum(sizes), transcendentals=0
+        ),
+        name="merge",
+    )(c.reshape(1).astype(jnp.int32), own, far)
+
+
+def join_kernel(c_ref, own_ref, far_ref, *outs, layout, size):
+    start = 0
+    for out_ref, segments, width in layout_refs(outs, layout):
+        for j in range(segments):
+            for source, side in ((own_ref, c_ref[0]), (far_ref, 1 - c_ref[0])):
+                at = pl.multiple_of(side * width, size)
+                out_ref[:, pl.ds(at + 2 * j * width, width)] = source[:, start : start + width].astype(F32)
+            start += width
+
+
+def layout_refs(outs, layout):
+    return [(o, n, w) for o, (n, w) in zip(outs, layout)]
+
+
+def join(own, far, c, layout):
+    rows = own.shape[0]
+    shapes = [jax.ShapeDtypeStruct((rows, 2 * n * w), F32) for n, w in layout]
+    return pl.pallas_call(
+        functools.partial(join_kernel, layout=layout, size=128),
+        grid_spec=pltpu.PrefetchScalarGridSpec(
+            num_scalar_prefetch=1,
+            grid=(1,),
+            in_specs=[pl.BlockSpec(v.shape, lambda i, idx: (0, 0)) for v in (own, far)],
+            out_specs=[pl.BlockSpec(v.shape, lambda i, idx: (0, 0)) for v in shapes],
+        ),
+        out_shape=shapes,
+        compiler_params=params(),
+        name="join",
+    )(c.reshape(1).astype(jnp.int32), own, far)
+
+
+def spread_kernel(p_ref, up_ref, down_ref, *, unit):
+    quarters, rows, cols = p_ref.shape
+    width = cols // 2
+    for s in range(quarters):
+        for f in range(width // unit):
+            up_ref[:, (f * quarters + s) * unit : (f * quarters + s + 1) * unit] = p_ref[
+                s, :, f * unit : (f + 1) * unit
+            ].astype(F32)
+        down_ref[s * rows : (s + 1) * rows, :] = p_ref[s, :, width:].astype(F32)
+
+
+def spread(pieces, unit):
+    quarters, rows, cols = pieces.shape
+    return pl.pallas_call(
+        functools.partial(spread_kernel, unit=unit),
+        out_shape=[
+            jax.ShapeDtypeStruct((rows, quarters * cols // 2), F32),
+            jax.ShapeDtypeStruct((quarters * rows, cols // 2), F32),
+        ],
+        compiler_params=params(),
+        name="spread",
+    )(pieces)
+
+
+def grad_kernel(side_ref, a_ref, b_ref, *refs):
+    out_ref = refs[-1]
+    total = dot_tn(a_ref[...], b_ref[...])
+    if len(refs) == 2:
+        total = total + refs[0][...].astype(F32)
+    out_ref[...] = total.astype(BF)
+
+
+def grad_half(a, b, side, more=None):
+    tokens, rows = a.shape
+    cols = b.shape[1] // 2
+    block = 384
+    blocks = cols // block
+    operands = [a, b] + ([] if more is None else [more])
+    out_spec = pl.BlockSpec((rows, block), lambda j, side: (0, j))
+    return pl.pallas_call(
+        grad_kernel,
+        grid_spec=pltpu.PrefetchScalarGridSpec(
+            num_scalar_prefetch=1,
+            grid=(blocks,),
+            in_specs=[
+                pl.BlockSpec((tokens, rows), lambda j, side: (0, 0)),
+                pl.BlockSpec((tokens, block), lambda j, side: (0, side[0] * blocks + j)),
+            ]
+            + [out_spec] * (len(operands) - 2),
+            out_specs=out_spec,
+        ),
+        out_shape=jax.ShapeDtypeStruct((rows, cols), BF),
+        compiler_params=params(),
+        cost_estimate=pl.CostEstimate(
+            flops=2 * tokens * rows * cols,
+            bytes_accessed=2 * tokens * (rows + cols) + 4 * rows * cols,
+            transcendentals=0,
+        ),
+        name="grad_half",
+    )(side.reshape(1).astype(jnp.int32), *operands)
 
 
 class Place:
@@ -390,30 +527,38 @@
     def shift_z(self, value, hops):
         return lax.ppermute(value, "fsdp", [(i, (i + 2 * hops) % self.n) for i in range(self.n)])
 
-    def gather(self, piece):
+    def places(self):
+        base = [2 * ((self.z - k) % 4) for k in range(4)]
+        return [b + self.y for b in base] + [b + 1 - self.y for b in base]
+
+    def shifts(self, piece):
+        return [self.shift_z(piece, k) for k in (1, 2, 3)]
+
+    def send_y(self, mats):
+        mats = [m.reshape(self.n // 2, 2, -1, m.shape[1]) for m in mats]
+        sent = jnp.concatenate([pick(m, 1 - self.y, 1).astype(BF) for m in mats], 2)
+        kept = jnp.concatenate([pick(m, self.y, 1).astype(BF) for m in mats], 2)
+        return sent, kept
+
+    def send_z(self, column):
+        own = pick(column, self.z, 0)
         if not self.direct:
-            return lax.all_gather(piece, "fsdp", axis=0, tiled=True)
-        columns = [piece] + [self.shift_z(piece, k) for k in (1, 2, 3)]
-        others = [self.swap_y(p) for p in columns]
-        base = [2 * ((self.z - k) % 4) for k in range(4)]
-        return assemble(
-            columns + others, [b + self.y for b in base] + [b + 1 - self.y for b in base]
-        )
-
-    def scatter(self, blocks):
-        rows, cols = blocks.shape[1:]
+            total = lax.psum(column, "fsdp")
+            return own, [pick(total, self.z, 0)]
+        return own, [self.shift_z(pick(column, (self.z + k) % 4, 0), k) for k in (1, 2, 3)]
+
+    def total(self, own, got):
         if not self.direct:
-            return lax.psum_scatter(
-                blocks.astype(BF), "fsdp", scatter_dimension=0, tiled=False
-            ).astype(F32)
-        blocks = blocks.reshape(4, 2, rows, cols)
-        sent = pick(blocks, 1 - self.y, 1)
-        kept = pick(blocks, self.y, 1)
-        column = (kept.astype(F32) + self.swap_y(sent.astype(BF)).astype(F32)).astype(BF)
-        total = pick(column, self.z, 0).astype(F32)
-        for k in (1, 2, 3):
-            total = total + self.shift_z(pick(column, (self.z + k) % 4, 0), k).astype(F32)
-        return total
+            return got[0].astype(F32)
+        return sum((g.astype(F32) for g in got), own.astype(F32))
+
+
+def tie(*values):
+    return lax.optimization_barrier(values)
+
+
+def added(first, second):
+    return (first.astype(F32) + second.astype(F32)).astype(BF)
 
 
 def pick(value, index, axis):
@@ -467,46 +612,60 @@
 
     vectors = jnp.stack([ln1_gain, ln1_bias, ln2_gain, ln2_bias, ln3_gain, ln3_bias], 1)
     vectors = jnp.pad(vectors, ((0, 0), (0, 128 - vectors.shape[1])))
-    qkv_half = pick(w_qkv.reshape(rows, 3, 2, half), c, 2).reshape(rows, 3 * half)
-    group_a = at.gather(jnp.concatenate([qkv_half, vectors], 1))
+    piece_a = jnp.concatenate(
+        [lax.dynamic_slice_in_dim(w_qkv, j * width + c * half, half, 1) for j in range(3)] + [vectors], 1
+    )
+
+    def half_of(weight):
+        return lax.dynamic_slice_in_dim(weight, c * (weight.shape[1] // 2), weight.shape[1] // 2, 1)
+
+    piece_b = jnp.concatenate([half_of(w) for w in (cross_kv, w_attn_out, cross_q, cross_out)], 1)
+    unit = w_down.shape[0] // 4
+    up_quarter = pick(w_up.reshape(rows, -1, 4, unit), at.s, 2).reshape(rows, -1)
+    down_quarter = pick(w_down.reshape(4, unit, width), at.s, 0)
+    piece_f = jnp.concatenate([up_quarter, down_quarter], 1)
+    if at.direct:
+        places = at.places()
+        first = at.swap_y(piece_a)
+        zs, first, piece_f = tie(at.shifts(piece_a), first, piece_f)
+        others = at.swap_y(jnp.concatenate(zs, 0))
+        zs_f, others, piece_b = tie(at.shifts(piece_f), others, piece_b)
+        group_a = assemble([piece_a, *zs, first, others], places, rows)
+        column_f = jnp.concatenate([piece_f, *zs_f], 0)
+        moving = (at.swap_x(column_f), at.swap_y(column_f), at.shifts(piece_b))
+    else:
+        group_a = lax.all_gather(piece_a, "fsdp", axis=0, tiled=True)
+        moving = ()
     wqkv = group_a[:, : 3 * half]
     gains = group_a[:, 3 * half : 3 * half + 6].T.astype(F32)
     g1, b1, g2, b2, g3, b3 = (gains[i] for i in range(6))
 
-    def half_of(weight):
-        return lax.dynamic_slice_in_dim(weight, c * (weight.shape[1] // 2), weight.shape[1] // 2, 1)
-
-    group_b = at.gather(
-        jnp.concatenate([half_of(w) for w in (cross_kv, w_attn_out, cross_q, cross_out)], 1)
-    )
-    group_b2 = at.swap_core(group_b)
-
-    def both(start, size):
-        a, b = group_b[:, start : start + size], group_b2[:, start : start + size]
-        return ordered(c, a, b, 1).reshape(width, 2 * size)
-
-    wckv = both(0, width)
-    wao = both(width, half)
-    wcq = both(width + half, half)
-    wco = both(2 * width, half)
-
-    unit = w_down.shape[0] // 4
-    up_quarter = pick(w_up.reshape(rows, -1, 4, unit), at.s, 2).reshape(rows, -1)
-    down_quarter = pick(w_down.reshape(4, unit, width), at.s, 0)
-    q00 = at.gather(jnp.concatenate([up_quarter, down_quarter], 1))
-    q10 = at.swap_x(q00)
-    q01 = at.swap_core(q00)
-    q11 = at.swap_core(q10)
-
     seqf = sequence.astype(F32)
     h1 = norm(seqf, g1, b1)
     qkv = dot(h1, wqkv).astype(BF)
+    qkv, moving = tie(qkv, moving)
+    if at.direct:
+        xcolumn, others_f, zs_b = moving
+        column_b = jnp.concatenate([piece_b, *zs_b], 0)
+        moving = (at.swap_x(others_f), at.swap_y(column_b))
     att_heads, lse = self_forward(qkv, segc, segr)
     by_x = att_heads.reshape(2, 2, piece, half)
     got = at.swap_x(pick(by_x, 1 - x, 0))
     chip = ordered(x, pick(by_x, x, 0), got, 0)
     got = at.swap_core(pick(chip, 1 - c, 1))
     att = ordered(c, pick(chip, c, 1), got, 2).reshape(tokens, width)
+    att, moving = tie(att, moving)
+    if at.direct:
+        group_b = assemble([column_b, moving[1]], places, rows)
+        q00 = assemble([column_f, others_f], places, rows)
+        q10 = assemble([xcolumn, moving[0]], places, rows)
+    else:
+        group_b = lax.all_gather(piece_b, "fsdp", axis=0, tiled=True)
+        q00 = lax.all_gather(piece_f, "fsdp", axis=0, tiled=True)
+        q10 = at.swap_x(q00)
+    wckv, wao, wcq, wco = merge(group_b, at.swap_core(group_b), c, (width, half, half, half))
+    q01 = at.swap_core(q00)
+    q11 = at.swap_core(q10)
 
     xin = inputs.reshape(tokens, width).astype(F32)
     x1 = xin + dot(att, wao)
@@ -518,44 +677,50 @@
     x2 = x1 + dot(cro, wco)
     h3 = norm(x2, g3, b3)
     dy = out_grad.reshape(tokens, width)
-    y, dh3, own_grads = feed_forward(h3, dy, [q00, q10])
-    y, dh3, far_grads = feed_forward(h3, dy, [q01, q11], (y, dh3))
-    outputs = (x2 + y).astype(BF).reshape(seqs, piece, width)
-
+    y, dh3, far_grads = feed_forward(h3, dy, [q01, q11])
     f0 = at.swap_core(far_grads[0])
     f1 = at.swap_core(far_grads[1])
-    away = (own_grads[1].astype(F32) + f1.astype(F32)).astype(BF)
-    ffn_sum = own_grads[0].astype(F32) + f0.astype(F32) + at.swap_x(away).astype(F32)
-    ffn_own = at.scatter(ffn_sum.reshape(at.n, rows, 2 * width)).astype(BF)
-    ffn_x = ordered(x, ffn_own, at.swap_x(ffn_own), 0)
-    ffn_all = ordered(c, ffn_x, at.swap_core(ffn_x), 1).reshape(4, rows, 2 * width).astype(F32)
-    grad_up = ffn_all[:, :, :width].reshape(4, rows, -1, unit).transpose(1, 2, 0, 3).reshape(rows, -1)
-    grad_down = ffn_all[:, :, width:].reshape(4 * unit, width)
+    y, dh3, own_grads = feed_forward(h3, dy, [q00, q10], (y, dh3))
+    outputs = (x2 + y).astype(BF).reshape(seqs, piece, width)
+
+    away, dh3 = tie(added(own_grads[1], f1), dh3)
+    ffn_got = at.swap_x(away)
 
     dv3, gg3, gb3 = norm_back(x2, g3, dh3)
     dx2 = dy.astype(F32) + dv3
     dc = dx2.astype(BF)
-    grad_co = dot_tn(cro, dc).astype(BF)
     dcro = dot_nt(dc, wco).astype(BF)
     dcq, dckv = cross_backward(cq, ckv, dcro)
-    grad_cq = dot_tn(h2, dcq).astype(BF)
     dh2 = dot_nt(dcq, wcq)
-    grad_ckv = dot_tn(nb, dckv).astype(BF)
-    neighbour_grad = dot_nt(dckv, wckv)
     dv2, gg2, gb2 = norm_back(x1, g2, dh2)
     dx1 = dx2 + dv2
     da = dx1.astype(BF)
-    grad_ao = dot_tn(att, da).astype(BF)
     datt = dot_nt(da, wao).astype(BF)
+    pairs = ((nb, dckv), (att, da), (h2, dcq), (cro, dc))
+    sent_b = [grad_half(a, b, 1 - c) for a, b in pairs]
+    sums_b = [grad_half(a, b, c, at.swap_core(v)) for (a, b), v in zip(pairs, sent_b)]
+    sent_b, kept_b = at.send_y(sums_b)
+    neighbour_grad = dot_nt(dckv, wckv)
 
     datt = datt.reshape(seqs, piece, 2, half)
     got = at.swap_core(pick(datt, 1 - c, 2))
     chip = ordered(c, pick(datt, c, 2), got, 1)
+    chip, ffn_got = tie(chip, ffn_got)
     got = at.swap_x(pick(chip, 1 - x, 0))
     do = ordered(x, pick(chip, x, 0), got, 0).reshape(4 * piece, half)
+    ffn_sum = own_grads[0].astype(F32) + f0.astype(F32) + ffn_got.astype(F32)
+    sent_f, kept_f = at.send_y([ffn_sum.astype(BF)])
+    do, sent_b, sent_f = tie(do, sent_b, sent_f)
+    got_f, got_b = at.swap_y(sent_f), at.swap_y(sent_b)
     dqkv = jnp.concatenate(self_backward(qkv, do, segc, segr, lse), 1)
+    dqkv, got_f = tie(dqkv, got_f)
+    moving_f = at.send_z(added(kept_f, got_f))
     grad_qkv = dot_tn(h1, dqkv).astype(BF)
+    sent_a, kept_a = at.send_y([grad_qkv])
     part = dot_nt(dqkv, wqkv).astype(BF).reshape(2, 2, piece, width)
+    part, sent_a, got_b = tie(part, sent_a, got_b)
+    got_a = at.swap_y(sent_a)
+    moving_b = at.send_z(added(kept_b, got_b))
     got = at.swap_core(pick(part, 1 - c, 1))
     chip = (pick(part, c, 1).astype(F32) + got.astype(F32)).astype(BF)
     got = at.swap_x(pick(chip, 1 - x, 0))
@@ -563,42 +728,27 @@
     dv1, gg1, gb1 = norm_back(xin, g1, dh1)
     input_grad = (dx1 + dv1).reshape(seqs, piece, width)
 
-    def reduce_halves(halves_sent, halves_kept):
-        got = at.swap_core(halves_sent)
-        blocks = halves_kept.astype(F32) + got.astype(F32)
-        return finish(blocks)
-
-    def finish(blocks):
-        own = at.scatter(blocks.reshape(at.n, rows, -1))
+    def finish(own):
         return own + at.swap_x(own.astype(BF)).astype(F32)
 
-    def halves(grad, which):
-        return lax.dynamic_slice_in_dim(grad, which * (grad.shape[1] // 2), grad.shape[1] // 2, 1)
-
-    def joined(own, other):
-        return ordered(c, own, other, 1).reshape(rows, -1)
-
-    three = (grad_ckv, grad_cq, grad_co)
-    own_b = reduce_halves(
-        jnp.concatenate([halves(g, 1 - c) for g in three], 1),
-        jnp.concatenate([halves(g, c) for g in three], 1),
+    input_grad, moving_f, got_a = tie(input_grad, moving_f, got_a)
+    vec = jnp.pad(jnp.stack([gg1, gb1, gg2, gb2, gg3, gb3], 1), ((0, 0), (0, 128 - 6)))
+    vec = vec + at.swap_core(vec)
+    vec = pick((vec + at.swap_y(vec)).reshape(at.n // 2, 2, rows, 128), at.y, 1).astype(BF)
+    moving_a = at.send_z(jnp.concatenate([added(kept_a, got_a), vec], 2))
+    ffn_own = at.total(*moving_f).astype(BF)
+    ffn_x = ordered(x, ffn_own, at.swap_x(ffn_own), 0)
+    ffn_all = ordered(c, ffn_x, at.swap_core(ffn_x), 1).reshape(4, rows, 2 * width)
+    grad_up, grad_down = spread(ffn_all, unit)
+    own_b = finish(at.total(*moving_b))
+    far_b = at.swap_core(own_b.astype(BF))
+    out_ckv, out_ao, out_cq, out_co = join(
+        own_b, far_b, c, ((1, width), (1, half), (1, half), (1, half))
     )
-    far_b = at.swap_core(own_b.astype(BF)).astype(F32)
-    out_ckv = joined(own_b[:, :width], far_b[:, :width])
-    out_cq = joined(own_b[:, width : width + half], far_b[:, width : width + half])
-    out_co = joined(own_b[:, width + half :], far_b[:, width + half :])
-
-    vec = jnp.stack([gg1, gb1, gg2, gb2, gg3, gb3], 1)
-    vec = vec + at.swap_core(vec)
-    vec = jnp.pad(vec, ((0, 0), (0, 128 - 6)))
-    kept_ao = halves(grad_ao, c).astype(F32) + at.swap_core(halves(grad_ao, 1 - c)).astype(F32)
-    own_a = finish(jnp.concatenate([grad_qkv.astype(F32), kept_ao, vec], 1))
-    far_a = at.swap_core(own_a[:, : 4 * half].astype(BF)).astype(F32)
-    out_qkv = ordered(
-        c, own_a[:, : 3 * half].reshape(rows, 3, half), far_a[:, : 3 * half].reshape(rows, 3, half), 2
-    ).reshape(rows, 6 * half)
-    out_ao = joined(own_a[:, 3 * half : 4 * half], far_a[:, 3 * half :])
-    vecs = own_a[:, 4 * half : 4 * half + 6].T
+    own_a = finish(at.total(*moving_a))
+    far_a = at.swap_core(own_a[:, : 3 * half].astype(BF))
+    (out_qkv,) = join(own_a, far_a, c, ((3, half),))
+    vecs = own_a[:, 3 * half : 3 * half + 6].T
 
     return (
         outputs, input_grad, neighbour_grad.reshape(neighbours.shape),

time: 568 us -> 518 us (0.912)
  local copies, waits for them, and re-layouts: 92.2 us -> 32.1 us
  Pallas kernels: 99.3 us -> 147 us
  waiting for transfers between devices: 177 us -> 208 us
  starting transfers between devices: 77.1 us -> 48 us
  other arithmetic: 63 us -> 40.3 us
  matrix products: 49.5 us -> 33.1 us
    pallas_call x3 -> x16, Pallas kernels: 11.4 us -> 59.1 us  [the longest x8 31.1 us: grad_half(): pl.pallas_call(grad_kernel, grid_spec=pltpu.PrefetchScalarGridSpec(num_sc...]
    ppermute x15 -> x8, waiting for transfers between devices: 85.8 us -> 43.2 us  [swap_y(): return lax.ppermute(value, 'fsdp', [(i, i ^ 1) for i in range(self.n)])]
    ppermute x18, waiting for transfers between devices: 69.3 us -> 112 us  [shift_z(): lax.ppermute(value, 'fsdp', [(i, (i + 2 * hops) % self.n) for i in range(...]
    ppermute x9 -> x10, waiting for transfers between devices: 22.3 us -> 49.7 us  [swap_x(): return lax.ppermute(value, 'seq', [(0, 2), (2, 0), (1, 3), (3, 1)])]
    ppermute x15 -> x8, starting transfers between devices: 31.9 us -> 7.09 us  [swap_y(): return lax.ppermute(value, 'fsdp', [(i, i ^ 1) for i in range(self.n)])]
    dot_general x5 -> x1, matrix products: 16.8 us -> 2.24 us  [dot_tn(): lax.dot_general(a, b, (((0,), (0,)), ((), ())), preferred_element_type=F32)]
    reshape x8 -> x0, local copies, waits for them, and re-layouts: 13.2 us -> none  [the longest x2 6.52 us: per_device(): ffn_all[:, :, :width].reshape(4, rows, -1, unit).transpose(1, 2, 0, 3)]
    another operation x6 -> x1, local copies, waits for them, and re-layouts: 12.9 us -> 0.81 us  [ordered(): return jnp.stack([low, high], axis)]
  transfers between devices with their start and end apart: 57 -> 53, of which waited for: 25 -> 26; matrix products, arithmetic and copies ran while one was open for 28% -> 19% of each run, Pallas kernels for 12% -> 22%
where the time goes in v2:
time: 518 us; the launch traced here: 510 us
  waiting for transfers between devices  208 us (40%)
  Pallas kernels  147 us (28%)
  starting transfers between devices  48 us (9%)
  other arithmetic  40.3 us (8%)
  matrix products  33.1 us (6%)
  local copies, waits for them, and re-layouts  32.1 us (6%)
    ppermute x18, waiting for transfers between devices, shift_z(): lax.ppermute(value, 'fsdp', [(i, (i + 2 * hops) % self.n) for i in range(...  112 us
    ppermute x10, waiting for transfers between devices, swap_x(): return lax.ppermute(value, 'seq', [(0, 2), (2, 0), (1, 3), (3, 1)])  49.7 us
    ppermute x8, waiting for transfers between devices, swap_y(): return lax.ppermute(value, 'fsdp', [(i, i ^ 1) for i in range(self.n)])  43.2 us
    pallas_call x8, Pallas kernels, grad_half(): pl.pallas_call(grad_kernel, grid_spec=pltpu.PrefetchScalarGridSpec(num_sc...  31.1 us
    pallas_call x2, Pallas kernels, feed_forward(): pl.pallas_call(functools.partial(ffn_kernel, quarters=n, carry=carry is n...  29.7 us
    pallas_call x1, Pallas kernels, cross_backward(): pl.pallas_call(cross_bwd_kernel, grid=(spans,), in_specs=[pl.BlockSpec((S...  18.7 us
    ppermute x17, starting transfers between devices, swap_core(): return lax.ppermute(value, 'seq', [(0, 1), (1, 0), (2, 3), (3, 2)])  17.4 us
    dot_general x5, matrix products, dot(): lax.dot_general(a, b, (((1,), (0,)), ((), ())), preferred_element_type=F32)  16.7 us
  transfers between devices with their start and end apart: 53, of which 26 were waited for; matrix products, arithmetic and copies ran while one was open for 19% of the time, Pallas kernels for 22%

profile of v2, /device:TPU:9, one launch (start us, length us, event | category | flops | bytes accessed | tf_op | source)
XLA Modules:
  0.0 510.1 jit_solution(6550697960532376967)
XLA Ops:
  7.8 1.8 dynamic-slice_bitcast_fusion.8
  13.3 11.2 %collective-permute-done.3.refs_2_ = bf16[96,1280]{1,0:T(8,128)(2,1)S(1)} collective-permute-done((bf16[96,1280]{1,0:T(8,128)(2,1)S(1)}, bf16[96,1280]{1,0:T(8,128)(2,1)S(1)}, u32[]{:S(2)}, u32[]{:S(2)}) %collective-permute-start.3) | collective-permute-done | bytes 245792 | tf_op jit(solution)/shard_map/ppermute | solution.py:528
  24.5 2.8 collective-permute-done.4.refs_3_
  36.4 2.7 collective-permute-start.1
  39.6 17.0 %collective-permute-done.7 = bf16[96,1536]{1,0:T(8,128)(2,1)S(1)} collective-permute-done((bf16[96,1536]{1,0:T(8,128)(2,1)S(1)}, bf16[96,1536]{1,0:T(8,128)(2,1)S(1)}, u32[]{:S(2)}, u32[]{:S(2)}) %collective-permute-start.7) | collective-permute-done | bytes 294944 | tf_op jit(solution)/shard_map/ppermute | solution.py:528
  56.6 2.0 collective-permute-done.8
  63.4 3.6 assemble.4
  74.7 3.6 convolution_convert_fusion.1.q_ref.k_ref.v_ref
  78.4 14.8 %collective-permute-done.13 = bf16[96,1920]{1,0:T(8,128)(2,1)} collective-permute-done((bf16[96,1920]{1,0:T(8,128)(2,1)S(1)}, bf16[96,1920]{1,0:T(8,128)(2,1)}, u32[]{:S(2)}, u32[]{:S(2)}) %collective-permute-start.13) | collective-permute-done | bytes 368672 | tf_op jit(solution)/shard_map/ppermute | solution.py:528
  93.2 3.1 collective-permute-done.14
  96.2 13.5 %self_forward.1 = (bf16[1024,384]{1,0:T(8,128)(2,1)}, f32[3,8,1024]{2,1,0:T(8,128)}) custom-call(bf16[1024,1152]{1,0:T(8,128)(2,1)} %convolution_convert_fusion.1.q_ref.k_ref.v_ref, bf16[1024,1152]{1,0:T(8,128)(2,1)} %convolution_convert_fusion.1.q_ref.k_ref.v_ref, bf16[1024,1152]{1,0:T(8,128)(2,1)} %convolution_convert_fusion.1.q_ref.k_ref.v_ref, ...), custom_call_target="tpu_custom_call" | custom-call | flops 1610612736 | bytes 3932160 | tf_op jit(solution)/shard_map/self_forward/pallas_call | solution.py:79
  115.7 5.4 %collective-permute-done.15 = bf16[2,256,384]{2,1,0:T(8,128)(2,1)} collective-permute-done((bf16[2,256,384]{2,1,0:T(8,128)(2,1)S(1)}, bf16[2,256,384]{2,1,0:T(8,128)(2,1)}, u32[]{:S(2)}, u32[]{:S(2)}) %collective-permute-start.15) | collective-permute-done | bytes 393248 | tf_op jit(solution)/shard_map/ppermute | solution.py:522
  123.1 2.3 collective-permute-start.16
  129.3 17.1 %collective-permute-done.17.refs_1_ = bf16[384,1536]{1,0:T(8,128)(2,1)} collective-permute-done((bf16[384,1536]{1,0:T(8,128)(2,1)}, bf16[384,1536]{1,0:T(8,128)(2,1)}, u32[]{:S(2)}, u32[]{:S(2)}) %collective-permute-start.17) | collective-permute-done | bytes 1179680 | tf_op jit(solution)/shard_map/ppermute | solution.py:522
  146.4 4.1 assemble.5.own_ref
  152.2 3.7 assemble.6.refs_0_.refs_2_
  156.1 3.7 assemble.7.refs_1_.refs_3_
  160.4 5.4 %merge.1 = (bf16[768,1536]{1,0:T(8,128)(2,1)}, bf16[768,768]{1,0:T(8,128)(2,1)}, bf16[768,768]{1,0:T(8,128)(2,1)}, bf16[768,768]{1,0:T(8,128)(2,1)}) custom-call(s32[1]{0:T(128)} %bitcast.36.c_ref.side_ref, bf16[768,1920]{1,0:T(8,128)(2,1)} %assemble.5.own_ref, bf16[768,1920]{1,0:T(8,128)(2,1)} %collective-permute-done.19.far_ref), custom_call_target="tpu_custom_call" | custom-call | bytes 11796480 | tf_op jit(solution)/shard_map/merge/pallas_call | solution.py:397
  165.7 2.1 fusion.59
  171.5 6.9 %fusion.k_ref.v_ref = bf16[2048,1536]{1,0:T(8,128)(2,1)} fusion(bf16[2048,768]{1,0:T(8,128)(2,1)S(1)} %bitcast.305, bf16[768,1536]{1,0:T(8,128)(2,1)S(1)} %copy-done.47), kind=kOutput, calls=%fused_computation.1 | convolution fusion | flops 4834983936 | bytes 11796480 | tf_op jit(solution)/shard_map/dot_general | solution.py:26
  178.4 10.1 %cross_forward.1.a_ref = bf16[512,768]{1,0:T(8,128)(2,1)} custom-call(bf16[512,768]{1,0:T(8,128)(2,1)} %convolution_convert_fusion.6.q_ref, bf16[2048,1536]{1,0:T(8,128)(2,1)} %fusion.k_ref.v_ref, bf16[2048,1536]{1,0:T(8,128)(2,1)} %fusion.k_ref.v_ref), custom_call_target="tpu_custom_call" | custom-call | flops 402653184 | bytes 7864320 | tf_op jit(solution)/shard_map/cross_forward/pallas_call | solution.py:207
  188.5 2.4 fusion.60
  192.4 14.7 %feed_forward.2 = (f32[512,768]{1,0:T(8,128)}, f32[512,768]{1,0:T(8,128)}, bf16[768,1536]{1,0:T(8,128)(2,1)}, bf16[768,1536]{1,0:T(8,128)(2,1)}) custom-call(bf16[512,768]{1,0:T(8,128)(2,1)} %add_convert_fusion.4.h_ref, bf16[512,768]{1,0:T(8,128)(2,1)} %bitcast.322, bf16[768,1536]{1,0:T(8,128)(2,1)} %collective-permute-done.20.refs_0_.refs_2_, ...), custom_call_target="tpu_custom_call" | custom-call | flops 7247757312 | bytes 15728640 | tf_op jit(solution)/shard_map/feed_forward/pallas_call | solution.py:320
  207.5 15.0 %feed_forward.3 = (f32[512,768]{1,0:T(8,128)}, f32[512,768]{1,0:T(8,128)}, bf16[768,1536]{1,0:T(8,128)(2,1)}, bf16[768,1536]{1,0:T(8,128)(2,1)}) custom-call(bf16[512,768]{1,0:T(8,128)(2,1)} %add_convert_fusion.4.h_ref, bf16[512,768]{1,0:T(8,128)(2,1)} %bitcast.323, bf16[768,1536]{1,0:T(8,128)(2,1)} %assemble.6.refs_0_.refs_2_, ...), custom_call_target="tpu_custom_call" | custom-call | flops 7247757312 | bytes 15728640 | tf_op jit(solution)/shard_map/feed_forward/pallas_call | solution.py:320
  222.6 4.6 add_convert_fusion.1
  228.8 2.0 fusion.58
  233.4 18.7 %cross_backward.1 = (bf16[512,768]{1,0:T(8,128)(2,1)}, bf16[2048,1536]{1,0:T(8,128)(2,1)}) custom-call(bf16[512,768]{1,0:T(8,128)(2,1)} %convolution_convert_fusion.6.q_ref, bf16[2048,1536]{1,0:T(8,128)(2,1)} %fusion.k_ref.v_ref, bf16[2048,1536]{1,0:T(8,128)(2,1)} %fusion.k_ref.v_ref, bf16[512,768]{1,0:T(8,128)(2,1)} %convolution_convert_fusion.5.do_ref), custom_call_target="tpu_custom_call" | custom-call | flops 1006632960 | bytes 14942208 | tf_op jit(solution)/shard_map/cross_backward/pallas_call | solution.py:249
  252.1 2.4 multiply_reduce_fusion.2
  255.9 2.0 fusion.57
  257.8 2.8 grad_half.10
  263.9 6.9 %grad_half.8 = bf16[768,768]{1,0:T(8,128)(2,1)} custom-call(s32[1]{0:T(128)} %bitcast.50.side_ref, bf16[2048,768]{1,0:T(8,128)(2,1)} %bitcast.303, bf16[2048,1536]{1,0:T(8,128)(2,1)} %get-tuple-element.112.b_ref), custom_call_target="tpu_custom_call" | custom-call | flops 2415919104 | bytes 8650752 | tf_op jit(solution)/shard_map/grad_half/pallas_call | solution.py:485
  271.1 2.6 grad_half.12
  273.9 2.6 grad_half.14
  278.3 3.1 grad_half.11
  282.3 2.8 grad_half.13
  285.1 2.9 grad_half.15
  290.5 7.2 %grad_half.9 = bf16[768,768]{1,0:T(8,128)(2,1)} custom-call(s32[1]{0:T(128)} %bitcast.36.c_ref.side_ref, bf16[2048,768]{1,0:T(8,128)(2,1)} %bitcast.304, bf16[2048,1536]{1,0:T(8,128)(2,1)} %get-tuple-element.112.b_ref, bf16[768,768]{1,0:T(8,128)(2,1)} %collective-permute-done.26.refs_0_), custom_call_target="tpu_custom_call" | custom-call | flops 2415919104 | bytes 8650752 | tf_op jit(solution)/shard_map/grad_half/pallas_call | solution.py:485
  297.7 2.1 dynamic-slice_bitcast_fusion.3
  301.1 6.6 %collective-permute-done.24 = bf16[768,1536]{1,0:T(8,128)(2,1)} collective-permute-done((bf16[768,1536]{1,0:T(8,128)(2,1)}, bf16[768,1536]{1,0:T(8,128)(2,1)}, u32[]{:S(2)}, u32[]{:S(2)}) %collective-permute-start.24) | collective-permute-done | bytes 2359328 | tf_op jit(solution)/shard_map/ppermute | solution.py:522
  309.0 3.3 add_convert_fusion
  313.5 4.1 collective-permute-done.25
  320.6 15.8 %self_backward.1 = (bf16[1024,384]{1,0:T(8,128)(2,1)}, bf16[1024,384]{1,0:T(8,128)(2,1)}, bf16[1024,384]{1,0:T(8,128)(2,1)}) custom-call(bf16[1024,1152]{1,0:T(8,128)(2,1)} %convolution_convert_fusion.1.q_ref.k_ref.v_ref, bf16[1024,1152]{1,0:T(8,128)(2,1)} %convolution_convert_fusion.1.q_ref.k_ref.v_ref, ...), custom_call_target="tpu_custom_call" | custom-call | flops 4026531840 | bytes 6291456 | tf_op jit(solution)/shard_map/self_backward/pallas_call | solution.py:146
  336.3 1.9 pad_maximum_fusion
  338.3 6.4 %collective-permute-done.31 = bf16[4,96,1536]{2,1,0:T(8,128)(2,1)} collective-permute-done((bf16[4,96,1536]{2,1,0:T(8,128)(2,1)}, bf16[4,96,1536]{2,1,0:T(8,128)(2,1)}, u32[]{:S(2)}, u32[]{:S(2)}) %collective-permute-start.31) | collective-permute-done | bytes 1179680 | tf_op jit(solution)/shard_map/ppermute | solution.py:525
  344.7 2.2 convolution_convert_fusion.2
  347.0 2.2 convolution_convert_fusion.3
  349.3 26.9 %collective-permute-done.32 = bf16[4,96,1920]{2,1,0:T(8,128)(2,1)} collective-permute-done((bf16[4,96,1920]{2,1,0:T(8,128)(2,1)}, bf16[4,96,1920]{2,1,0:T(8,128)(2,1)}, u32[]{:S(2)}, u32[]{:S(2)}) %collective-permute-start.32) | collective-permute-done | bytes 1474592 | tf_op jit(solution)/shard_map/ppermute | solution.py:525
  376.3 2.7 collective-permute-start.33
  385.3 5.7 %collective-permute-done.46 = bf16[96,1920]{1,0:T(8,128)(2,1)S(1)} collective-permute-done((bf16[96,1920]{1,0:T(8,128)(2,1)S(1)}, bf16[96,1920]{1,0:T(8,128)(2,1)S(1)}, u32[]{:S(2)}, u32[]{:S(2)}) %collective-permute-start.46) | collective-permute-done | bytes 368672 | tf_op jit(solution)/shard_map/ppermute | solution.py:528
  391.2 21.8 %collective-permute-done.47 = bf16[96,1920]{1,0:T(8,128)(2,1)S(1)} collective-permute-done((bf16[96,1920]{1,0:T(8,128)(2,1)S(1)}, bf16[96,1920]{1,0:T(8,128)(2,1)S(1)}, u32[]{:S(2)}, u32[]{:S(2)}) %collective-permute-start.47) | collective-permute-done | bytes 368672 | tf_op jit(solution)/shard_map/ppermute | solution.py:528
  413.2 13.3 %collective-permute-done.48 = bf16[96,1920]{1,0:T(8,128)(2,1)S(1)} collective-permute-done((bf16[96,1920]{1,0:T(8,128)(2,1)S(1)}, bf16[96,1920]{1,0:T(8,128)(2,1)S(1)}, u32[]{:S(2)}, u32[]{:S(2)}) %collective-permute-start.48) | collective-permute-done | bytes 368672 | tf_op jit(solution)/shard_map/ppermute | solution.py:528
  429.5 7.9 %collective-permute-done.49 = bf16[96,1920]{1,0:T(8,128)(2,1)S(1)} collective-permute-done((bf16[96,1920]{1,0:T(8,128)(2,1)S(1)}, bf16[96,1920]{1,0:T(8,128)(2,1)S(1)}, u32[]{:S(2)}, u32[]{:S(2)}) %collective-permute-start.49) | collective-permute-done | bytes 368672 | tf_op jit(solution)/shard_map/ppermute | solution.py:522
  439.7 6.7 %collective-permute-done.34 = bf16[256,768]{1,0:T(8,128)(2,1)S(1)} collective-permute-done((bf16[256,768]{1,0:T(8,128)(2,1)S(1)}, bf16[256,768]{1,0:T(8,128)(2,1)S(1)}, u32[]{:S(2)}, u32[]{:S(2)}) %collective-permute-start.34) | collective-permute-done | bytes 393248 | tf_op jit(solution)/shard_map/ppermute | solution.py:522
  446.4 2.5 collective-permute-start.50
  449.9 1.7 fusion.11
  453.1 7.0 %fusion.61 = f32[2048,768]{1,0:T(8,128)} fusion(bf16[2048,1536]{1,0:T(8,128)(2,1)S(1)} %bitcast.302, bf16[768,1536]{1,0:T(8,128)(2,1)S(1)} %copy-done.48), kind=kOutput, calls=%fused_computation.223 | convolution fusion | flops 4831838208 | bytes 14942208 | tf_op jit(solution)/shard_map/dot_general | solution.py:30
  460.8 2.4 join.3
  466.0 9.8 %collective-permute-done.40 = f32[768,128]{0,1:T(8,128)S(1)} collective-permute-done((f32[768,128]{0,1:T(8,128)S(1)}, f32[768,128]{0,1:T(8,128)S(1)}, u32[]{:S(2)}, u32[]{:S(2)}) %collective-permute-start.40) | collective-permute-done | bytes 393248 | tf_op jit(solution)/shard_map/ppermute | solution.py:525
  477.7 4.7 collective-permute-done.41
  482.4 13.9 %collective-permute-done.42 = bf16[96,1280]{1,0:T(8,128)(2,1)S(1)} collective-permute-done((bf16[96,1280]{1,0:T(8,128)(2,1)S(1)}, bf16[96,1280]{1,0:T(8,128)(2,1)S(1)}, u32[]{:S(2)}, u32[]{:S(2)}) %collective-permute-start.42) | collective-permute-done | bytes 245792 | tf_op jit(solution)/shard_map/ppermute | solution.py:528
  498.6 3.0 spread.1
  501.6 1.9 collective-permute-done.44
  503.8 2.1 collective-permute-start.45
  507.6 2.1 join.2
  (310 shorter events, 97.3 us)
Async XLA Ops:
  2.7 10.6 %collective-permute-start.2 = (bf16[96,1280]{1,0:T(8,128)(2,1)S(1)}, bf16[96,1280]{1,0:T(8,128)(2,1)S(1)}, u32[]{:S(2)}, u32[]{:S(2)}) collective-permute-start(bf16[96,1280]{1,0:T(8,128)(2,1)S(1)} %fusion.41.refs_0_), channel_id=1, source_target_pairs={{0,8},{4,12},{8,16},{12,20},{16,24},{20,28},{24,0},{28,4},{1,9},{5... | collective-permute-start | bytes 737288 | tf_op jit(solution)/shard_map/ppermute | solution.py:528
  4.1 20.4 %collective-permute-start.3 = (bf16[96,1280]{1,0:T(8,128)(2,1)S(1)}, bf16[96,1280]{1,0:T(8,128)(2,1)S(1)}, u32[]{:S(2)}, u32[]{:S(2)}) collective-permute-start(bf16[96,1280]{1,0:T(8,128)(2,1)S(1)} %fusion.41.refs_0_), channel_id=1, source_target_pairs={{0,16},{4,20},{8,24},{12,28},{16,0},{20,4},{24,8},{28,12},{1,17},{... | collective-permute-start | bytes 737288 | tf_op jit(solution)/shard_map/ppermute | solution.py:528
  5.1 22.2 %collective-permute-start.4 = (bf16[96,1280]{1,0:T(8,128)(2,1)S(1)}, bf16[96,1280]{1,0:T(8,128)(2,1)S(1)}, u32[]{:S(2)}, u32[]{:S(2)}) collective-permute-start(bf16[96,1280]{1,0:T(8,128)(2,1)S(1)} %fusion.41.refs_0_), channel_id=1, source_target_pairs={{0,24},{4,28},{8,0},{12,4},{16,8},{20,12},{24,16},{28,20},{1,25},{... | collective-permute-start | bytes 737288 | tf_op jit(solution)/shard_map/ppermute | solution.py:528
  6.5 20.8 %collective-permute-start.5 = (bf16[96,1280]{1,0:T(8,128)(2,1)S(1)}, bf16[96,1280]{1,0:T(8,128)(2,1)}, u32[]{:S(2)}, u32[]{:S(2)}) collective-permute-start(bf16[96,1280]{1,0:T(8,128)(2,1)S(1)} %fusion.41.refs_0_), channel_id=1, source_target_pairs={{0,4},{4,0},{8,12},{12,8},{16,20},{20,16},{24,28},{28,24},{1,5},{5... | collective-permute-start | bytes 737288 | tf_op jit(solution)/shard_map/ppermute | solution.py:525
  9.5 24.8 %collective-permute-start = (bf16[256,768]{1,0:T(8,128)(2,1)}, bf16[256,768]{1,0:T(8,128)(2,1)}, u32[]{:S(2)}, u32[]{:S(2)}) collective-permute-start(bf16[256,768]{1,0:T(8,128)(2,1)} %dynamic-slice_bitcast_fusion.8), channel_id=1, source_target_pairs={{0,2},{2,0},{1,3},{3,1},{4,6},{6,4},{5,7},{7,5},{8,10},{10,8},{9,1... | collective-permute-start | bytes 1179656 | tf_op jit(solution)/shard_map/ppermute | solution.py:522
  13.3 21.1 %copy-start.2 = (bf16[2,256,768]{2,1,0:T(8,128)(2,1)S(1)}, bf16[2,256,768]{2,1,0:T(8,128)(2,1)}, u32[]{:S(2)}) copy-start(bf16[2,256,768]{2,1,0:T(8,128)(2,1)} %param.17) | copy-start | bytes 2359300
  13.3 22.1 %copy-start.32 = (bf16[96,1280]{1,0:T(8,128)(2,1)}, bf16[96,1280]{1,0:T(8,128)(2,1)S(1)}, u32[]{:S(2)}) copy-start(bf16[96,1280]{1,0:T(8,128)(2,1)S(1)} %collective-permute-done.2.refs_1_) | copy-start | bytes 737284
  28.3 30.3 %collective-permute-start.9 = (bf16[288,1280]{1,0:T(8,128)(2,1)}, bf16[288,1280]{1,0:T(8,128)(2,1)S(1)}, u32[]{:S(2)}, u32[]{:S(2)}) collective-permute-start(bf16[288,1280]{1,0:T(8,128)(2,1)} %pad_maximum_fusion.8), channel_id=1, source_target_pairs={{0,4},{4,0},{8,12},{12,8},{16,20},{20,16},{24,28},{28,24},{1,5},{5... | collective-permute-start | bytes 2211848 | tf_op jit(solution)/shard_map/ppermute | solution.py:525
  31.8 7.8 %collective-permute-start.6 = (bf16[96,1536]{1,0:T(8,128)(2,1)S(1)}, bf16[96,1536]{1,0:T(8,128)(2,1)S(1)}, u32[]{:S(2)}, u32[]{:S(2)}) collective-permute-start(bf16[96,1536]{1,0:T(8,128)(2,1)S(1)} %pad_maximum_fusion.11), channel_id=1, source_target_pairs={{0,8},{4,12},{8,16},{12,20},{16,24},{20,28},{24,0},{28,4},{1,9},{5... | collective-permute-start | bytes 884744 | tf_op jit(solution)/shard_map/ppermute | solution.py:528
  31.8 24.8 %collective-permute-start.7 = (bf16[96,1536]{1,0:T(8,128)(2,1)S(1)}, bf16[96,1536]{1,0:T(8,128)(2,1)S(1)}, u32[]{:S(2)}, u32[]{:S(2)}) collective-permute-start(bf16[96,1536]{1,0:T(8,128)(2,1)S(1)} %pad_maximum_fusion.11), channel_id=1, source_target_pairs={{0,16},{4,20},{8,24},{12,28},{16,0},{20,4},{24,8},{28,12},{1,17},{... | collective-permute-start | bytes 884744 | tf_op jit(solution)/shard_map/ppermute | solution.py:528
  32.1 26.5 %collective-permute-start.8 = (bf16[96,1536]{1,0:T(8,128)(2,1)S(1)}, bf16[96,1536]{1,0:T(8,128)(2,1)S(1)}, u32[]{:S(2)}, u32[]{:S(2)}) collective-permute-start(bf16[96,1536]{1,0:T(8,128)(2,1)S(1)} %pad_maximum_fusion.11), channel_id=1, source_target_pairs={{0,24},{4,28},{8,0},{12,4},{16,8},{20,12},{24,16},{28,20},{1,25},{... | collective-permute-start | bytes 884744 | tf_op jit(solution)/shard_map/ppermute | solution.py:528
  36.4 32.9 %collective-permute-start.1 = (bf16[2,256,768]{2,1,0:T(8,128)(2,1)}, bf16[2,256,768]{2,1,0:T(8,128)(2,1)}, u32[]{:S(2)}, u32[]{:S(2)}) collective-permute-start(bf16[2,256,768]{2,1,0:T(8,128)(2,1)} %pad_maximum_fusion.3), channel_id=1, source_target_pairs={{0,1},{1,0},{2,3},{3,2},{4,5},{5,4},{6,7},{7,6},{8,9},{9,8},{10,11... | collective-permute-start | bytes 2359304 | tf_op jit(solution)/shard_map/ppermute | solution.py:519
  60.9 35.4 %collective-permute-start.10 = (bf16[384,1536]{1,0:T(8,128)(2,1)}, bf16[384,1536]{1,0:T(8,128)(2,1)}, u32[]{:S(2)}, u32[]{:S(2)}) collective-permute-start(bf16[384,1536]{1,0:T(8,128)(2,1)} %constant_dynamic-update-slice_fusion.refs_0_), channel_id=1, source_target_pairs={{0,2},{2,0},{1,3},{3,1},{4,6},{6,4},{5,7},{7,5},{8,10},{10,8},{9,1... | collective-permute-start | bytes 3538952 | tf_op jit(solution)/shard_map/ppermute | solution.py:522
  62.1 34.2 %collective-permute-start.11 = (bf16[384,1536]{1,0:T(8,128)(2,1)}, bf16[384,1536]{1,0:T(8,128)(2,1)}, u32[]{:S(2)}, u32[]{:S(2)}) collective-permute-start(bf16[384,1536]{1,0:T(8,128)(2,1)} %constant_dynamic-update-slice_fusion.refs_0_), channel_id=1, source_target_pairs={{0,4},{4,0},{8,12},{12,8},{16,20},{20,16},{24,28},{28,24},{1,5},{5... | collective-permute-start | bytes 3538952 | tf_op jit(solution)/shard_map/ppermute | solution.py:525
  62.3 16.1 %collective-permute-start.12 = (bf16[96,1920]{1,0:T(8,128)(2,1)S(1)}, bf16[96,1920]{1,0:T(8,128)(2,1)}, u32[]{:S(2)}, u32[]{:S(2)}) collective-permute-start(bf16[96,1920]{1,0:T(8,128)(2,1)S(1)} %pad_maximum_fusion.10), channel_id=1, source_target_pairs={{0,8},{4,12},{8,16},{12,20},{16,24},{20,28},{24,0},{28,4},{1,9},{5... | collective-permute-start | bytes 1105928 | tf_op jit(solution)/shard_map/ppermute | solution.py:528
  62.3 30.9 %collective-permute-start.13 = (bf16[96,1920]{1,0:T(8,128)(2,1)S(1)}, bf16[96,1920]{1,0:T(8,128)(2,1)}, u32[]{:S(2)}, u32[]{:S(2)}) collective-permute-start(bf16[96,1920]{1,0:T(8,128)(2,1)S(1)} %pad_maximum_fusion.10), channel_id=1, source_target_pairs={{0,16},{4,20},{8,24},{12,28},{16,0},{20,4},{24,8},{28,12},{1,17},{... | collective-permute-start | bytes 1105928 | tf_op jit(solution)/shard_map/ppermute | solution.py:528
  69.3 26.9 %collective-permute-start.14 = (bf16[96,1920]{1,0:T(8,128)(2,1)S(1)}, bf16[96,1920]{1,0:T(8,128)(2,1)S(1)}, u32[]{:S(2)}, u32[]{:S(2)}) collective-permute-start(bf16[96,1920]{1,0:T(8,128)(2,1)S(1)} %pad_maximum_fusion.10), channel_id=1, source_target_pairs={{0,24},{4,28},{8,0},{12,4},{16,8},{20,12},{24,16},{28,20},{1,25},{... | collective-permute-start | bytes 1105928 | tf_op jit(solution)/shard_map/ppermute | solution.py:528
  110.8 10.3 %collective-permute-start.15 = (bf16[2,256,384]{2,1,0:T(8,128)(2,1)S(1)}, bf16[2,256,384]{2,1,0:T(8,128)(2,1)}, u32[]{:S(2)}, u32[]{:S(2)}) collective-permute-start(bf16[2,256,384]{2,1,0:T(8,128)(2,1)S(1)} %dynamic-slice_bitcast_fusion.7), channel_id=1, source_target_pairs={{0,2},{2,0},{1,3},{3,1},{4,6},{6,4},{5,7},{7,5},{8,10},{10,8},{9,1... | collective-permute-start | bytes 1179656 | tf_op jit(solution)/shard_map/ppermute | solution.py:522
  113.2 15.0 %copy-start.21 = (bf16[384,1920]{1,0:T(8,128)(2,1)}, bf16[384,1920]{1,0:T(8,128)(2,1)S(1)}, u32[]{:S(2)}) copy-start(bf16[384,1920]{1,0:T(8,128)(2,1)S(1)} %constant_dynamic-update-slice_fusion.4.refs_0_) | copy-start | bytes 4423684
  113.2 33.2 %collective-permute-start.18 = (bf16[384,1920]{1,0:T(8,128)(2,1)S(1)}, bf16[384,1920]{1,0:T(8,128)(2,1)}, u32[]{:S(2)}, u32[]{:S(2)}) collective-permute-start(bf16[384,1920]{1,0:T(8,128)(2,1)S(1)} %constant_dynamic-update-slice_fusion.4.refs_0_), channel_id=1, source_target_pairs={{0,4},{4,0},{8,12},{12,8},{16,20},{20,16},{24,28},{28,24},{1,5},{5... | collective-permute-start | bytes 4423688 | tf_op jit(solution)/shard_map/ppermute | solution.py:525
  114.5 31.9 %collective-permute-start.17 = (bf16[384,1536]{1,0:T(8,128)(2,1)}, bf16[384,1536]{1,0:T(8,128)(2,1)}, u32[]{:S(2)}, u32[]{:S(2)}) collective-permute-start(bf16[384,1536]{1,0:T(8,128)(2,1)} %collective-permute-done.11.refs_1_), channel_id=1, source_target_pairs={{0,2},{2,0},{1,3},{3,1},{4,6},{6,4},{5,7},{7,5},{8,10},{10,8},{9,1... | collective-permute-start | bytes 3538952 | tf_op jit(solution)/shard_map/ppermute | solution.py:522
  123.1 4.0 collective-permute-start.16
  129.3 36.5 %copy-start.5 = (bf16[64,8,2,384]{3,1,2,0:T(8,128)(2,1)}, bf16[64,8,2,384]{3,1,2,0:T(8,128)(2,1)S(1)}, u32[]{:S(2)}) copy-start(bf16[64,8,2,384]{3,1,2,0:T(8,128)(2,1)S(1)} %copy.114) | copy-start | bytes 2359300
  150.5 9.8 %collective-permute-start.19 = (bf16[768,1920]{1,0:T(8,128)(2,1)}, bf16[768,1920]{1,0:T(8,128)(2,1)}, u32[]{:S(2)}, u32[]{:S(2)}) collective-permute-start(bf16[768,1920]{1,0:T(8,128)(2,1)} %assemble.5.own_ref), channel_id=1, source_target_pairs={{0,1},{1,0},{2,3},{3,2},{4,5},{5,4},{6,7},{7,6},{8,9},{9,8},{10,11... | collective-permute-start | bytes 8847368 | tf_op jit(solution)/shard_map/ppermute | solution.py:519
  156.0 36.4 %collective-permute-start.20 = (bf16[768,1536]{1,0:T(8,128)(2,1)}, bf16[768,1536]{1,0:T(8,128)(2,1)}, u32[]{:S(2)}, u32[]{:S(2)}) collective-permute-start(bf16[768,1536]{1,0:T(8,128)(2,1)} %assemble.6.refs_0_.refs_2_), channel_id=1, source_target_pairs={{0,1},{1,0},{2,3},{3,2},{4,5},{5,4},{6,7},{7,6},{8,9},{9,8},{10,11... | collective-permute-start | bytes 7077896 | tf_op jit(solution)/shard_map/ppermute | solution.py:519
  159.8 32.6 %collective-permute-start.21 = (bf16[768,1536]{1,0:T(8,128)(2,1)}, bf16[768,1536]{1,0:T(8,128)(2,1)}, u32[]{:S(2)}, u32[]{:S(2)}) collective-permute-start(bf16[768,1536]{1,0:T(8,128)(2,1)} %assemble.7.refs_1_.refs_3_), channel_id=1, source_target_pairs={{0,1},{1,0},{2,3},{3,2},{4,5},{5,4},{6,7},{7,6},{8,9},{9,8},{10,11... | collective-permute-start | bytes 7077896 | tf_op jit(solution)/shard_map/ppermute | solution.py:519
  207.0 15.6 %collective-permute-start.22 = (bf16[768,1536]{1,0:T(8,128)(2,1)}, bf16[768,1536]{1,0:T(8,128)(2,1)}, u32[]{:S(2)}, u32[]{:S(2)}) collective-permute-start(bf16[768,1536]{1,0:T(8,128)(2,1)} %get-tuple-element.106), channel_id=1, source_target_pairs={{0,1},{1,0},{2,3},{3,2},{4,5},{5,4},{6,7},{7,6},{8,9},{9,8},{10,11... | collective-permute-start | bytes 7077896 | tf_op jit(solution)/shard_map/ppermute | solution.py:519
  207.1 102.0 %collective-permute-start.30 = (bf16[768,1536]{1,0:T(8,128)(2,1)}, bf16[768,1536]{1,0:T(8,128)(2,1)}, u32[]{:S(2)}, u32[]{:S(2)}) collective-permute-start(bf16[768,1536]{1,0:T(8,128)(2,1)} %get-tuple-element.114), channel_id=1, source_target_pairs={{0,1},{1,0},{2,3},{3,2},{4,5},{5,4},{6,7},{7,6},{8,9},{9,8},{10,11... | collective-permute-start | bytes 7077896 | tf_op jit(solution)/shard_map/ppermute | solution.py:519
  233.4 18.7 %copy-start.51 = (bf16[768,768]{1,0:T(8,128)(2,1)S(1)}, bf16[768,768]{1,0:T(8,128)(2,1)}, u32[]{:S(2)}) copy-start(bf16[768,768]{1,0:T(8,128)(2,1)} %get-tuple-element.97) | copy-start | bytes 3538948
  254.6 53.1 %collective-permute-start.24 = (bf16[768,1536]{1,0:T(8,128)(2,1)}, bf16[768,1536]{1,0:T(8,128)(2,1)}, u32[]{:S(2)}, u32[]{:S(2)}) collective-permute-start(bf16[768,1536]{1,0:T(8,128)(2,1)} %add_convert_fusion.1), channel_id=1, source_target_pairs={{0,2},{2,0},{1,3},{3,1},{4,6},{6,4},{5,7},{7,5},{8,10},{10,8},{9,1... | collective-permute-start | bytes 7077896 | tf_op jit(solution)/shard_map/ppermute | solution.py:522
  260.6 16.0 %collective-permute-start.27 = (bf16[768,384]{1,0:T(8,128)(2,1)}, bf16[768,384]{1,0:T(8,128)(2,1)}, u32[]{:S(2)}, u32[]{:S(2)}) collective-permute-start(bf16[768,384]{1,0:T(8,128)(2,1)} %grad_half.10), channel_id=1, source_target_pairs={{0,1},{1,0},{2,3},{3,2},{4,5},{5,4},{6,7},{7,6},{8,9},{9,8},{10,11... | collective-permute-start | bytes 1769480 | tf_op jit(solution)/shard_map/ppermute | solution.py:519
  263.7 10.1 %collective-permute-start.23 = (bf16[2,256,384]{2,1,0:T(8,128)(2,1)S(1)}, bf16[2,256,384]{2,1,0:T(8,128)(2,1)S(1)}, u32[]{:S(2)}, u32[]{:S(2)}) collective-permute-start(bf16[2,256,384]{2,1,0:T(8,128)(2,1)S(1)} %bitcast.329), channel_id=1, source_target_pairs={{0,1},{1,0},{2,3},{3,2},{4,5},{5,4},{6,7},{7,6},{8,9},{9,8},{10,11... | collective-permute-start | bytes 1179656 | tf_op jit(solution)/shard_map/ppermute | solution.py:519
  270.8 19.7 %collective-permute-start.26 = (bf16[768,768]{1,0:T(8,128)(2,1)}, bf16[768,768]{1,0:T(8,128)(2,1)}, u32[]{:S(2)}, u32[]{:S(2)}) collective-permute-start(bf16[768,768]{1,0:T(8,128)(2,1)} %grad_half.8), channel_id=1, source_target_pairs={{0,1},{1,0},{2,3},{3,2},{4,5},{5,4},{6,7},{7,6},{8,9},{9,8},{10,11... | collective-permute-start | bytes 3538952 | tf_op jit(solution)/shard_map/ppermute | solution.py:519
  273.8 7.7 %collective-permute-start.28 = (bf16[768,384]{1,0:T(8,128)(2,1)}, bf16[768,384]{1,0:T(8,128)(2,1)S(1)}, u32[]{:S(2)}, u32[]{:S(2)}) collective-permute-start(bf16[768,384]{1,0:T(8,128)(2,1)} %grad_half.12), channel_id=1, source_target_pairs={{0,1},{1,0},{2,3},{3,2},{4,5},{5,4},{6,7},{7,6},{8,9},{9,8},{10,11... | collective-permute-start | bytes 1769480 | tf_op jit(solution)/shard_map/ppermute | solution.py:519
  276.6 8.6 %collective-permute-start.29 = (bf16[768,384]{1,0:T(8,128)(2,1)}, bf16[768,384]{1,0:T(8,128)(2,1)}, u32[]{:S(2)}, u32[]{:S(2)}) collective-permute-start(bf16[768,384]{1,0:T(8,128)(2,1)} %grad_half.14), channel_id=1, source_target_pairs={{0,1},{1,0},{2,3},{3,2},{4,5},{5,4},{6,7},{7,6},{8,9},{9,8},{10,11... | collective-permute-start | bytes 1769480 | tf_op jit(solution)/shard_map/ppermute | solution.py:519
  278.3 29.4 %copy-start.12 = (bf16[2,2,256,384]{3,2,0,1:T(8,128)(2,1)}, bf16[2,2,256,384]{3,2,0,1:T(8,128)(2,1)S(1)}, u32[]{:S(2)}) copy-start(bf16[2,2,256,384]{3,2,0,1:T(8,128)(2,1)S(1)} %pad_maximum_fusion.5) | copy-start | bytes 2359300
  307.8 9.8 %collective-permute-start.25 = (bf16[2,256,384]{2,1,0:T(8,128)(2,1)S(1)}, bf16[2,256,384]{2,1,0:T(8,128)(2,1)S(1)}, u32[]{:S(2)}, u32[]{:S(2)}) collective-permute-start(bf16[2,256,384]{2,1,0:T(8,128)(2,1)S(1)} %dynamic-slice_bitcast_fusion.6), channel_id=1, source_target_pairs={{0,2},{2,0},{1,3},{3,1},{4,6},{6,4},{5,7},{7,5},{8,10},{10,8},{9,1... | collective-permute-start | bytes 1179656 | tf_op jit(solution)/shard_map/ppermute | solution.py:522
  318.6 26.1 %collective-permute-start.31 = (bf16[4,96,1536]{2,1,0:T(8,128)(2,1)}, bf16[4,96,1536]{2,1,0:T(8,128)(2,1)}, u32[]{:S(2)}, u32[]{:S(2)}) collective-permute-start(bf16[4,96,1536]{2,1,0:T(8,128)(2,1)} %dynamic-slice_bitcast_fusion), channel_id=1, source_target_pairs={{0,4},{4,0},{8,12},{12,8},{16,20},{20,16},{24,28},{28,24},{1,5},{5... | collective-permute-start | bytes 3538952 | tf_op jit(solution)/shard_map/ppermute | solution.py:525
  320.3 56.0 %collective-permute-start.32 = (bf16[4,96,1920]{2,1,0:T(8,128)(2,1)}, bf16[4,96,1920]{2,1,0:T(8,128)(2,1)}, u32[]{:S(2)}, u32[]{:S(2)}) collective-permute-start(bf16[4,96,1920]{2,1,0:T(8,128)(2,1)} %pad_maximum_fusion.1), channel_id=1, source_target_pairs={{0,4},{4,0},{8,12},{12,8},{16,20},{20,16},{24,28},{28,24},{1,5},{5... | collective-permute-start | bytes 4423688 | tf_op jit(solution)/shard_map/ppermute | solution.py:525
  349.3 29.8 %copy-start.16 = (bf16[4,96,768]{2,1,0:T(8,128)(2,1)S(1)}, bf16[4,96,768]{2,1,0:T(8,128)(2,1)}, u32[]{:S(2)}) copy-start(bf16[4,96,768]{2,1,0:T(8,128)(2,1)} %get-tuple-element.178) | copy-start | bytes 1769476
  349.3 29.7 %copy-start.27 = (bf16[4,96,384]{2,1,0:T(8,128)(2,1)S(1)}, bf16[4,96,384]{2,1,0:T(8,128)(2,1)}, u32[]{:S(2)}) copy-start(bf16[4,96,384]{2,1,0:T(8,128)(2,1)} %get-tuple-element.203) | copy-start | bytes 884740
  349.3 29.7 %copy-start.28 = (bf16[4,96,384]{2,1,0:T(8,128)(2,1)S(1)}, bf16[4,96,384]{2,1,0:T(8,128)(2,1)}, u32[]{:S(2)}) copy-start(bf16[4,96,384]{2,1,0:T(8,128)(2,1)} %get-tuple-element.205) | copy-start | bytes 884740
  349.3 29.7 %copy-start.29 = (bf16[4,96,384]{2,1,0:T(8,128)(2,1)S(1)}, bf16[4,96,384]{2,1,0:T(8,128)(2,1)}, u32[]{:S(2)}) copy-start(bf16[4,96,384]{2,1,0:T(8,128)(2,1)} %get-tuple-element.207) | copy-start | bytes 884740
  376.3 51.7 %collective-permute-start.33 = (bf16[2,256,768]{2,1,0:T(8,128)(2,1)S(1)}, bf16[2,256,768]{2,1,0:T(8,128)(2,1)S(1)}, u32[]{:S(2)}, u32[]{:S(2)}) collective-permute-start(bf16[2,256,768]{2,1,0:T(8,128)(2,1)S(1)} %dynamic-slice_bitcast_fusion.2), channel_id=1, source_target_pairs={{0,1},{1,0},{2,3},{3,2},{4,5},{5,4},{6,7},{7,6},{8,9},{9,8},{10,11... | collective-permute-start | bytes 2359304 | tf_op jit(solution)/shard_map/ppermute | solution.py:519
  380.9 10.2 %collective-permute-start.46 = (bf16[96,1920]{1,0:T(8,128)(2,1)S(1)}, bf16[96,1920]{1,0:T(8,128)(2,1)S(1)}, u32[]{:S(2)}, u32[]{:S(2)}) collective-permute-start(bf16[96,1920]{1,0:T(8,128)(2,1)S(1)} %get-tuple-element.173), channel_id=1, source_target_pairs={{0,8},{4,12},{8,16},{12,20},{16,24},{20,28},{24,0},{28,4},{1,9},{5... | collective-permute-start | bytes 1105928 | tf_op jit(solution)/shard_map/ppermute | solution.py:528
  380.9 32.0 %collective-permute-start.47 = (bf16[96,1920]{1,0:T(8,128)(2,1)S(1)}, bf16[96,1920]{1,0:T(8,128)(2,1)S(1)}, u32[]{:S(2)}, u32[]{:S(2)}) collective-permute-start(bf16[96,1920]{1,0:T(8,128)(2,1)S(1)} %get-tuple-element.175), channel_id=1, source_target_pairs={{0,16},{4,20},{8,24},{12,28},{16,0},{20,4},{24,8},{28,12},{1,17},{... | collective-permute-start | bytes 1105928 | tf_op jit(solution)/shard_map/ppermute | solution.py:528
  381.1 45.4 %collective-permute-start.48 = (bf16[96,1920]{1,0:T(8,128)(2,1)S(1)}, bf16[96,1920]{1,0:T(8,128)(2,1)S(1)}, u32[]{:S(2)}, u32[]{:S(2)}) collective-permute-start(bf16[96,1920]{1,0:T(8,128)(2,1)S(1)} %get-tuple-element.174), channel_id=1, source_target_pairs={{0,24},{4,28},{8,0},{12,4},{16,8},{20,12},{24,16},{28,20},{1,25},{... | collective-permute-start | bytes 1105928 | tf_op jit(solution)/shard_map/ppermute | solution.py:528
  384.2 67.5 %collective-permute-start.35 = (bf16[96,1536]{1,0:T(8,128)(2,1)S(1)}, bf16[96,1536]{1,0:T(8,128)(2,1)S(1)}, u32[]{:S(2)}, u32[]{:S(2)}) collective-permute-start(bf16[96,1536]{1,0:T(8,128)(2,1)S(1)} %get-tuple-element.182), channel_id=1, source_target_pairs={{0,8},{4,12},{8,16},{12,20},{16,24},{20,28},{24,0},{28,4},{1,9},{5... | collective-permute-start | bytes 884744 | tf_op jit(solution)/shard_map/ppermute | solution.py:528
  391.0 60.6 %collective-permute-start.36 = (bf16[96,1536]{1,0:T(8,128)(2,1)S(1)}, bf16[96,1536]{1,0:T(8,128)(2,1)S(1)}, u32[]{:S(2)}, u32[]{:S(2)}) collective-permute-start(bf16[96,1536]{1,0:T(8,128)(2,1)S(1)} %get-tuple-element.181), channel_id=1, source_target_pairs={{0,16},{4,20},{8,24},{12,28},{16,0},{20,4},{24,8},{28,12},{1,17},{... | collective-permute-start | bytes 884744 | tf_op jit(solution)/shard_map/ppermute | solution.py:528
  412.9 38.7 %collective-permute-start.37 = (bf16[96,1536]{1,0:T(8,128)(2,1)S(1)}, bf16[96,1536]{1,0:T(8,128)(2,1)S(1)}, u32[]{:S(2)}, u32[]{:S(2)}) collective-permute-start(bf16[96,1536]{1,0:T(8,128)(2,1)S(1)} %get-tuple-element.180), channel_id=1, source_target_pairs={{0,24},{4,28},{8,0},{12,4},{16,8},{20,12},{24,16},{28,20},{1,25},{... | collective-permute-start | bytes 884744 | tf_op jit(solution)/shard_map/ppermute | solution.py:528
  426.5 25.1 %collective-permute-start.38 = (bf16[4,96,1152]{2,1,0:T(8,128)(2,1)S(1)}, bf16[4,96,1152]{2,1,0:T(8,128)(2,1)S(1)}, u32[]{:S(2)}, u32[]{:S(2)}) collective-permute-start(bf16[4,96,1152]{2,1,0:T(8,128)(2,1)S(1)} %dynamic-slice_bitcast_fusion.1), channel_id=1, source_target_pairs={{0,4},{4,0},{8,12},{12,8},{16,20},{20,16},{24,28},{28,24},{1,5},{5... | collective-permute-start | bytes 2654216 | tf_op jit(solution)/shard_map/ppermute | solution.py:525
  428.0 9.4 %collective-permute-start.49 = (bf16[96,1920]{1,0:T(8,128)(2,1)S(1)}, bf16[96,1920]{1,0:T(8,128)(2,1)S(1)}, u32[]{:S(2)}, u32[]{:S(2)}) collective-permute-start(bf16[96,1920]{1,0:T(8,128)(2,1)S(1)} %fusion.50), channel_id=1, source_target_pairs={{0,2},{2,0},{1,3},{3,1},{4,6},{6,4},{5,7},{7,5},{8,10},{10,8},{9,1... | collective-permute-start | bytes 1105928 | tf_op jit(solution)/shard_map/ppermute | solution.py:522
  429.3 23.8 %slice-start = ((s8[6291456]{0:T(1024)(128)(4,1)}), s8[4194304]{0:T(1024)(128)(4,1)S(1)}, s32[]{:S(2)}) async-start(s8[6291456]{0:T(1024)(128)(4,1)} %bitcast.301), calls=%async_computation | async-start | bytes 8388608
  437.4 9.0 %collective-permute-start.34 = (bf16[256,768]{1,0:T(8,128)(2,1)S(1)}, bf16[256,768]{1,0:T(8,128)(2,1)S(1)}, u32[]{:S(2)}, u32[]{:S(2)}) collective-permute-start(bf16[256,768]{1,0:T(8,128)(2,1)S(1)} %dynamic-slice_bitcast_fusion.5), channel_id=1, source_target_pairs={{0,2},{2,0},{1,3},{3,1},{4,6},{6,4},{5,7},{7,5},{8,10},{10,8},{9,1... | collective-permute-start | bytes 1179656 | tf_op jit(solution)/shard_map/ppermute | solution.py:522
  446.4 13.7 %collective-permute-start.50 = (bf16[96,1920]{1,0:T(8,128)(2,1)S(1)}, bf16[96,1920]{1,0:T(8,128)(2,1)S(1)}, u32[]{:S(2)}, u32[]{:S(2)}) collective-permute-start(bf16[96,1920]{1,0:T(8,128)(2,1)S(1)} %get-tuple-element.164), channel_id=1, source_target_pairs={{0,1},{1,0},{2,3},{3,2},{4,5},{5,4},{6,7},{7,6},{8,9},{9,8},{10,11... | collective-permute-start | bytes 1105928 | tf_op jit(solution)/shard_map/ppermute | solution.py:519
  451.8 12.2 %collective-permute-start.51 = (bf16[96,1536]{1,0:T(8,128)(2,1)S(1)}, bf16[96,1536]{1,0:T(8,128)(2,1)S(1)}, u32[]{:S(2)}, u32[]{:S(2)}) collective-permute-start(bf16[96,1536]{1,0:T(8,128)(2,1)S(1)} %add_convert_fusion.6), channel_id=1, source_target_pairs={{0,2},{2,0},{1,3},{3,1},{4,6},{6,4},{5,7},{7,5},{8,10},{10,8},{9,1... | collective-permute-start | bytes 884744 | tf_op jit(solution)/shard_map/ppermute | solution.py:522
  463.3 2.1 collective-permute-start.39
  464.2 13.5 %collective-permute-start.52 = (bf16[2,96,1536]{2,1,0:T(8,128)(2,1)S(1)}, bf16[2,96,1536]{2,1,0:T(8,128)(2,1)S(1)}, u32[]{:S(2)}, u32[]{:S(2)}) collective-permute-start(bf16[2,96,1536]{2,1,0:T(8,128)(2,1)S(1)} %pad_maximum_fusion.9), channel_id=1, source_target_pairs={{0,1},{1,0},{2,3},{3,2},{4,5},{5,4},{6,7},{7,6},{8,9},{9,8},{10,11... | collective-permute-start | bytes 1769480 | tf_op jit(solution)/shard_map/ppermute | solution.py:519
  465.4 10.4 %collective-permute-start.40 = (f32[768,128]{0,1:T(8,128)S(1)}, f32[768,128]{0,1:T(8,128)S(1)}, u32[]{:S(2)}, u32[]{:S(2)}) collective-permute-start(f32[768,128]{0,1:T(8,128)S(1)} %pad_add_fusion), channel_id=1, source_target_pairs={{0,4},{4,0},{8,12},{12,8},{16,20},{20,16},{24,28},{28,24},{1,5},{5... | collective-permute-start | bytes 1179656 | tf_op jit(solution)/shard_map/ppermute | solution.py:525
  476.1 6.3 %collective-permute-start.41 = (bf16[96,1280]{1,0:T(8,128)(2,1)S(1)}, bf16[96,1280]{1,0:T(8,128)(2,1)S(1)}, u32[]{:S(2)}, u32[]{:S(2)}) collective-permute-start(bf16[96,1280]{1,0:T(8,128)(2,1)S(1)} %get-tuple-element.196), channel_id=1, source_target_pairs={{0,8},{4,12},{8,16},{12,20},{16,24},{20,28},{24,0},{28,4},{1,9},{5... | collective-permute-start | bytes 737288 | tf_op jit(solution)/shard_map/ppermute | solution.py:528
  476.2 20.2 %collective-permute-start.42 = (bf16[96,1280]{1,0:T(8,128)(2,1)S(1)}, bf16[96,1280]{1,0:T(8,128)(2,1)S(1)}, u32[]{:S(2)}, u32[]{:S(2)}) collective-permute-start(bf16[96,1280]{1,0:T(8,128)(2,1)S(1)} %get-tuple-element.197), channel_id=1, source_target_pairs={{0,16},{4,20},{8,24},{12,28},{16,0},{20,4},{24,8},{28,12},{1,17},{... | collective-permute-start | bytes 737288 | tf_op jit(solution)/shard_map/ppermute | solution.py:528
  476.2 20.7 %collective-permute-start.43 = (bf16[96,1280]{1,0:T(8,128)(2,1)S(1)}, bf16[96,1280]{1,0:T(8,128)(2,1)S(1)}, u32[]{:S(2)}, u32[]{:S(2)}) collective-permute-start(bf16[96,1280]{1,0:T(8,128)(2,1)S(1)} %get-tuple-element.198), channel_id=1, source_target_pairs={{0,24},{4,28},{8,0},{12,4},{16,8},{20,12},{24,16},{28,20},{1,25},{... | collective-permute-start | bytes 737288 | tf_op jit(solution)/shard_map/ppermute | solution.py:528
  497.1 6.4 %collective-permute-start.44 = (bf16[96,1280]{1,0:T(8,128)(2,1)S(1)}, bf16[96,1280]{1,0:T(8,128)(2,1)S(1)}, u32[]{:S(2)}, u32[]{:S(2)}) collective-permute-start(bf16[96,1280]{1,0:T(8,128)(2,1)S(1)} %fusion.55), channel_id=1, source_target_pairs={{0,2},{2,0},{1,3},{3,1},{4,6},{6,4},{5,7},{7,5},{8,10},{10,8},{9,1... | collective-permute-start | bytes 737288 | tf_op jit(solution)/shard_map/ppermute | solution.py:522
  503.8 3.2 collective-permute-start.45
  (43 other events, 166.0 us)

commit v3 on v2

--- a/solution.py
+++ b/solution.py
@@ -651,10 +651,9 @@
     att_heads, lse = self_forward(qkv, segc, segr)
     by_x = att_heads.reshape(2, 2, piece, half)
     got = at.swap_x(pick(by_x, 1 - x, 0))
-    chip = ordered(x, pick(by_x, x, 0), got, 0)
+    chip, moving = tie(ordered(x, pick(by_x, x, 0), got, 0), moving)
     got = at.swap_core(pick(chip, 1 - c, 1))
     att = ordered(c, pick(chip, c, 1), got, 2).reshape(tokens, width)
-    att, moving = tie(att, moving)
     if at.direct:
         group_b = assemble([column_b, moving[1]], places, rows)
         q00 = assemble([column_f, others_f], places, rows)
@@ -698,6 +697,11 @@
     datt = dot_nt(da, wao).astype(BF)
     pairs = ((nb, dckv), (att, da), (h2, dcq), (cro, dc))
     sent_b = [grad_half(a, b, 1 - c) for a, b in pairs]
+    datt, sent_b, ffn_got = tie(datt, sent_b, ffn_got)
+    ffn_sum = own_grads[0].astype(F32) + f0.astype(F32) + ffn_got.astype(F32)
+    ffn_own = lax.psum_scatter(
+        ffn_sum.astype(BF).reshape(at.n, rows, 2 * width), "fsdp", scatter_dimension=0, tiled=False
+    )
     sums_b = [grad_half(a, b, c, at.swap_core(v)) for (a, b), v in zip(pairs, sent_b)]
     sent_b, kept_b = at.send_y(sums_b)
     neighbour_grad = dot_nt(dckv, wckv)
@@ -705,22 +709,18 @@
     datt = datt.reshape(seqs, piece, 2, half)
     got = at.swap_core(pick(datt, 1 - c, 2))
     chip = ordered(c, pick(datt, c, 2), got, 1)
-    chip, ffn_got = tie(chip, ffn_got)
     got = at.swap_x(pick(chip, 1 - x, 0))
     do = ordered(x, pick(chip, x, 0), got, 0).reshape(4 * piece, half)
-    ffn_sum = own_grads[0].astype(F32) + f0.astype(F32) + ffn_got.astype(F32)
-    sent_f, kept_f = at.send_y([ffn_sum.astype(BF)])
-    do, sent_b, sent_f = tie(do, sent_b, sent_f)
-    got_f, got_b = at.swap_y(sent_f), at.swap_y(sent_b)
+    do, sent_b = tie(do, sent_b)
+    got_b = at.swap_y(sent_b)
     dqkv = jnp.concatenate(self_backward(qkv, do, segc, segr, lse), 1)
-    dqkv, got_f = tie(dqkv, got_f)
-    moving_f = at.send_z(added(kept_f, got_f))
+    dqkv, got_b = tie(dqkv, got_b)
+    moving_b = at.send_z(added(kept_b, got_b))
     grad_qkv = dot_tn(h1, dqkv).astype(BF)
     sent_a, kept_a = at.send_y([grad_qkv])
     part = dot_nt(dqkv, wqkv).astype(BF).reshape(2, 2, piece, width)
-    part, sent_a, got_b = tie(part, sent_a, got_b)
+    part, sent_a = tie(part, sent_a)
     got_a = at.swap_y(sent_a)
-    moving_b = at.send_z(added(kept_b, got_b))
     got = at.swap_core(pick(part, 1 - c, 1))
     chip = (pick(part, c, 1).astype(F32) + got.astype(F32)).astype(BF)
     got = at.swap_x(pick(chip, 1 - x, 0))
@@ -731,12 +731,12 @@
     def finish(own):
         return own + at.swap_x(own.astype(BF)).astype(F32)
 
-    input_grad, moving_f, got_a = tie(input_grad, moving_f, got_a)
-    vec = jnp.pad(jnp.stack([gg1, gb1, gg2, gb2, gg3, gb3], 1), ((0, 0), (0, 128 - 6)))
+    input_grad, moving_b, got_a = tie(input_grad, moving_b, got_a)
+    vec = jnp.stack([gg1, gb1, gg2, gb2, gg3, gb3], 0)
     vec = vec + at.swap_core(vec)
-    vec = pick((vec + at.swap_y(vec)).reshape(at.n // 2, 2, rows, 128), at.y, 1).astype(BF)
+    vec = jnp.pad((vec + at.swap_y(vec)).T, ((0, 0), (0, 128 - 6)))
+    vec = pick(vec.reshape(at.n // 2, 2, rows, 128), at.y, 1).astype(BF)
     moving_a = at.send_z(jnp.concatenate([added(kept_a, got_a), vec], 2))
-    ffn_own = at.total(*moving_f).astype(BF)
     ffn_x = ordered(x, ffn_own, at.swap_x(ffn_own), 0)
     ffn_all = ordered(c, ffn_x, at.swap_core(ffn_x), 1).reshape(4, rows, 2 * width)
     grad_up, grad_down = spread(ffn_all, unit)

time: 518 us -> 483 us (0.932)
  waiting for transfers between devices: 208 us -> 154 us
  between operations: 2.23 us -> 15.6 us
  starting transfers between devices: 48 us -> 41.5 us
  local copies, waits for them, and re-layouts: 32.1 us -> 37.7 us
  other arithmetic: 40.3 us -> 45.5 us
    ppermute x8 -> x7, waiting for transfers between devices: 43.2 us -> 18.1 us  [swap_y(): return lax.ppermute(value, 'fsdp', [(i, i ^ 1) for i in range(self.n)])]
    ppermute x18 -> x15, waiting for transfers between devices: 112 us -> 95.4 us  [shift_z(): lax.ppermute(value, 'fsdp', [(i, (i + 2 * hops) % self.n) for i in range(...]
    ppermute x10, waiting for transfers between devices: 49.7 us -> 40 us  [swap_x(): return lax.ppermute(value, 'seq', [(0, 2), (2, 0), (1, 3), (3, 1)])]
    unnamed x122 -> x125, local copies, waits for them, and re-layouts: 11.1 us -> 12.3 us
    ppermute x18 -> x15, starting transfers between devices: 12.9 us -> 13.7 us  [shift_z(): lax.ppermute(value, 'fsdp', [(i, (i + 2 * hops) % self.n) for i in range(...]
  transfers between devices with their start and end apart: 53 -> 50, of which waited for: 26 -> 17; matrix products, arithmetic and copies ran while one was open for 19% -> 22% of each run, Pallas kernels for 22% -> 26%
where the time goes in v3:
time: 483 us; the launch traced here: 475 us
  waiting for transfers between devices  154 us (32%)
  Pallas kernels  147 us (30%)
  other arithmetic  45.5 us (9%)
  starting transfers between devices  41.5 us (9%)
  local copies, waits for them, and re-layouts  37.7 us (8%)
  matrix products  33.6 us (7%)
  between operations  15.6 us (3%)
    ppermute x15, waiting for transfers between devices, shift_z(): lax.ppermute(value, 'fsdp', [(i, (i + 2 * hops) % self.n) for i in range(...  95.4 us
    ppermute x10, waiting for transfers between devices, swap_x(): return lax.ppermute(value, 'seq', [(0, 2), (2, 0), (1, 3), (3, 1)])  40 us
    pallas_call x8, Pallas kernels, grad_half(): pl.pallas_call(grad_kernel, grid_spec=pltpu.PrefetchScalarGridSpec(num_sc...  30.9 us
    pallas_call x2, Pallas kernels, feed_forward(): pl.pallas_call(functools.partial(ffn_kernel, quarters=n, carry=carry is n...  29.6 us
    pallas_call x1, Pallas kernels, cross_backward(): pl.pallas_call(cross_bwd_kernel, grid=(spans,), in_specs=[pl.BlockSpec((S...  18.6 us
    ppermute x7, waiting for transfers between devices, swap_y(): return lax.ppermute(value, 'fsdp', [(i, i ^ 1) for i in range(self.n)])  18.1 us
    dot_general x5, matrix products, dot(): lax.dot_general(a, b, (((1,), (0,)), ((), ())), preferred_element_type=F32)  16.7 us
    pallas_call x1, Pallas kernels, self_backward(): pl.pallas_call(functools.partial(self_bwd_kernel, block=256), grid=(pairs...  16 us
  transfers between devices with their start and end apart: 50, of which 17 were waited for; matrix products, arithmetic and copies ran while one was open for 22% of the time, Pallas kernels for 26%

profile of v3, /device:TPU:9, one launch (start us, length us, event | category | flops | bytes accessed | tf_op | source)
XLA Modules:
  0.0 474.6 jit_solution(9521935599192309936)
XLA Ops:
  14.4 1.8 dynamic-slice_bitcast_fusion.7
  20.7 10.4 %collective-permute-done.3.refs_2_ = bf16[96,1280]{1,0:T(8,128)(2,1)S(1)} collective-permute-done((bf16[96,1280]{1,0:T(8,128)(2,1)S(1)}, bf16[96,1280]{1,0:T(8,128)(2,1)S(1)}, u32[]{:S(2)}, u32[]{:S(2)}) %collective-permute-start.3) | collective-permute-done | bytes 245792 | tf_op jit(solution)/shard_map/ppermute | solution.py:528
  31.1 2.8 collective-permute-done.4.refs_3_
  37.3 1.5 collective-permute-start.8
  41.5 2.7 collective-permute-start.1
  44.9 16.9 %collective-permute-done.7 = bf16[96,1536]{1,0:T(8,128)(2,1)S(1)} collective-permute-done((bf16[96,1536]{1,0:T(8,128)(2,1)S(1)}, bf16[96,1536]{1,0:T(8,128)(2,1)S(1)}, u32[]{:S(2)}, u32[]{:S(2)}) %collective-permute-start.7) | collective-permute-done | bytes 294944 | tf_op jit(solution)/shard_map/ppermute | solution.py:528
  61.8 2.0 collective-permute-done.8
  68.5 3.7 assemble.4
  74.5 1.5 collective-permute-start.14
  79.9 3.7 convolution_convert_fusion.1.q_ref.k_ref.v_ref
  83.6 14.7 %collective-permute-done.13 = bf16[96,1920]{1,0:T(8,128)(2,1)} collective-permute-done((bf16[96,1920]{1,0:T(8,128)(2,1)S(1)}, bf16[96,1920]{1,0:T(8,128)(2,1)}, u32[]{:S(2)}, u32[]{:S(2)}) %collective-permute-start.13) | collective-permute-done | bytes 368672 | tf_op jit(solution)/shard_map/ppermute | solution.py:528
  98.3 3.1 collective-permute-done.14
  105.7 13.5 %self_forward.1 = (bf16[1024,384]{1,0:T(8,128)(2,1)}, f32[3,8,1024]{2,1,0:T(8,128)}) custom-call(bf16[1024,1152]{1,0:T(8,128)(2,1)} %convolution_convert_fusion.1.q_ref.k_ref.v_ref, bf16[1024,1152]{1,0:T(8,128)(2,1)} %convolution_convert_fusion.1.q_ref.k_ref.v_ref, bf16[1024,1152]{1,0:T(8,128)(2,1)} %convolution_convert_fusion.1.q_ref.k_ref.v_ref, ...), custom_call_target="tpu_custom_call" | custom-call | flops 1610612736 | bytes 3932160 | tf_op jit(solution)/shard_map/self_forward/pallas_call | solution.py:79
  121.5 17.7 %collective-permute-done.15 = bf16[2,256,384]{2,1,0:T(8,128)(2,1)S(1)} collective-permute-done((bf16[2,256,384]{2,1,0:T(8,128)(2,1)S(1)}, bf16[2,256,384]{2,1,0:T(8,128)(2,1)S(1)}, u32[]{:S(2)}, u32[]{:S(2)}) %collective-permute-start.15) | collective-permute-done | bytes 393248 | tf_op jit(solution)/shard_map/ppermute | solution.py:522
  140.3 4.1 assemble.5.own_ref
  144.5 1.7 collective-permute-start.19
  146.3 3.7 assemble.6.refs_0_.refs_2_
  150.6 3.7 assemble.7.refs_1_.refs_3_
  155.6 5.6 %merge.1 = (bf16[768,1536]{1,0:T(8,128)(2,1)}, bf16[768,768]{1,0:T(8,128)(2,1)}, bf16[768,768]{1,0:T(8,128)(2,1)}, bf16[768,768]{1,0:T(8,128)(2,1)}) custom-call(s32[1]{0:T(128)} %bitcast.36.c_ref.side_ref, bf16[768,1920]{1,0:T(8,128)(2,1)} %assemble.5.own_ref, bf16[768,1920]{1,0:T(8,128)(2,1)} %collective-permute-done.19.far_ref), custom_call_target="tpu_custom_call" | custom-call | bytes 11796480 | tf_op jit(solution)/shard_map/merge/pallas_call | solution.py:397
  161.2 2.1 fusion.56
  164.6 1.7 convolution_convert_fusion.6.q_ref
  167.0 6.9 %fusion.k_ref.v_ref = bf16[2048,1536]{1,0:T(8,128)(2,1)} fusion(bf16[2048,768]{1,0:T(8,128)(2,1)S(1)} %bitcast.275, bf16[768,1536]{1,0:T(8,128)(2,1)S(1)} %copy-done.49), kind=kOutput, calls=%fused_computation.1 | convolution fusion | flops 4834983936 | bytes 11796480 | tf_op jit(solution)/shard_map/dot_general | solution.py:26
  173.9 10.1 %cross_forward.1.a_ref = bf16[512,768]{1,0:T(8,128)(2,1)} custom-call(bf16[512,768]{1,0:T(8,128)(2,1)} %convolution_convert_fusion.6.q_ref, bf16[2048,1536]{1,0:T(8,128)(2,1)} %fusion.k_ref.v_ref, bf16[2048,1536]{1,0:T(8,128)(2,1)} %fusion.k_ref.v_ref), custom_call_target="tpu_custom_call" | custom-call | flops 402653184 | bytes 7864320 | tf_op jit(solution)/shard_map/cross_forward/pallas_call | solution.py:207
  183.9 2.4 fusion.57
  187.8 14.6 %feed_forward.2 = (f32[512,768]{1,0:T(8,128)}, f32[512,768]{1,0:T(8,128)}, bf16[768,1536]{1,0:T(8,128)(2,1)}, bf16[768,1536]{1,0:T(8,128)(2,1)}) custom-call(bf16[512,768]{1,0:T(8,128)(2,1)} %add_convert_fusion.4.h_ref, bf16[512,768]{1,0:T(8,128)(2,1)} %bitcast.291, bf16[768,1536]{1,0:T(8,128)(2,1)} %collective-permute-done.20.refs_0_.refs_2_, ...), custom_call_target="tpu_custom_call" | custom-call | flops 7247757312 | bytes 15728640 | tf_op jit(solution)/shard_map/feed_forward/pallas_call | solution.py:320
  204.4 15.0 %feed_forward.3 = (f32[512,768]{1,0:T(8,128)}, f32[512,768]{1,0:T(8,128)}, bf16[768,1536]{1,0:T(8,128)(2,1)}, bf16[768,1536]{1,0:T(8,128)(2,1)}) custom-call(bf16[512,768]{1,0:T(8,128)(2,1)} %add_convert_fusion.4.h_ref, bf16[512,768]{1,0:T(8,128)(2,1)} %bitcast.292, bf16[768,1536]{1,0:T(8,128)(2,1)} %assemble.6.refs_0_.refs_2_, ...), custom_call_target="tpu_custom_call" | custom-call | flops 7247757312 | bytes 15728640 | tf_op jit(solution)/shard_map/feed_forward/pallas_call | solution.py:320
  219.5 4.5 add_convert_fusion.1
  225.6 2.3 fusion.55
  227.9 2.8 grad_half.11
  230.7 1.7 convolution_convert_fusion.5.do_ref
  232.5 18.6 %cross_backward.1 = (bf16[512,768]{1,0:T(8,128)(2,1)}, bf16[2048,1536]{1,0:T(8,128)(2,1)}) custom-call(bf16[512,768]{1,0:T(8,128)(2,1)} %convolution_convert_fusion.6.q_ref, bf16[2048,1536]{1,0:T(8,128)(2,1)} %fusion.k_ref.v_ref, bf16[2048,1536]{1,0:T(8,128)(2,1)} %fusion.k_ref.v_ref, bf16[512,768]{1,0:T(8,128)(2,1)} %convolution_convert_fusion.5.do_ref), custom_call_target="tpu_custom_call" | custom-call | flops 1006632960 | bytes 14942208 | tf_op jit(solution)/shard_map/cross_backward/pallas_call | solution.py:249
  251.1 2.8 grad_half.10
  253.9 1.7 multiply_reduce_fusion.2
  255.6 2.0 fusion.54
  257.5 2.7 grad_half.9
  260.2 6.9 %grad_half.8 = bf16[768,768]{1,0:T(8,128)(2,1)} custom-call(s32[1]{0:T(128)} %bitcast.41.side_ref, bf16[2048,768]{1,0:T(8,128)(2,1)} %bitcast.273, bf16[2048,1536]{1,0:T(8,128)(2,1)} %get-tuple-element.112.b_ref), custom_call_target="tpu_custom_call" | custom-call | flops 2415919104 | bytes 8650752 | tf_op jit(solution)/shard_map/grad_half/pallas_call | solution.py:485
  267.2 2.1 convolution_convert_fusion.4
  269.3 8.2 %collective-permute-done.23 = bf16[768,1536]{1,0:T(8,128)(2,1)} collective-permute-done((bf16[768,1536]{1,0:T(8,128)(2,1)}, bf16[768,1536]{1,0:T(8,128)(2,1)}, u32[]{:S(2)}, u32[]{:S(2)}) %collective-permute-start.23) | collective-permute-done | bytes 2359328 | tf_op jit(solution)/shard_map/ppermute | solution.py:522
  277.7 1.6 constant_dynamic-slice_fusion.1
  285.2 2.8 grad_half.13
  288.0 2.8 grad_half.14
  290.9 2.9 grad_half.15
  299.4 7.1 %grad_half.12 = bf16[768,768]{1,0:T(8,128)(2,1)} custom-call(s32[1]{0:T(128)} %bitcast.36.c_ref.side_ref, bf16[2048,768]{1,0:T(8,128)(2,1)} %bitcast.274, bf16[2048,1536]{1,0:T(8,128)(2,1)} %get-tuple-element.112.b_ref, bf16[768,768]{1,0:T(8,128)(2,1)} %copy-done.26), custom_call_target="tpu_custom_call" | custom-call | flops 2415919104 | bytes 8650752 | tf_op jit(solution)/shard_map/grad_half/pallas_call | solution.py:485
  310.0 4.8 %add_convert_fusion = bf16[768,1536]{1,0:T(8,128)(2,1)} fusion(bf16[768,1536]{1,0:T(8,128)(2,1)} %collective-permute-done.23, bf16[768,1536]{1,0:T(8,128)(2,1)} %collective-permute-done.46, bf16[768,1536]{1,0:T(8,128)(2,1)S(1)} %copy-done.16), kind=kLoop, calls=%fused_computation.2 | loop fusion | flops 7077888 | bytes 9437184 | tf_op jit(solution)/shard_map/convert_element_type | solution.py:703
  314.8 16.0 %self_backward.1 = (bf16[1024,384]{1,0:T(8,128)(2,1)}, bf16[1024,384]{1,0:T(8,128)(2,1)}, bf16[1024,384]{1,0:T(8,128)(2,1)}) custom-call(bf16[1024,1152]{1,0:T(8,128)(2,1)} %convolution_convert_fusion.1.q_ref.k_ref.v_ref, bf16[1024,1152]{1,0:T(8,128)(2,1)} %convolution_convert_fusion.1.q_ref.k_ref.v_ref, ...), custom_call_target="tpu_custom_call" | custom-call | flops 4026531840 | bytes 6291456 | tf_op jit(solution)/shard_map/self_backward/pallas_call | solution.py:146
  330.8 2.0 pad_maximum_fusion
  332.8 16.8 %collective-permute-done.30 = bf16[4,96,1920]{2,1,0:T(8,128)(2,1)S(1)} collective-permute-done((bf16[4,96,1920]{2,1,0:T(8,128)(2,1)}, bf16[4,96,1920]{2,1,0:T(8,128)(2,1)S(1)}, u32[]{:S(2)}, u32[]{:S(2)}) %collective-permute-start.30) | collective-permute-done | bytes 1474592 | tf_op jit(solution)/shard_map/ppermute | solution.py:525
  349.6 2.3 convolution_convert_fusion.2
  351.9 2.2 convolution_convert_fusion.3
  355.2 2.6 collective-permute-start.31
  357.8 7.0 %fusion.58 = f32[2048,768]{1,0:T(8,128)} fusion(bf16[2048,1536]{1,0:T(8,128)(2,1)S(1)} %bitcast.272, bf16[768,1536]{1,0:T(8,128)(2,1)S(1)} %copy-done.50), kind=kOutput, calls=%fused_computation.214 | convolution fusion | flops 4831838208 | bytes 14942208 | tf_op jit(solution)/shard_map/dot_general | solution.py:30
  370.1 1.8 collective-permute-start.35
  372.0 5.4 %collective-permute-done.32 = bf16[256,768]{1,0:T(8,128)(2,1)S(1)} collective-permute-done((bf16[256,768]{1,0:T(8,128)(2,1)S(1)}, bf16[256,768]{1,0:T(8,128)(2,1)S(1)}, u32[]{:S(2)}, u32[]{:S(2)}) %collective-permute-start.32) | collective-permute-done | bytes 393248 | tf_op jit(solution)/shard_map/ppermute | solution.py:522
  380.8 1.7 collective-permute-start.37
  382.5 2.5 fusion.10
  385.0 25.7 %collective-permute-done.34 = bf16[96,1920]{1,0:T(8,128)(2,1)} collective-permute-done((bf16[96,1920]{1,0:T(8,128)(2,1)}, bf16[96,1920]{1,0:T(8,128)(2,1)}, u32[]{:S(2)}, u32[]{:S(2)}) %collective-permute-start.34) | collective-permute-done | bytes 368672 | tf_op jit(solution)/shard_map/ppermute | solution.py:528
  414.9 2.2 collective-permute-start.40
  420.9 13.5 %collective-permute-done.40 = bf16[96,1280]{1,0:T(8,128)(2,1)S(1)} collective-permute-done((bf16[96,1280]{1,0:T(8,128)(2,1)S(1)}, bf16[96,1280]{1,0:T(8,128)(2,1)S(1)}, u32[]{:S(2)}, u32[]{:S(2)}) %collective-permute-start.40) | collective-permute-done | bytes 245792 | tf_op jit(solution)/shard_map/ppermute | solution.py:528
  434.4 4.8 %collective-permute-done.41 = bf16[96,1280]{1,0:T(8,128)(2,1)S(1)} collective-permute-done((bf16[96,1280]{1,0:T(8,128)(2,1)S(1)}, bf16[96,1280]{1,0:T(8,128)(2,1)S(1)}, u32[]{:S(2)}, u32[]{:S(2)}) %collective-permute-start.41) | collective-permute-done | bytes 245792 | tf_op jit(solution)/shard_map/ppermute | solution.py:528
  441.5 2.3 fusion.53
  444.8 8.7 %collective-permute-done.47 = bf16[96,1536]{1,0:T(8,128)(2,1)S(1)} collective-permute-done((bf16[96,1536]{1,0:T(8,128)(2,1)}, bf16[96,1536]{1,0:T(8,128)(2,1)S(1)}, u32[]{:S(2)}, u32[]{:S(2)}) %collective-permute-start.47) | collective-permute-done | bytes 294944 | tf_op jit(solution)/shard_map/ppermute | solution.py:522
  457.9 2.4 join.3
  461.0 2.1 join.2
  464.2 3.0 spread.1
  (303 shorter events, 88.4 us)
Async XLA Ops:
  7.2 11.0 %copy-start = (bf16[384,768]{1,0:T(8,128)(2,1)S(1)}, bf16[384,768]{1,0:T(8,128)(2,1)}, u32[]{:S(2)}) copy-start(bf16[384,768]{1,0:T(8,128)(2,1)} %param.32) | copy-start | bytes 1769476
  7.2 10.2 %copy-start.37 = (bf16[96,3072]{1,0:T(8,128)(2,1)S(1)}, bf16[96,3072]{1,0:T(8,128)(2,1)}, u32[]{:S(2)}) copy-start(bf16[96,3072]{1,0:T(8,128)(2,1)} %param.31) | copy-start | bytes 1769476
  7.2 433.8 %reduce-scatter.2.cloned.1.call-start = ((), (), s32[]{:S(2)}) async-start(), calls=%async_computation.1 | async-start | bytes 2654208 | tf_op jit(solution)/shard_map/reduce_scatter | solution.py:702
  9.3 11.4 %collective-permute-start.2 = (bf16[96,1280]{1,0:T(8,128)(2,1)S(1)}, bf16[96,1280]{1,0:T(8,128)(2,1)S(1)}, u32[]{:S(2)}, u32[]{:S(2)}) collective-permute-start(bf16[96,1280]{1,0:T(8,128)(2,1)S(1)} %fusion.38.refs_0_), channel_id=1, source_target_pairs={{0,8},{4,12},{8,16},{12,20},{16,24},{20,28},{24,0},{28,4},{1,9},{5... | collective-permute-start | bytes 737288 | tf_op jit(solution)/shard_map/ppermute | solution.py:528
  10.7 20.4 %collective-permute-start.3 = (bf16[96,1280]{1,0:T(8,128)(2,1)S(1)}, bf16[96,1280]{1,0:T(8,128)(2,1)S(1)}, u32[]{:S(2)}, u32[]{:S(2)}) collective-permute-start(bf16[96,1280]{1,0:T(8,128)(2,1)S(1)} %fusion.38.refs_0_), channel_id=1, source_target_pairs={{0,16},{4,20},{8,24},{12,28},{16,0},{20,4},{24,8},{28,12},{1,17},{... | collective-permute-start | bytes 737288 | tf_op jit(solution)/shard_map/ppermute | solution.py:528
  11.8 22.2 %collective-permute-start.4 = (bf16[96,1280]{1,0:T(8,128)(2,1)S(1)}, bf16[96,1280]{1,0:T(8,128)(2,1)S(1)}, u32[]{:S(2)}, u32[]{:S(2)}) collective-permute-start(bf16[96,1280]{1,0:T(8,128)(2,1)S(1)} %fusion.38.refs_0_), channel_id=1, source_target_pairs={{0,24},{4,28},{8,0},{12,4},{16,8},{20,12},{24,16},{28,20},{1,25},{... | collective-permute-start | bytes 737288 | tf_op jit(solution)/shard_map/ppermute | solution.py:528
  13.2 20.8 %collective-permute-start.5 = (bf16[96,1280]{1,0:T(8,128)(2,1)S(1)}, bf16[96,1280]{1,0:T(8,128)(2,1)}, u32[]{:S(2)}, u32[]{:S(2)}) collective-permute-start(bf16[96,1280]{1,0:T(8,128)(2,1)S(1)} %fusion.38.refs_0_), channel_id=1, source_target_pairs={{0,4},{4,0},{8,12},{12,8},{16,20},{20,16},{24,28},{28,24},{1,5},{5... | collective-permute-start | bytes 737288 | tf_op jit(solution)/shard_map/ppermute | solution.py:525
  16.2 23.3 %collective-permute-start = (bf16[256,768]{1,0:T(8,128)(2,1)}, bf16[256,768]{1,0:T(8,128)(2,1)}, u32[]{:S(2)}, u32[]{:S(2)}) collective-permute-start(bf16[256,768]{1,0:T(8,128)(2,1)} %dynamic-slice_bitcast_fusion.7), channel_id=1, source_target_pairs={{0,2},{2,0},{1,3},{3,1},{4,6},{6,4},{5,7},{7,5},{8,10},{10,8},{9,1... | collective-permute-start | bytes 1179656 | tf_op jit(solution)/shard_map/ppermute | solution.py:522
  20.7 18.8 %copy-start.2 = (bf16[2,256,768]{2,1,0:T(8,128)(2,1)S(1)}, bf16[2,256,768]{2,1,0:T(8,128)(2,1)}, u32[]{:S(2)}) copy-start(bf16[2,256,768]{2,1,0:T(8,128)(2,1)} %param.17) | copy-start | bytes 2359300
  20.7 19.9 %copy-start.33 = (bf16[96,1280]{1,0:T(8,128)(2,1)}, bf16[96,1280]{1,0:T(8,128)(2,1)S(1)}, u32[]{:S(2)}) copy-start(bf16[96,1280]{1,0:T(8,128)(2,1)S(1)} %collective-permute-done.2.refs_1_) | copy-start | bytes 737284
  34.9 28.9 %collective-permute-start.9 = (bf16[288,1280]{1,0:T(8,128)(2,1)}, bf16[288,1280]{1,0:T(8,128)(2,1)}, u32[]{:S(2)}, u32[]{:S(2)}) collective-permute-start(bf16[288,1280]{1,0:T(8,128)(2,1)} %pad_maximum_fusion.8), channel_id=1, source_target_pairs={{0,4},{4,0},{8,12},{12,8},{16,20},{20,16},{24,28},{28,24},{1,5},{5... | collective-permute-start | bytes 2211848 | tf_op jit(solution)/shard_map/ppermute | solution.py:525
  37.0 7.9 %collective-permute-start.6 = (bf16[96,1536]{1,0:T(8,128)(2,1)S(1)}, bf16[96,1536]{1,0:T(8,128)(2,1)S(1)}, u32[]{:S(2)}, u32[]{:S(2)}) collective-permute-start(bf16[96,1536]{1,0:T(8,128)(2,1)S(1)} %pad_maximum_fusion.11), channel_id=1, source_target_pairs={{0,8},{4,12},{8,16},{12,20},{16,24},{20,28},{24,0},{28,4},{1,9},{5... | collective-permute-start | bytes 884744 | tf_op jit(solution)/shard_map/ppermute | solution.py:528
  37.0 24.8 %collective-permute-start.7 = (bf16[96,1536]{1,0:T(8,128)(2,1)S(1)}, bf16[96,1536]{1,0:T(8,128)(2,1)S(1)}, u32[]{:S(2)}, u32[]{:S(2)}) collective-permute-start(bf16[96,1536]{1,0:T(8,128)(2,1)S(1)} %pad_maximum_fusion.11), channel_id=1, source_target_pairs={{0,16},{4,20},{8,24},{12,28},{16,0},{20,4},{24,8},{28,12},{1,17},{... | collective-permute-start | bytes 884744 | tf_op jit(solution)/shard_map/ppermute | solution.py:528
  37.3 26.5 %collective-permute-start.8 = (bf16[96,1536]{1,0:T(8,128)(2,1)S(1)}, bf16[96,1536]{1,0:T(8,128)(2,1)S(1)}, u32[]{:S(2)}, u32[]{:S(2)}) collective-permute-start(bf16[96,1536]{1,0:T(8,128)(2,1)S(1)} %pad_maximum_fusion.11), channel_id=1, source_target_pairs={{0,24},{4,28},{8,0},{12,4},{16,8},{20,12},{24,16},{28,20},{1,25},{... | collective-permute-start | bytes 884744 | tf_op jit(solution)/shard_map/ppermute | solution.py:528
  41.5 32.9 %collective-permute-start.1 = (bf16[2,256,768]{2,1,0:T(8,128)(2,1)}, bf16[2,256,768]{2,1,0:T(8,128)(2,1)}, u32[]{:S(2)}, u32[]{:S(2)}) collective-permute-start(bf16[2,256,768]{2,1,0:T(8,128)(2,1)} %pad_maximum_fusion.3), channel_id=1, source_target_pairs={{0,1},{1,0},{2,3},{3,2},{4,5},{5,4},{6,7},{7,6},{8,9},{9,8},{10,11... | collective-permute-start | bytes 2359304 | tf_op jit(solution)/shard_map/ppermute | solution.py:519
  66.0 35.4 %collective-permute-start.10 = (bf16[384,1536]{1,0:T(8,128)(2,1)}, bf16[384,1536]{1,0:T(8,128)(2,1)}, u32[]{:S(2)}, u32[]{:S(2)}) collective-permute-start(bf16[384,1536]{1,0:T(8,128)(2,1)} %constant_dynamic-update-slice_fusion.refs_0_), channel_id=1, source_target_pairs={{0,2},{2,0},{1,3},{3,1},{4,6},{6,4},{5,7},{7,5},{8,10},{10,8},{9,1... | collective-permute-start | bytes 3538952 | tf_op jit(solution)/shard_map/ppermute | solution.py:522
  67.2 34.2 %collective-permute-start.11 = (bf16[384,1536]{1,0:T(8,128)(2,1)}, bf16[384,1536]{1,0:T(8,128)(2,1)}, u32[]{:S(2)}, u32[]{:S(2)}) collective-permute-start(bf16[384,1536]{1,0:T(8,128)(2,1)} %constant_dynamic-update-slice_fusion.refs_0_), channel_id=1, source_target_pairs={{0,4},{4,0},{8,12},{12,8},{16,20},{20,16},{24,28},{28,24},{1,5},{5... | collective-permute-start | bytes 3538952 | tf_op jit(solution)/shard_map/ppermute | solution.py:525
  67.4 16.2 %collective-permute-start.12 = (bf16[96,1920]{1,0:T(8,128)(2,1)S(1)}, bf16[96,1920]{1,0:T(8,128)(2,1)S(1)}, u32[]{:S(2)}, u32[]{:S(2)}) collective-permute-start(bf16[96,1920]{1,0:T(8,128)(2,1)S(1)} %pad_maximum_fusion.10), channel_id=1, source_target_pairs={{0,8},{4,12},{8,16},{12,20},{16,24},{20,28},{24,0},{28,4},{1,9},{5... | collective-permute-start | bytes 1105928 | tf_op jit(solution)/shard_map/ppermute | solution.py:528
  67.4 30.9 %collective-permute-start.13 = (bf16[96,1920]{1,0:T(8,128)(2,1)S(1)}, bf16[96,1920]{1,0:T(8,128)(2,1)}, u32[]{:S(2)}, u32[]{:S(2)}) collective-permute-start(bf16[96,1920]{1,0:T(8,128)(2,1)S(1)} %pad_maximum_fusion.10), channel_id=1, source_target_pairs={{0,16},{4,20},{8,24},{12,28},{16,0},{20,4},{24,8},{28,12},{1,17},{... | collective-permute-start | bytes 1105928 | tf_op jit(solution)/shard_map/ppermute | solution.py:528
  74.5 26.9 %collective-permute-start.14 = (bf16[96,1920]{1,0:T(8,128)(2,1)S(1)}, bf16[96,1920]{1,0:T(8,128)(2,1)S(1)}, u32[]{:S(2)}, u32[]{:S(2)}) collective-permute-start(bf16[96,1920]{1,0:T(8,128)(2,1)S(1)} %pad_maximum_fusion.10), channel_id=1, source_target_pairs={{0,24},{4,28},{8,0},{12,4},{16,8},{20,12},{24,16},{28,20},{1,25},{... | collective-permute-start | bytes 1105928 | tf_op jit(solution)/shard_map/ppermute | solution.py:528
  83.6 20.4 %copy-start.46 = (s32[2,1024]{1,0:T(2,128)S(1)}, s32[2,1024]{1,0:T(2,128)}, u32[]{:S(2)}) copy-start(s32[2,1024]{1,0:T(2,128)} %param.18) | copy-start | bytes 24580
  102.4 16.7 %copy-start.20 = (bf16[384,1920]{1,0:T(8,128)(2,1)}, bf16[384,1920]{1,0:T(8,128)(2,1)S(1)}, u32[]{:S(2)}) copy-start(bf16[384,1920]{1,0:T(8,128)(2,1)S(1)} %constant_dynamic-update-slice_fusion.4.refs_0_) | copy-start | bytes 4423684
  102.5 37.9 %collective-permute-start.17 = (bf16[384,1920]{1,0:T(8,128)(2,1)S(1)}, bf16[384,1920]{1,0:T(8,128)(2,1)}, u32[]{:S(2)}, u32[]{:S(2)}) collective-permute-start(bf16[384,1920]{1,0:T(8,128)(2,1)S(1)} %constant_dynamic-update-slice_fusion.4.refs_0_), channel_id=1, source_target_pairs={{0,4},{4,0},{8,12},{12,8},{16,20},{20,16},{24,28},{28,24},{1,5},{5... | collective-permute-start | bytes 4423688 | tf_op jit(solution)/shard_map/ppermute | solution.py:525
  103.8 36.6 %collective-permute-start.16 = (bf16[384,1536]{1,0:T(8,128)(2,1)}, bf16[384,1536]{1,0:T(8,128)(2,1)}, u32[]{:S(2)}, u32[]{:S(2)}) collective-permute-start(bf16[384,1536]{1,0:T(8,128)(2,1)} %collective-permute-done.11.refs_1_), channel_id=1, source_target_pairs={{0,2},{2,0},{1,3},{3,1},{4,6},{6,4},{5,7},{7,5},{8,10},{10,8},{9,1... | collective-permute-start | bytes 3538952 | tf_op jit(solution)/shard_map/ppermute | solution.py:522
  120.2 19.0 %collective-permute-start.15 = (bf16[2,256,384]{2,1,0:T(8,128)(2,1)S(1)}, bf16[2,256,384]{2,1,0:T(8,128)(2,1)S(1)}, u32[]{:S(2)}, u32[]{:S(2)}) collective-permute-start(bf16[2,256,384]{2,1,0:T(8,128)(2,1)S(1)} %dynamic-slice_bitcast_fusion.6), channel_id=1, source_target_pairs={{0,2},{2,0},{1,3},{3,1},{4,6},{6,4},{5,7},{7,5},{8,10},{10,8},{9,1... | collective-permute-start | bytes 1179656 | tf_op jit(solution)/shard_map/ppermute | solution.py:522
  144.5 11.1 %collective-permute-start.19 = (bf16[768,1920]{1,0:T(8,128)(2,1)}, bf16[768,1920]{1,0:T(8,128)(2,1)}, u32[]{:S(2)}, u32[]{:S(2)}) collective-permute-start(bf16[768,1920]{1,0:T(8,128)(2,1)} %assemble.5.own_ref), channel_id=1, source_target_pairs={{0,1},{1,0},{2,3},{3,2},{4,5},{5,4},{6,7},{7,6},{8,9},{9,8},{10,11... | collective-permute-start | bytes 8847368 | tf_op jit(solution)/shard_map/ppermute | solution.py:519
  146.2 8.2 %collective-permute-start.18 = (bf16[2,256,384]{2,1,0:T(8,128)(2,1)S(1)}, bf16[2,256,384]{2,1,0:T(8,128)(2,1)S(1)}, u32[]{:S(2)}, u32[]{:S(2)}) collective-permute-start(bf16[2,256,384]{2,1,0:T(8,128)(2,1)S(1)} %dynamic-slice_bitcast_fusion.5), channel_id=1, source_target_pairs={{0,1},{1,0},{2,3},{3,2},{4,5},{5,4},{6,7},{7,6},{8,9},{9,8},{10,11... | collective-permute-start | bytes 1179656 | tf_op jit(solution)/shard_map/ppermute | solution.py:519
  150.1 37.8 %collective-permute-start.20 = (bf16[768,1536]{1,0:T(8,128)(2,1)}, bf16[768,1536]{1,0:T(8,128)(2,1)}, u32[]{:S(2)}, u32[]{:S(2)}) collective-permute-start(bf16[768,1536]{1,0:T(8,128)(2,1)} %assemble.6.refs_0_.refs_2_), channel_id=1, source_target_pairs={{0,1},{1,0},{2,3},{3,2},{4,5},{5,4},{6,7},{7,6},{8,9},{9,8},{10,11... | collective-permute-start | bytes 7077896 | tf_op jit(solution)/shard_map/ppermute | solution.py:519
  154.3 33.5 %collective-permute-start.21 = (bf16[768,1536]{1,0:T(8,128)(2,1)}, bf16[768,1536]{1,0:T(8,128)(2,1)}, u32[]{:S(2)}, u32[]{:S(2)}) collective-permute-start(bf16[768,1536]{1,0:T(8,128)(2,1)} %assemble.7.refs_1_.refs_3_), channel_id=1, source_target_pairs={{0,1},{1,0},{2,3},{3,2},{4,5},{5,4},{6,7},{7,6},{8,9},{9,8},{10,11... | collective-permute-start | bytes 7077896 | tf_op jit(solution)/shard_map/ppermute | solution.py:519
  202.5 17.0 %collective-permute-start.22 = (bf16[768,1536]{1,0:T(8,128)(2,1)}, bf16[768,1536]{1,0:T(8,128)(2,1)}, u32[]{:S(2)}, u32[]{:S(2)}) collective-permute-start(bf16[768,1536]{1,0:T(8,128)(2,1)} %get-tuple-element.108), channel_id=1, source_target_pairs={{0,1},{1,0},{2,3},{3,2},{4,5},{5,4},{6,7},{7,6},{8,9},{9,8},{10,11... | collective-permute-start | bytes 7077896 | tf_op jit(solution)/shard_map/ppermute | solution.py:519
  204.3 105.0 %collective-permute-start.46 = (bf16[768,1536]{1,0:T(8,128)(2,1)}, bf16[768,1536]{1,0:T(8,128)(2,1)}, u32[]{:S(2)}, u32[]{:S(2)}) collective-permute-start(bf16[768,1536]{1,0:T(8,128)(2,1)} %get-tuple-element.140), channel_id=1, source_target_pairs={{0,1},{1,0},{2,3},{3,2},{4,5},{5,4},{6,7},{7,6},{8,9},{9,8},{10,11... | collective-permute-start | bytes 7077896 | tf_op jit(solution)/shard_map/ppermute | solution.py:519
  224.7 52.8 %collective-permute-start.23 = (bf16[768,1536]{1,0:T(8,128)(2,1)}, bf16[768,1536]{1,0:T(8,128)(2,1)}, u32[]{:S(2)}, u32[]{:S(2)}) collective-permute-start(bf16[768,1536]{1,0:T(8,128)(2,1)} %add_convert_fusion.1), channel_id=1, source_target_pairs={{0,2},{2,0},{1,3},{3,1},{4,6},{6,4},{5,7},{7,5},{8,10},{10,8},{9,1... | collective-permute-start | bytes 7077896 | tf_op jit(solution)/shard_map/ppermute | solution.py:522
  279.4 4.2 collective-permute-start.24
  281.1 3.8 collective-permute-start.27
  281.2 6.8 %collective-permute-start.28 = (bf16[768,384]{1,0:T(8,128)(2,1)}, bf16[768,384]{1,0:T(8,128)(2,1)}, u32[]{:S(2)}, u32[]{:S(2)}) collective-permute-start(bf16[768,384]{1,0:T(8,128)(2,1)} %grad_half.10), channel_id=1, source_target_pairs={{0,1},{1,0},{2,3},{3,2},{4,5},{5,4},{6,7},{7,6},{8,9},{9,8},{10,11... | collective-permute-start | bytes 1769480 | tf_op jit(solution)/shard_map/ppermute | solution.py:519
  281.7 9.2 %collective-permute-start.29 = (bf16[768,384]{1,0:T(8,128)(2,1)}, bf16[768,384]{1,0:T(8,128)(2,1)}, u32[]{:S(2)}, u32[]{:S(2)}) collective-permute-start(bf16[768,384]{1,0:T(8,128)(2,1)} %grad_half.11), channel_id=1, source_target_pairs={{0,1},{1,0},{2,3},{3,2},{4,5},{5,4},{6,7},{7,6},{8,9},{9,8},{10,11... | collective-permute-start | bytes 1769480 | tf_op jit(solution)/shard_map/ppermute | solution.py:519
  283.5 14.8 %collective-permute-start.26 = (bf16[768,768]{1,0:T(8,128)(2,1)}, bf16[768,768]{1,0:T(8,128)(2,1)S(1)}, u32[]{:S(2)}, u32[]{:S(2)}) collective-permute-start(bf16[768,768]{1,0:T(8,128)(2,1)} %grad_half.8), channel_id=1, source_target_pairs={{0,1},{1,0},{2,3},{3,2},{4,5},{5,4},{6,7},{7,6},{8,9},{9,8},{10,11... | collective-permute-start | bytes 3538952 | tf_op jit(solution)/shard_map/ppermute | solution.py:519
  284.9 11.4 %collective-permute-start.25 = (bf16[2,256,384]{2,1,0:T(8,128)(2,1)}, bf16[2,256,384]{2,1,0:T(8,128)(2,1)}, u32[]{:S(2)}, u32[]{:S(2)}) collective-permute-start(bf16[2,256,384]{2,1,0:T(8,128)(2,1)} %fusion.27), channel_id=1, source_target_pairs={{0,2},{2,0},{1,3},{3,1},{4,6},{6,4},{5,7},{7,5},{8,10},{10,8},{9,1... | collective-permute-start | bytes 1179656 | tf_op jit(solution)/shard_map/ppermute | solution.py:522
  309.1 40.6 %collective-permute-start.30 = (bf16[4,96,1920]{2,1,0:T(8,128)(2,1)}, bf16[4,96,1920]{2,1,0:T(8,128)(2,1)S(1)}, u32[]{:S(2)}, u32[]{:S(2)}) collective-permute-start(bf16[4,96,1920]{2,1,0:T(8,128)(2,1)} %pad_maximum_fusion.1), channel_id=1, source_target_pairs={{0,4},{4,0},{8,12},{12,8},{16,20},{20,16},{24,28},{28,24},{1,5},{5... | collective-permute-start | bytes 4423688 | tf_op jit(solution)/shard_map/ppermute | solution.py:525
  330.8 18.8 %copy-start.25 = (bf16[1024,768]{1,0:T(8,128)(2,1)S(1)}, bf16[1024,768]{1,0:T(8,128)(2,1)}, u32[]{:S(2)}) copy-start(bf16[1024,768]{1,0:T(8,128)(2,1)} %copy-done.24) | copy-start | bytes 4718596
  332.8 19.1 %copy-start.15 = (bf16[768,1280]{1,0:T(8,128)(2,1)S(1)}, bf16[768,1280]{1,0:T(8,128)(2,1)}, u32[]{:S(2)}) copy-start(bf16[768,1280]{1,0:T(8,128)(2,1)} %assemble.4) | copy-start | bytes 5898244
  355.2 10.2 %copy-start.47 = (f32[768]{0:T(1024)S(1)}, f32[768]{0:T(1024)}, u32[]{:S(2)}) copy-start(f32[768]{0:T(1024)} %get-tuple-element.153) | copy-start | bytes 9220
  355.2 11.9 %collective-permute-start.31 = (bf16[2,256,768]{2,1,0:T(8,128)(2,1)S(1)}, bf16[2,256,768]{2,1,0:T(8,128)(2,1)S(1)}, u32[]{:S(2)}, u32[]{:S(2)}) collective-permute-start(bf16[2,256,768]{2,1,0:T(8,128)(2,1)S(1)} %dynamic-slice_bitcast_fusion.1), channel_id=1, source_target_pairs={{0,1},{1,0},{2,3},{3,2},{4,5},{5,4},{6,7},{7,6},{8,9},{9,8},{10,11... | collective-permute-start | bytes 2359304 | tf_op jit(solution)/shard_map/ppermute | solution.py:519
  367.4 10.0 %collective-permute-start.32 = (bf16[256,768]{1,0:T(8,128)(2,1)S(1)}, bf16[256,768]{1,0:T(8,128)(2,1)S(1)}, u32[]{:S(2)}, u32[]{:S(2)}) collective-permute-start(bf16[256,768]{1,0:T(8,128)(2,1)S(1)} %dynamic-slice_bitcast_fusion.4), channel_id=1, source_target_pairs={{0,2},{2,0},{1,3},{3,1},{4,6},{6,4},{5,7},{7,5},{8,10},{10,8},{9,1... | collective-permute-start | bytes 1179656 | tf_op jit(solution)/shard_map/ppermute | solution.py:522
  370.0 15.0 %collective-permute-start.33 = (bf16[96,1920]{1,0:T(8,128)(2,1)}, bf16[96,1920]{1,0:T(8,128)(2,1)}, u32[]{:S(2)}, u32[]{:S(2)}) collective-permute-start(bf16[96,1920]{1,0:T(8,128)(2,1)} %get-tuple-element.179), channel_id=1, source_target_pairs={{0,8},{4,12},{8,16},{12,20},{16,24},{20,28},{24,0},{28,4},{1,9},{5... | collective-permute-start | bytes 1105928 | tf_op jit(solution)/shard_map/ppermute | solution.py:528
  370.0 40.7 %collective-permute-start.34 = (bf16[96,1920]{1,0:T(8,128)(2,1)}, bf16[96,1920]{1,0:T(8,128)(2,1)}, u32[]{:S(2)}, u32[]{:S(2)}) collective-permute-start(bf16[96,1920]{1,0:T(8,128)(2,1)} %get-tuple-element.178), channel_id=1, source_target_pairs={{0,16},{4,20},{8,24},{12,28},{16,0},{20,4},{24,8},{28,12},{1,17},{... | collective-permute-start | bytes 1105928 | tf_op jit(solution)/shard_map/ppermute | solution.py:528
  370.1 10.0 %copy-start.43 = (f32[1,768]{1,0:T(1,128)S(1)}, f32[1,768]{1,0:T(1,128)}, u32[]{:S(2)}) copy-start(f32[1,768]{1,0:T(1,128)} %stack.216) | copy-start | bytes 9220
  370.1 10.0 %copy-start.44 = (f32[1,768]{1,0:T(1,128)S(1)}, f32[1,768]{1,0:T(1,128)}, u32[]{:S(2)}) copy-start(f32[1,768]{1,0:T(1,128)} %stack.217) | copy-start | bytes 9220
  370.1 12.4 %copy-start.11 = (f32[512,768]{1,0:T(8,128)S(1)}, f32[512,768]{1,0:T(8,128)}, u32[]{:S(2)}) copy-start(f32[512,768]{1,0:T(8,128)} %get-tuple-element.171) | copy-start | bytes 4718596
  370.1 41.6 %collective-permute-start.35 = (bf16[96,1920]{1,0:T(8,128)(2,1)}, bf16[96,1920]{1,0:T(8,128)(2,1)}, u32[]{:S(2)}, u32[]{:S(2)}) collective-permute-start(bf16[96,1920]{1,0:T(8,128)(2,1)} %get-tuple-element.177), channel_id=1, source_target_pairs={{0,24},{4,28},{8,0},{12,4},{16,8},{20,12},{24,16},{28,20},{1,25},{... | collective-permute-start | bytes 1105928 | tf_op jit(solution)/shard_map/ppermute | solution.py:528
  371.8 39.9 %collective-permute-start.36 = (bf16[4,96,1152]{2,1,0:T(8,128)(2,1)}, bf16[4,96,1152]{2,1,0:T(8,128)(2,1)}, u32[]{:S(2)}, u32[]{:S(2)}) collective-permute-start(bf16[4,96,1152]{2,1,0:T(8,128)(2,1)} %dynamic-slice_bitcast_fusion), channel_id=1, source_target_pairs={{0,4},{4,0},{8,12},{12,8},{16,20},{20,16},{24,28},{28,24},{1,5},{5... | collective-permute-start | bytes 2654216 | tf_op jit(solution)/shard_map/ppermute | solution.py:525
  380.8 30.9 %collective-permute-start.37 = (f32[6,768]{1,0:T(8,128)S(1)}, f32[6,768]{1,0:T(8,128)S(1)}, u32[]{:S(2)}, u32[]{:S(2)}) collective-permute-start(f32[6,768]{1,0:T(8,128)S(1)} %stack.220), channel_id=1, source_target_pairs={{0,1},{1,0},{2,3},{3,2},{4,5},{5,4},{6,7},{7,6},{8,9},{9,8},{10,11... | collective-permute-start | bytes 55304 | tf_op jit(solution)/shard_map/ppermute | solution.py:519
  382.5 29.3 %copy-start.22 = (bf16[768,1152]{1,0:T(8,128)(2,1)S(1)}, bf16[768,1152]{1,0:T(8,128)(2,1)}, u32[]{:S(2)}) copy-start(bf16[768,1152]{1,0:T(8,128)(2,1)} %copy-done.21) | copy-start | bytes 5308420
  411.7 2.7 collective-permute-start.38
  414.8 6.1 %collective-permute-start.39 = (bf16[96,1280]{1,0:T(8,128)(2,1)S(1)}, bf16[96,1280]{1,0:T(8,128)(2,1)S(1)}, u32[]{:S(2)}, u32[]{:S(2)}) collective-permute-start(bf16[96,1280]{1,0:T(8,128)(2,1)S(1)} %get-tuple-element.197), channel_id=1, source_target_pairs={{0,8},{4,12},{8,16},{12,20},{16,24},{20,28},{24,0},{28,4},{1,9},{5... | collective-permute-start | bytes 737288 | tf_op jit(solution)/shard_map/ppermute | solution.py:528
  414.9 19.6 %collective-permute-start.40 = (bf16[96,1280]{1,0:T(8,128)(2,1)S(1)}, bf16[96,1280]{1,0:T(8,128)(2,1)S(1)}, u32[]{:S(2)}, u32[]{:S(2)}) collective-permute-start(bf16[96,1280]{1,0:T(8,128)(2,1)S(1)} %get-tuple-element.198), channel_id=1, source_target_pairs={{0,16},{4,20},{8,24},{12,28},{16,0},{20,4},{24,8},{28,12},{1,17},{... | collective-permute-start | bytes 737288 | tf_op jit(solution)/shard_map/ppermute | solution.py:528
  417.1 22.1 %collective-permute-start.41 = (bf16[96,1280]{1,0:T(8,128)(2,1)S(1)}, bf16[96,1280]{1,0:T(8,128)(2,1)S(1)}, u32[]{:S(2)}, u32[]{:S(2)}) collective-permute-start(bf16[96,1280]{1,0:T(8,128)(2,1)S(1)} %get-tuple-element.199), channel_id=1, source_target_pairs={{0,24},{4,28},{8,0},{12,4},{16,8},{20,12},{24,16},{28,20},{1,25},{... | collective-permute-start | bytes 737288 | tf_op jit(solution)/shard_map/ppermute | solution.py:528
  419.8 21.7 %collective-permute-start.44 = (bf16[96,1920]{1,0:T(8,128)(2,1)S(1)}, bf16[96,1920]{1,0:T(8,128)(2,1)S(1)}, u32[]{:S(2)}, u32[]{:S(2)}) collective-permute-start(bf16[96,1920]{1,0:T(8,128)(2,1)S(1)} %fusion.47), channel_id=1, source_target_pairs={{0,2},{2,0},{1,3},{3,1},{4,6},{6,4},{5,7},{7,5},{8,10},{10,8},{9,1... | collective-permute-start | bytes 1105928 | tf_op jit(solution)/shard_map/ppermute | solution.py:522
  440.0 15.1 %collective-permute-start.42 = (bf16[96,1280]{1,0:T(8,128)(2,1)}, bf16[96,1280]{1,0:T(8,128)(2,1)}, u32[]{:S(2)}, u32[]{:S(2)}) collective-permute-start(bf16[96,1280]{1,0:T(8,128)(2,1)} %fusion.52), channel_id=1, source_target_pairs={{0,2},{2,0},{1,3},{3,1},{4,6},{6,4},{5,7},{7,5},{8,10},{10,8},{9,1... | collective-permute-start | bytes 737288 | tf_op jit(solution)/shard_map/ppermute | solution.py:522
  441.0 12.5 %copy-start.39 = (bf16[1,96,1536]{2,1,0:T(8,128)(2,1)S(1)}, bf16[1,96,1536]{2,1,0:T(8,128)(2,1)}, u32[]{:S(2)}) copy-start(bf16[1,96,1536]{2,1,0:T(8,128)(2,1)} %reduce-scatter.2.cloned.1.call-done) | copy-start | bytes 884740
  441.0 12.5 %collective-permute-start.47 = (bf16[96,1536]{1,0:T(8,128)(2,1)}, bf16[96,1536]{1,0:T(8,128)(2,1)S(1)}, u32[]{:S(2)}, u32[]{:S(2)}) collective-permute-start(bf16[96,1536]{1,0:T(8,128)(2,1)} %bitcast.299), channel_id=1, source_target_pairs={{0,2},{2,0},{1,3},{3,1},{4,6},{6,4},{5,7},{7,5},{8,10},{10,8},{9,1... | collective-permute-start | bytes 884744 | tf_op jit(solution)/shard_map/ppermute | solution.py:522
  443.8 13.4 %collective-permute-start.45 = (bf16[96,1920]{1,0:T(8,128)(2,1)S(1)}, bf16[96,1920]{1,0:T(8,128)(2,1)S(1)}, u32[]{:S(2)}, u32[]{:S(2)}) collective-permute-start(bf16[96,1920]{1,0:T(8,128)(2,1)S(1)} %get-tuple-element.168), channel_id=1, source_target_pairs={{0,1},{1,0},{2,3},{3,2},{4,5},{5,4},{6,7},{7,6},{8,9},{9,8},{10,11... | collective-permute-start | bytes 1105928 | tf_op jit(solution)/shard_map/ppermute | solution.py:519
  453.7 9.3 %collective-permute-start.48 = (bf16[2,96,1536]{2,1,0:T(8,128)(2,1)S(1)}, bf16[2,96,1536]{2,1,0:T(8,128)(2,1)S(1)}, u32[]{:S(2)}, u32[]{:S(2)}) collective-permute-start(bf16[2,96,1536]{2,1,0:T(8,128)(2,1)S(1)} %pad_maximum_fusion.9), channel_id=1, source_target_pairs={{0,1},{1,0},{2,3},{3,2},{4,5},{5,4},{6,7},{7,6},{8,9},{9,8},{10,11... | collective-permute-start | bytes 1769480 | tf_op jit(solution)/shard_map/ppermute | solution.py:519
  456.3 4.0 collective-permute-start.43
  (41 other events, 160.1 us)
Sparse Core Ops, SparseCore 0:
  314.9 87.7 reduce-scatter.1
